TPU v7x, 32 devices: a whole 2x2x4 slice. The times are simulated.
32 devices in a mesh: expert: 8 (over z, x), shard: 4 (over y, core).
Axes of the slice: x: 2, y: 2, z: 4, core: 2. Of those that a mesh axis runs over, the one named last changes fastest.
Arguments:
- tokens: bfloat16 [2, 3072, 2048], P(None, ('expert', 'shard')), may hold values from -6 to 6
- cotangent: bfloat16 [2, 3072, 2048], P(None, ('expert', 'shard')), may hold values from -6 to 6
- block_ids: int32 [2, 8, 384], P(None, 'expert'), may hold values from 0 to 2, never falling along the last dimension, each value on 1 to 256 neighbouring positions
- routes: int32 [2, 3072, 8], P(None, ('expert', 'shard')), may hold values from 0 to 15, all different within a row; in each aligned block of 96 rows (0 to 95, 96 to 191, ..., all dimensions but the last counted through in order) at most 54 rows name the same one
- w_query: bfloat16 [2048, 2048], P(('expert', 'shard')), may hold values from -0.125 to 0.125
- w_key: bfloat16 [2048, 2048], P(('expert', 'shard')), may hold values from -0.125 to 0.125
- w_value: bfloat16 [2048, 2048], P(('expert', 'shard')), may hold values from -0.125 to 0.125
- w_out: bfloat16 [2048, 2048], P(('expert', 'shard')), may hold values from -1.5 to 1.5
- router: bfloat16 [2048, 16], P(('expert', 'shard')), may hold values from -0.0625 to 0.0625
- attention_gain: bfloat16 [2048], P(('expert', 'shard')), may hold values from 0.099609375 to 1.8984375
- query_gain: bfloat16 [2048], P(('expert', 'shard')), may hold values from 0.099609375 to 1.8984375
- key_gain: bfloat16 [2048], P(('expert', 'shard')), may hold values from 0.099609375 to 1.8984375
- mixture_gain: bfloat16 [2048], P(('expert', 'shard')), may hold values from 0.099609375 to 1.8984375
- w_gate: bfloat16 [16, 2048, 1024], P('expert', 'shard'), may hold values from -0.125 to 0.125
- w_up: bfloat16 [16, 2048, 1024], P('expert', 'shard'), may hold values from -0.125 to 0.125
- w_down: bfloat16 [16, 1024, 2048], P('expert', 'shard'), may hold values from -6 to 6
Outputs:
- output: bfloat16 [2, 3072, 2048], P(None, ('expert', 'shard'))
- input_grad: bfloat16 [2, 3072, 2048], P(None, ('expert', 'shard'))
- w_query_grad: float32 [2048, 2048], P(('expert', 'shard'))
- w_key_grad: float32 [2048, 2048], P(('expert', 'shard'))
- w_value_grad: float32 [2048, 2048], P(('expert', 'shard'))
- w_out_grad: float32 [2048, 2048], P(('expert', 'shard'))
- router_grad: float32 [2048, 16], P(('expert', 'shard'))
- attention_gain_grad: float32 [2048], P(('expert', 'shard'))
- query_gain_grad: float32 [2048], P(('expert', 'shard'))
- key_gain_grad: float32 [2048], P(('expert', 'shard'))
- mixture_gain_grad: float32 [2048], P(('expert', 'shard'))
- w_gate_grad: float32 [16, 2048, 1024], P('expert', 'shard')
- w_up_grad: float32 [16, 2048, 1024], P('expert', 'shard')
- w_down_grad: float32 [16, 1024, 2048], P('expert', 'shard')
Inputs may be any that keep to these rules, and one draw needn't show every extreme that they name: `routes`: each token names 8 different experts. In the rows of one device in one micro-batch (aligned blocks of 96 rows) no expert is named more than 54 times, and in some such block one expert exactly 54 times. `block_ids`: along each sequence the block numbers never fall; each block holds 1 to 256 positions, one block exactly 256.
All inputs are finite; a program needn't handle non-finite values.
Results may differ from a plain program's by a relative error of at most 0.022.
Values may be sent and summed in bfloat16 or wider, within the bound.
No kernel may reach another device: no remote copies, remote signals or barrier semaphores. Data moves between devices by JAX's collectives and lax.ppermute only.
A program may use at most 384 MiB of HBM per device.

v0:
```python
import jax
import jax.numpy as jnp
from jax import lax
from jax.sharding import PartitionSpec as P

HEADS = 16
HEAD_DIM = 128
MICRO = 2


epsilon = 1e-05
rope_base = 10000.0
masked_value = -1e30


def rms_scale(values, gain_row):
    return (
        values * lax.rsqrt(jnp.mean(values * values, axis=-1, keepdims=True) + epsilon) * gain_row
    )


def rotate(values, positions):
    half_dim = values.shape[-1] // 2
    inverse_rate = rope_base ** (-2.0 * jnp.arange(half_dim, dtype=jnp.float32) / values.shape[-1])
    angles = positions.astype(jnp.float32)[:, None] * inverse_rate[None, :]
    cosine = jnp.cos(angles)[:, None, :]
    sine_part = jnp.sin(angles)[:, None, :]
    first_half = values[..., :half_dim]
    second_half = values[..., half_dim:]
    return jnp.concatenate(
        [
            first_half * cosine - second_half * sine_part,
            second_half * cosine + first_half * sine_part,
        ],
        axis=-1,
    )


def swiglu(gate_part, up_part):
    return jax.nn.silu(gate_part) * up_part


def to_low(values):
    return values.astype(jnp.bfloat16)


def matmul(left, right):
    return jnp.dot(left, right, preferred_element_type=jnp.float32)


def times_transpose(left, right):
    return lax.dot_general(
        left, right, (((1,), (1,)), ((), ())), preferred_element_type=jnp.float32
    )


def transpose_times(left, right):
    return lax.dot_general(
        left, right, (((0,), (0,)), ((), ())), preferred_element_type=jnp.float32
    )


def local(
    tokens,
    cotangent,
    block_ids,
    routes,
    w_query,
    w_key,
    w_value,
    w_out,
    router,
    attention_gain,
    query_gain,
    key_gain,
    mixture_gain,
    w_gate,
    w_up,
    w_down,
):
    tok_rows = tokens.shape[1]
    model_width = tokens.shape[2]
    top_count = routes.shape[2]
    expert_count = router.shape[1]
    local_experts = w_gate.shape[0]
    owner_count = lax.axis_size("expert")
    capacity = (tok_rows * top_count * 9 + 8 * expert_count - 1) // (8 * expert_count)
    pair_count = tok_rows * top_count
    head_count = HEADS
    head_size = HEAD_DIM
    score_scale = HEAD_DIM ** (-0.5)
    shard_index = lax.axis_index("shard")
    positions = shard_index * tok_rows + jnp.arange(tok_rows, dtype=jnp.int32)
    earlier = (jnp.arange(pair_count)[:, None] > jnp.arange(pair_count)[None, :]).astype(
        jnp.bfloat16
    )
    expert_ids = jnp.arange(expert_count, dtype=jnp.int32)
    pair_token = jnp.arange(pair_count, dtype=jnp.int32) // top_count
    layer_sums = None
    expert_sums = None
    outputs_list = []
    grads_list = []
    for micro_index in range(MICRO):
        front_layer = (
            lax.all_gather(w_query, ("expert", "shard"), axis=0, tiled=True),
            lax.all_gather(w_key, ("expert", "shard"), axis=0, tiled=True),
            lax.all_gather(w_value, ("expert", "shard"), axis=0, tiled=True),
            lax.all_gather(w_out, ("expert", "shard"), axis=0, tiled=True),
            lax.all_gather(router, ("expert", "shard"), axis=0, tiled=True),
            lax.all_gather(attention_gain, ("expert", "shard"), axis=0, tiled=True),
            lax.all_gather(query_gain, ("expert", "shard"), axis=0, tiled=True),
            lax.all_gather(key_gain, ("expert", "shard"), axis=0, tiled=True),
            lax.all_gather(mixture_gain, ("expert", "shard"), axis=0, tiled=True),
        )
        front_expert = (
            lax.all_gather(w_gate, "shard", axis=1, tiled=True),
            lax.all_gather(w_up, "shard", axis=1, tiled=True),
            lax.all_gather(w_down, "shard", axis=1, tiled=True),
        )
        token_rows = tokens[micro_index].astype(jnp.float32)
        gain_attention = front_layer[5].astype(jnp.float32)
        gain_query = front_layer[6].astype(jnp.float32)
        gain_key = front_layer[7].astype(jnp.float32)
        gain_mixture = front_layer[8].astype(jnp.float32)
        attention_normed, attention_back = jax.vjp(rms_scale, token_rows, gain_attention)
        attention_in = to_low(attention_normed)
        query_linear = matmul(attention_in, front_layer[0])
        key_linear = matmul(attention_in, front_layer[1])
        value_linear = matmul(attention_in, front_layer[2])

        def rotary_piece(linear, gain_row):
            return rotate(
                rms_scale(linear, gain_row).reshape(tok_rows, head_count, head_size), positions
            )

        query_turned, query_back = jax.vjp(rotary_piece, query_linear, gain_query)
        key_turned, key_back = jax.vjp(rotary_piece, key_linear, gain_key)
        query_low = to_low(query_turned)
        key_low = to_low(key_turned)
        value_low = to_low(value_linear).reshape(tok_rows, head_count, head_size)
        all_keys, all_values = (
            lax.all_gather(key_low, "shard", axis=0, tiled=True),
            lax.all_gather(value_low, "shard", axis=0, tiled=True),
        )
        blocks_seq = block_ids[micro_index, 0]
        blocks_own = lax.dynamic_slice_in_dim(blocks_seq, shard_index * tok_rows, tok_rows)
        visible = (blocks_seq[None, :] <= blocks_own[:, None])[None, :, :]

        def masked_scores():
            raw_scores = (
                jnp.einsum("qhd,khd->hqk", query_low, all_keys, preferred_element_type=jnp.float32)
                * score_scale
            )
            return jnp.where(visible, raw_scores, masked_value)

        scores = masked_scores()
        row_peak = jnp.max(scores, axis=-1, keepdims=True)
        exponent = jnp.exp(scores - row_peak)
        row_total = jnp.sum(exponent, axis=-1, keepdims=True)
        softmax_rows = exponent / row_total
        log_total = row_peak + jnp.log(row_total)
        attended = jnp.einsum(
            "hqk,khd->qhd", to_low(softmax_rows), all_values, preferred_element_type=jnp.float32
        )
        attended_low = to_low(attended.reshape(tok_rows, model_width))
        hidden_state = token_rows + matmul(attended_low, front_layer[3])
        mixture_normed, mixture_back = jax.vjp(rms_scale, hidden_state, gain_mixture)
        mixture_in = to_low(mixture_normed)
        logits = matmul(mixture_in, front_layer[4])
        route_now = routes[micro_index]

        def gate_piece(logit_rows):
            return jnp.take_along_axis(jax.nn.softmax(logit_rows, axis=-1), route_now, axis=1)

        gate_values, gate_back = jax.vjp(gate_piece, logits)
        pair_expert = route_now.reshape(-1)
        member = (pair_expert[:, None] == expert_ids[None, :]).astype(jnp.bfloat16)
        before_count = jnp.dot(earlier, member, preferred_element_type=jnp.float32)
        slot_index = jnp.sum(before_count * member.astype(jnp.float32), axis=1).astype(jnp.int32)
        pair_place = pair_expert * capacity + slot_index
        send_rows = (
            jnp.zeros((expert_count * capacity, model_width), jnp.bfloat16)
            .at[pair_place]
            .set(mixture_in[pair_token])
        )
        send_rows = send_rows.reshape(owner_count, local_experts, capacity, model_width)
        received = lax.all_to_all(send_rows, "expert", split_axis=0, concat_axis=0, tiled=True)
        gate_linear = jnp.einsum(
            "sjcd,jdf->sjcf", received, front_expert[0], preferred_element_type=jnp.float32
        )
        up_linear = jnp.einsum(
            "sjcd,jdf->sjcf", received, front_expert[1], preferred_element_type=jnp.float32
        )
        inner_values = to_low(swiglu(gate_linear, up_linear))
        expert_rows = to_low(
            jnp.einsum(
                "sjcf,jfd->sjcd", inner_values, front_expert[2], preferred_element_type=jnp.float32
            )
        )
        returned = lax.all_to_all(
            expert_rows, "expert", split_axis=0, concat_axis=0, tiled=True
        ).reshape(expert_count * capacity, model_width)
        pair_rows = (
            returned[pair_place].reshape(tok_rows, top_count, model_width).astype(jnp.float32)
        )
        mixture_out = jnp.sum(gate_values[:, :, None] * pair_rows, axis=1)
        outputs_list.append((hidden_state + mixture_out).astype(jnp.bfloat16))
        output_grad = cotangent[micro_index].astype(jnp.float32)
        gate_grad = jnp.einsum("tkd,td->tk", pair_rows, output_grad)
        (logit_grad,) = gate_back(gate_grad)
        logit_low = to_low(logit_grad)
        pair_grad = to_low(gate_values[:, :, None] * output_grad[:, None, :]).reshape(
            pair_count, model_width
        )
        grad_send = (
            jnp.zeros((expert_count * capacity, model_width), jnp.bfloat16)
            .at[pair_place]
            .set(pair_grad)
        )
        grad_send = grad_send.reshape(owner_count, local_experts, capacity, model_width)
        grad_received = lax.all_to_all(grad_send, "expert", split_axis=0, concat_axis=0, tiled=True)
        inner_grad = jnp.einsum(
            "sjcd,jfd->sjcf", grad_received, front_expert[2], preferred_element_type=jnp.float32
        )
        grad_down = jnp.einsum(
            "sjcf,sjcd->jfd", inner_values, grad_received, preferred_element_type=jnp.float32
        )
        unused_values, swiglu_back = jax.vjp(swiglu, gate_linear, up_linear)
        gate_linear_grad, up_linear_grad = swiglu_back(inner_grad)
        gate_low = to_low(gate_linear_grad)
        up_low = to_low(up_linear_grad)
        grad_gate = jnp.einsum(
            "sjcd,sjcf->jdf", received, gate_low, preferred_element_type=jnp.float32
        )
        grad_up = jnp.einsum("sjcd,sjcf->jdf", received, up_low, preferred_element_type=jnp.float32)
        rows_grad = jnp.einsum(
            "sjcf,jdf->sjcd", gate_low, front_expert[0], preferred_element_type=jnp.float32
        )
        rows_grad = rows_grad + jnp.einsum(
            "sjcf,jdf->sjcd", up_low, front_expert[1], preferred_element_type=jnp.float32
        )
        returned_grad = lax.all_to_all(
            to_low(rows_grad), "expert", split_axis=0, concat_axis=0, tiled=True
        ).reshape(expert_count * capacity, model_width)
        mixture_in_grad = jnp.sum(
            returned_grad[pair_place].reshape(tok_rows, top_count, model_width).astype(jnp.float32),
            axis=1,
        )
        mixture_in_grad = mixture_in_grad + times_transpose(logit_low, front_layer[4])
        grad_router = transpose_times(mixture_in, logit_low)
        hidden_from_mixture, grad_mixture_gain = mixture_back(mixture_in_grad)
        hidden_grad = output_grad + hidden_from_mixture
        hidden_low = to_low(hidden_grad)
        grad_out = transpose_times(attended_low, hidden_low)
        attended_grad = to_low(times_transpose(hidden_low, front_layer[3])).reshape(
            tok_rows, head_count, head_size
        )
        scores_again = masked_scores()
        softmax_again = jnp.exp(scores_again - log_total)
        weight_grad = jnp.einsum(
            "qhd,khd->hqk", attended_grad, all_values, preferred_element_type=jnp.float32
        )
        row_delta = jnp.sum(softmax_again * weight_grad, axis=-1, keepdims=True)
        score_grad = to_low(softmax_again * (weight_grad - row_delta))
        query_grad = (
            jnp.einsum("hqk,khd->qhd", score_grad, all_keys, preferred_element_type=jnp.float32)
            * score_scale
        )
        keys_grad = (
            jnp.einsum("hqk,qhd->khd", score_grad, query_low, preferred_element_type=jnp.float32)
            * score_scale
        )
        values_grad = jnp.einsum(
            "hqk,qhd->khd", to_low(softmax_again), attended_grad, preferred_element_type=jnp.float32
        )
        own_keys_grad, own_values_grad = (
            lax.psum_scatter(
                keys_grad.astype(jnp.bfloat16), "shard", scatter_dimension=0, tiled=True
            ).astype(jnp.float32),
            lax.psum_scatter(
                values_grad.astype(jnp.bfloat16), "shard", scatter_dimension=0, tiled=True
            ).astype(jnp.float32),
        )
        query_linear_grad, grad_query_gain = query_back(query_grad)
        key_linear_grad, grad_key_gain = key_back(own_keys_grad)
        query_low_grad = to_low(query_linear_grad)
        key_low_grad = to_low(key_linear_grad)
        value_low_grad = to_low(own_values_grad.reshape(tok_rows, model_width))
        grad_query = transpose_times(attention_in, query_low_grad)
        grad_key = transpose_times(attention_in, key_low_grad)
        grad_value = transpose_times(attention_in, value_low_grad)
        attention_in_grad = (
            times_transpose(query_low_grad, front_layer[0])
            + times_transpose(key_low_grad, front_layer[1])
            + times_transpose(value_low_grad, front_layer[2])
        )
        input_from_attention, grad_attention_gain = attention_back(attention_in_grad)
        grads_list.append((hidden_grad + input_from_attention).astype(jnp.bfloat16))
        layer_part = (
            lax.psum_scatter(grad_query, ("expert", "shard"), scatter_dimension=0, tiled=True),
            lax.psum_scatter(grad_key, ("expert", "shard"), scatter_dimension=0, tiled=True),
            lax.psum_scatter(grad_value, ("expert", "shard"), scatter_dimension=0, tiled=True),
            lax.psum_scatter(grad_out, ("expert", "shard"), scatter_dimension=0, tiled=True),
            lax.psum_scatter(grad_router, ("expert", "shard"), scatter_dimension=0, tiled=True),
            lax.psum_scatter(
                grad_attention_gain, ("expert", "shard"), scatter_dimension=0, tiled=True
            ),
            lax.psum_scatter(grad_query_gain, ("expert", "shard"), scatter_dimension=0, tiled=True),
            lax.psum_scatter(grad_key_gain, ("expert", "shard"), scatter_dimension=0, tiled=True),
            lax.psum_scatter(
                grad_mixture_gain, ("expert", "shard"), scatter_dimension=0, tiled=True
            ),
        )
        expert_part = (
            lax.psum_scatter(
                grad_gate.astype(jnp.bfloat16), "shard", scatter_dimension=1, tiled=True
            ).astype(jnp.float32),
            lax.psum_scatter(
                grad_up.astype(jnp.bfloat16), "shard", scatter_dimension=1, tiled=True
            ).astype(jnp.float32),
            lax.psum_scatter(
                grad_down.astype(jnp.bfloat16), "shard", scatter_dimension=1, tiled=True
            ).astype(jnp.float32),
        )
        if layer_sums is None:
            layer_sums = tuple(layer_part)
            expert_sums = tuple(expert_part)
        else:
            layer_sums = tuple(
                (total_now + part_now for total_now, part_now in zip(layer_sums, layer_part))
            )
            expert_sums = tuple(
                (total_now + part_now for total_now, part_now in zip(expert_sums, expert_part))
            )
    return (
        jnp.stack(outputs_list),
        jnp.stack(grads_list),
        layer_sums[0],
        layer_sums[1],
        layer_sums[2],
        layer_sums[3],
        layer_sums[4],
        layer_sums[5],
        layer_sums[6],
        layer_sums[7],
        layer_sums[8],
        expert_sums[0],
        expert_sums[1],
        expert_sums[2],
    )


def solution(mesh):
    placed = (
        P(None, ("expert", "shard"), None),
        P(None, ("expert", "shard"), None),
        P(None, "expert", None),
        P(None, ("expert", "shard"), None),
        P(("expert", "shard"), None),
        P(("expert", "shard"), None),
        P(("expert", "shard"), None),
        P(("expert", "shard"), None),
        P(("expert", "shard"), None),
        P(("expert", "shard")),
        P(("expert", "shard")),
        P(("expert", "shard")),
        P(("expert", "shard")),
        P("expert", "shard", None),
        P("expert", "shard", None),
        P("expert", "shard", None),
    )
    return jax.shard_map(
        local,
        mesh=mesh,
        in_specs=placed,
        out_specs=(
            P(None, ("expert", "shard"), None),
            P(None, ("expert", "shard"), None),
            P(("expert", "shard"), None),
            P(("expert", "shard"), None),
            P(("expert", "shard"), None),
            P(("expert", "shard"), None),
            P(("expert", "shard"), None),
            P(("expert", "shard")),
            P(("expert", "shard")),
            P(("expert", "shard")),
            P(("expert", "shard")),
            P("expert", "shard", None),
            P("expert", "shard", None),
            P("expert", "shard", None),
        ),
        check_vma=False,
    )
```

profile of v0, /device:TPU:2, one launch (start us, length us, event | category | flops | bytes accessed | tf_op | source)
XLA Modules:
  0.0 2777.9 jit_solution(12286728917020021444)
XLA Ops:
  12.9 42.0 %all-reduce.17 = (bf16[2048]{0:T(1024)(128)(2,1)S(1)}, bf16[2048]{0:T(1024)(128)(2,1)S(1)}, bf16[2048]{0:T(1024)(128)(2,1)S(1)}, bf16[2048]{0:T(1024)(128)(2,1)}) all-reduce(bf16[2048]{0:T(1024)(128)(2,1)S(1)} %dynamic-update-slice, bf16[2048]{0:T(1024)(128)(2,1)S(1)} %dynamic-update-slice.2, ...), channel_id=1, replica_groups=mesh['expert'=8,'shard'=4] {'expert','shard'}, use_global_device_ids=true, to_apply=%add.8 | all-reduce | flops 8192 | bytes 32768
  57.8 31.5 %all-gather.17.cloned.1.call-done = bf16[2048,2048]{1,0:T(8,128)(2,1)} async-done(((bf16[64,2048]{1,0:T(8,128)(2,1)}), bf16[2048,2048]{1,0:T(8,128)(2,1)}) %all-gather.17.cloned.1.call-update) | async-done | bytes 8388624 | tf_op jit(solution)/shard_map/all_gather | solution.py:105
  98.0 69.8 %all-gather.19.cloned.1.call-done = bf16[2048,2048]{1,0:T(8,128)(2,1)} async-done(((bf16[64,2048]{1,0:T(8,128)(2,1)}), bf16[2048,2048]{1,0:T(8,128)(2,1)}) %all-gather.19.cloned.1.call-update) | async-done | bytes 8388624 | tf_op jit(solution)/shard_map/all_gather | solution.py:106
  182.7 63.8 %all-gather.13.cloned.1.call-done = bf16[2048,2048]{1,0:T(8,128)(2,1)} async-done(((bf16[64,2048]{1,0:T(8,128)(2,1)}), bf16[2048,2048]{1,0:T(8,128)(2,1)}) %all-gather.13.cloned.1.call-update) | async-done | bytes 8388624 | tf_op jit(solution)/shard_map/all_gather | solution.py:107
  258.8 8.0 all-gather.21.cloned.1.call-done
  271.3 17.2 all-gather.15.cloned.1.call-done
  290.6 77.6 %all-gather.23.cloned.1.call-done = bf16[2048,2048]{1,0:T(8,128)(2,1)} async-done(((bf16[64,2048]{1,0:T(8,128)(2,1)}), bf16[2048,2048]{1,0:T(8,128)(2,1)}) %all-gather.23.cloned.1.call-update) | async-done | bytes 8388624 | tf_op jit(solution)/shard_map/all_gather | solution.py:108
  374.2 22.7 scatter_custom_fusion
  396.9 16.2 reshape.607
  413.1 7.5 copy.93
  426.6 101.0 %all-gather = bf16[32,64,16]{1,2,0:T(8,128)(2,1)S(1)} all-gather(bf16[1,64,16]{1,2,0:T(8,128)(2,1)S(1)} %bitcast.547), channel_id=1, replica_groups=mesh['expert'=8,'shard'=4] {'expert','shard'}, dimensions={0}, use_global_device_ids=true | all-gather | bytes 67584 | tf_op jit(solution)/shard_map/all_gather | solution.py:109
  534.8 12.7 scatter_custom_fusion.2
  552.3 7.5 copy.110
  559.7 7.8 all-to-all-start.4
  567.6 11.1 fusion.14
  578.7 67.7 %all-to-all-done.4 = bf16[8,2,54,2048]{3,1,2,0:T(2,128)(2,1)} async-done(((bf16[8,2,54,2048]{3,1,2,0:T(2,128)(2,1)}), bf16[8,2,54,2048]{3,1,2,0:T(2,128)(2,1)}, u32[]{:S(2)}, u32[]{:S(2)}) %all-to-all-start.4) | async-done | bytes 3538976 | tf_op jit(solution)/shard_map/all_to_all | solution.py:221
  646.4 11.2 fusion.2
  657.6 14.9 fusion.32
  672.5 8.3 convert_bitcast_fusion.1
  693.3 11.0 fusion.10
  704.4 9.9 fusion.70
  719.7 51.5 %all-to-all-done.1 = bf16[8,2,54,2048]{3,1,2,0:T(2,128)(2,1)} async-done(((bf16[8,2,54,2048]{3,1,2,0:T(2,128)(2,1)}), bf16[8,2,54,2048]{3,1,2,0:T(2,128)(2,1)}, u32[]{:S(2)}, u32[]{:S(2)}) %all-to-all-start.1) | async-done | bytes 3538976 | tf_op jit(solution)/shard_map/all_to_all | solution.py:200
  788.3 13.5 all-gather.31.cloned.1.call-done
  828.0 36.6 %scatter_fusion = f32[96,16]{0,1:T(8,128)S(1)} fusion(f32[96,16]{0,1:T(8,128)S(1)} %broadcast_in_dim.57.clone, s32[768]{0:T(1024)S(1)} %reshape.723, f32[768]{0:T(1024)S(1)} %reshape.725), kind=kCustom, calls=%fused_computation.12 | custom fusion | flops 768 | bytes 15360 | tf_op jit(solution)/shard_map/transpose(jvp(jit(take_along_axis)))/scatter-add | solution.py:173
  884.0 29.8 %scatter_custom_fusion.1 = bf16[864,2048]{1,0:T(8,128)(2,1)S(1)} fusion(s32[768]{0:T(1024)} %fusion.218, bf16[96,2048]{1,0:T(8,128)(2,1)} %get-tuple-element.116, s32[1024]{0:T(1024)} %pad_clamp_fusion.2, bf16[]{:T(256)} %constant.89.clone.1), kind=kCustom, calls=%fused_computation.103 | custom fusion | bytes 3539456 | tf_op jit(solution)/shard_map/scatter | solution.py:184
  916.8 7.5 copy.105
  937.9 11.9 scatter_custom_fusion.3
  952.5 7.5 copy.120
  960.0 49.6 %all-to-all-done.2 = bf16[8,2,54,2048]{3,1,2,0:T(2,128)(2,1)} async-done(((bf16[8,2,54,2048]{3,1,2,0:T(2,128)(2,1)}), bf16[8,2,54,2048]{3,1,2,0:T(2,128)(2,1)}, u32[]{:S(2)}, u32[]{:S(2)}) %all-to-all-start.2) | async-done | bytes 3538976 | tf_op jit(solution)/shard_map/all_to_all | solution.py:187
  1014.0 11.1 fusion.12
  1025.1 67.6 %all-to-all-done.6 = bf16[8,2,54,2048]{3,1,2,0:T(2,128)(2,1)S(1)} async-done(((bf16[8,2,54,2048]{3,1,2,0:T(2,128)(2,1)}), bf16[8,2,54,2048]{3,1,2,0:T(2,128)(2,1)S(1)}, u32[]{:S(2)}, u32[]{:S(2)}) %all-to-all-start.6) | async-done | bytes 3538976 | tf_op jit(solution)/shard_map/all_to_all | solution.py:221
  1092.7 8.7 fusion
  1101.4 12.8 fusion.35
  1114.2 8.3 convert_bitcast_fusion
  1132.2 10.9 fusion.8
  1143.1 10.0 fusion.73
  1158.5 52.4 %all-to-all-done.3 = bf16[8,2,54,2048]{3,1,2,0:T(2,128)(2,1)S(1)} async-done(((bf16[8,2,54,2048]{3,1,2,0:T(2,128)(2,1)}), bf16[8,2,54,2048]{3,1,2,0:T(2,128)(2,1)S(1)}, u32[]{:S(2)}, u32[]{:S(2)}) %all-to-all-start.3) | async-done | bytes 3538976 | tf_op jit(solution)/shard_map/all_to_all | solution.py:200
  1242.1 36.6 %scatter_fusion.1 = f32[96,16]{0,1:T(8,128)S(1)} fusion(f32[96,16]{0,1:T(8,128)S(1)} %broadcast_in_dim.57, s32[768]{0:T(1024)S(1)} %reshape.729, f32[768]{0:T(1024)S(1)} %reshape.731), kind=kCustom, calls=%fused_computation.13 | custom fusion | flops 768 | bytes 15360 | tf_op jit(solution)/shard_map/transpose(jvp(jit(take_along_axis)))/scatter-add | solution.py:173
  1282.7 11.3 all-to-all-done.7
  1314.8 6.4 fusion.104
  1326.9 6.4 fusion.105
  1354.4 11.8 bitcast_convert_fusion.5
  1367.7 13.5 bitcast_convert_fusion.4
  1382.7 13.4 bitcast_convert_fusion.3
  1397.6 13.4 bitcast_convert_fusion.2
  1412.5 10.1 bitcast_convert_fusion.1
  1424.1 10.4 bitcast_convert_fusion
  1438.1 8.2 convolution_add_fusion
  1447.5 9.2 fusion.161
  1456.7 14.2 convolution_add_fusion.1
  1488.8 8.3 convolution_add_fusion.2
  1505.3 8.3 convolution_add_fusion.3
  1517.0 56.9 %reduce-scatter.46.cloned.1.call-done = f32[64,16]{1,0:T(8,128)} async-done(((f32[2048,16]{1,0:T(8,128)}), f32[64,16]{1,0:T(8,128)}) %reduce-scatter.46.cloned.1.call-update) | async-done | bytes 4112
  1584.2 6.3 fusion.257
  1603.6 50.0 %all-reduce.16 = (f32[2048]{0:T(1024)S(1)}, f32[2048]{0:T(1024)S(1)}, f32[2048]{0:T(1024)S(1)}, f32[2048]{0:T(1024)S(1)}) all-reduce(f32[2048]{0:T(1024)S(1)} %add.425, f32[2048]{0:T(1024)S(1)} %copy-done.107, f32[2048]{0:T(1024)S(1)} %copy-done.106, ...), channel_id=20, replica_groups=mesh['expert'=8,'shard'=4] {'expert','shard'}, use_global_device_ids=true, to_apply=%region_55.57.clone | all-reduce | flops 8192 | bytes 65536
  1658.6 70.0 %reduce-scatter.28.cloned.1.call-done = bf16[2,512,1024]{2,1,0:T(8,128)(2,1)} async-done(((bf16[2,2048,1024]{2,1,0:T(8,128)(2,1)}), bf16[2,512,1024]{2,1,0:T(8,128)(2,1)}) %reduce-scatter.28.cloned.1.call-update) | async-done | bytes 2097168 | tf_op jit(solution)/shard_map/reduce_scatter | solution.py:315
  1733.8 68.9 %reduce-scatter.30.cloned.1.call-done = bf16[2,512,1024]{2,1,0:T(8,128)(2,1)} async-done(((bf16[2,2048,1024]{2,1,0:T(8,128)(2,1)}), bf16[2,512,1024]{2,1,0:T(8,128)(2,1)}) %reduce-scatter.30.cloned.1.call-update) | async-done | bytes 2097168 | tf_op jit(solution)/shard_map/reduce_scatter | solution.py:318
  1802.6 73.9 %reduce-scatter.32.cloned.1.call-done = bf16[2,512,1024]{2,1,0:T(8,128)(2,1)} async-done(((bf16[2,2048,1024]{2,1,0:T(8,128)(2,1)}), bf16[2,512,1024]{2,1,0:T(8,128)(2,1)}) %reduce-scatter.32.cloned.1.call-update) | async-done | bytes 2097168 | tf_op jit(solution)/shard_map/reduce_scatter | solution.py:318
  1881.6 68.9 %reduce-scatter.34.cloned.1.call-done = bf16[2,256,2048]{2,1,0:T(8,128)(2,1)} async-done(((bf16[2,1024,2048]{2,1,0:T(8,128)(2,1)}), bf16[2,256,2048]{2,1,0:T(8,128)(2,1)}) %reduce-scatter.34.cloned.1.call-update) | async-done | bytes 2097168 | tf_op jit(solution)/shard_map/reduce_scatter | solution.py:321
  1950.5 74.0 %reduce-scatter.36.cloned.1.call-done = bf16[2,256,2048]{2,1,0:T(8,128)(2,1)} async-done(((bf16[2,1024,2048]{2,1,0:T(8,128)(2,1)}), bf16[2,256,2048]{2,1,0:T(8,128)(2,1)}) %reduce-scatter.36.cloned.1.call-update) | async-done | bytes 2097168 | tf_op jit(solution)/shard_map/reduce_scatter | solution.py:321
  2029.6 179.1 %reduce-scatter.44.cloned.1.call-done = f32[64,2048]{1,0:T(8,128)} async-done(((f32[2048,2048]{1,0:T(8,128)}), f32[64,2048]{1,0:T(8,128)}) %reduce-scatter.44.cloned.1.call-update) | async-done | bytes 524304 | tf_op jit(solution)/shard_map/reduce_scatter | solution.py:303
  2208.7 187.4 %reduce-scatter.42.cloned.1.call-done = f32[64,2048]{1,0:T(8,128)} async-done(((f32[2048,2048]{1,0:T(8,128)}), f32[64,2048]{1,0:T(8,128)}) %reduce-scatter.42.cloned.1.call-update) | async-done | bytes 524304 | tf_op jit(solution)/shard_map/reduce_scatter | solution.py:302
  2396.0 187.8 %reduce-scatter.40.cloned.1.call-done = f32[64,2048]{1,0:T(8,128)} async-done(((f32[2048,2048]{1,0:T(8,128)}), f32[64,2048]{1,0:T(8,128)}) %reduce-scatter.40.cloned.1.call-update) | async-done | bytes 524304 | tf_op jit(solution)/shard_map/reduce_scatter | solution.py:301
  2583.9 187.0 %reduce-scatter.38.cloned.1.call-done = f32[64,2048]{1,0:T(8,128)} async-done(((f32[2048,2048]{1,0:T(8,128)}), f32[64,2048]{1,0:T(8,128)}) %reduce-scatter.38.cloned.1.call-update) | async-done | bytes 524304 | tf_op jit(solution)/shard_map/reduce_scatter | solution.py:300
  (601 shorter events, 359.8 us)
Async XLA Ops:
  7.2 82.1 %all-gather.17.cloned.1.call-start = ((), (), s32[]{:S(2)}) async-start(), calls=%async_computation.25 | async-start | bytes 8650752 | tf_op jit(solution)/shard_map/all_gather | solution.py:105
  7.9 159.9 %all-gather.19.cloned.1.call-start = ((), (), s32[]{:S(2)}) async-start(), calls=%async_computation.26 | async-start | bytes 8650752 | tf_op jit(solution)/shard_map/all_gather | solution.py:106
  8.7 237.8 %all-gather.13.cloned.1.call-start = ((), (), s32[]{:S(2)}) async-start(), calls=%async_computation.23 | async-start | bytes 8650752 | tf_op jit(solution)/shard_map/all_gather | solution.py:107
  9.4 257.4 %all-gather.21.cloned.1.call-start = ((), (), s32[]{:S(2)}) async-start(), calls=%async_computation.27 | async-start | bytes 1966080 | tf_op jit(solution)/shard_map/all_gather | solution.py:142
  54.9 721.3 %copy-start.28 = (f32[2048]{0:T(1024)}, f32[2048]{0:T(1024)S(1)}, u32[]{:S(2)}) copy-start(f32[2048]{0:T(1024)S(1)} %convert_element_type.355) | copy-start | bytes 24580
  54.9 120.4 %copy-start.87 = (f32[2048]{0:T(1024)}, f32[2048]{0:T(1024)S(1)}, u32[]{:S(2)}) copy-start(f32[2048]{0:T(1024)S(1)} %convert_element_type.360) | copy-start | bytes 24580
  54.9 42.0 %copy-start.85 = (f32[2048]{0:T(1024)}, f32[2048]{0:T(1024)S(1)}, u32[]{:S(2)}) copy-start(f32[2048]{0:T(1024)S(1)} %convert_element_type.358) | copy-start | bytes 24580
  56.4 111.5 %copy-start.89 = (f32[96]{0:T(128)}, f32[96]{0:T(128)S(1)}, u32[]{:S(2)}) copy-start(f32[96]{0:T(128)S(1)} %fusion.219) | copy-start | bytes 1156
  56.9 116.2 %copy-start.94 = (f32[96]{0:T(128)}, f32[96]{0:T(128)S(1)}, u32[]{:S(2)}) copy-start(f32[96]{0:T(128)S(1)} %fusion.223) | copy-start | bytes 1156
  57.8 36.8 %copy-start.2 = (bf16[2,96,2048]{2,1,0:T(8,128)(2,1)S(1)}, bf16[2,96,2048]{2,1,0:T(8,128)(2,1)}, u32[]{:S(2)}) copy-start(bf16[2,96,2048]{2,1,0:T(8,128)(2,1)} %param.18) | copy-start | bytes 2359300
  177.7 68.8 %copy-start.90 = (f32[96]{0:T(128)S(1)}, f32[96]{0:T(128)}, u32[]{:S(2)}) copy-start(f32[96]{0:T(128)} %copy-done.89) | copy-start | bytes 1156
  181.4 85.4 %copy-start.40 = (bf16[96,16,64]{2,0,1:T(8,128)(2,1)}, bf16[96,16,64]{2,0,1:T(8,128)(2,1)S(1)}, u32[]{:S(2)}) copy-start(bf16[96,16,64]{2,0,1:T(8,128)(2,1)S(1)} %get-tuple-element.58) | copy-start | bytes 589828
  182.3 106.1 %all-gather.15.cloned.1.call-start = ((), (), s32[]{:S(2)}) async-start(), calls=%async_computation.24 | async-start | bytes 1966080 | tf_op jit(solution)/shard_map/all_gather | solution.py:143
  252.2 115.9 %all-gather.23.cloned.1.call-start = ((), (), s32[]{:S(2)}) async-start(), calls=%async_computation.28 | async-start | bytes 8650752 | tf_op jit(solution)/shard_map/all_gather | solution.py:108
  252.8 314.8 %all-gather.27.cloned.1.call-start = ((), (), s32[]{:S(2)}) async-start(), calls=%async_computation.30 | async-start | bytes 10485760 | tf_op jit(solution)/shard_map/all_gather | solution.py:117
  253.6 325.2 %all-gather.29.cloned.1.call-start = ((), (), s32[]{:S(2)}) async-start(), calls=%async_computation.31 | async-start | bytes 10485760 | tf_op jit(solution)/shard_map/all_gather | solution.py:118
  254.3 118.9 %copy-start.80 = (f32[2048]{0:T(1024)}, f32[2048]{0:T(1024)S(1)}, u32[]{:S(2)}) copy-start(f32[2048]{0:T(1024)S(1)} %convert_element_type.365) | copy-start | bytes 24580
  269.2 21.3 copy-start.4
  290.6 82.6 %copy-start.54 = (bf16[16,12,8,128]{3,2,1,0:T(8,128)(2,1)}, bf16[16,12,8,128]{3,2,1,0:T(8,128)(2,1)S(1)}, u32[]{:S(2)}) copy-start(bf16[16,12,8,128]{3,2,1,0:T(8,128)(2,1)S(1)} %fusion.100) | copy-start | bytes 1179652
  373.2 39.9 %copy-start.148 = (f32[96]{0:T(128)}, f32[96]{0:T(128)S(1)}, u32[]{:S(2)}) copy-start(f32[96]{0:T(128)S(1)} %get-tuple-element.137) | copy-start | bytes 1156
  373.2 39.9 %copy-start.124 = (f32[96]{0:T(128)}, f32[96]{0:T(128)S(1)}, u32[]{:S(2)}) copy-start(f32[96]{0:T(128)S(1)} %fusion.222) | copy-start | bytes 1156
  374.2 154.9 %copy-start.52 = (bf16[96,2048]{1,0:T(8,128)(2,1)}, bf16[96,2048]{1,0:T(8,128)(2,1)S(1)}, u32[]{:S(2)}) copy-start(bf16[96,2048]{1,0:T(8,128)(2,1)S(1)} %multiply_convert_fusion.5) | copy-start | bytes 1179652
  420.6 107.2 %copy-start.57 = (bf16[2,96,2048]{2,1,0:T(8,128)(2,1)S(1)}, bf16[2,96,2048]{2,1,0:T(8,128)(2,1)}, u32[]{:S(2)}) copy-start(bf16[2,96,2048]{2,1,0:T(8,128)(2,1)} %param.19) | copy-start | bytes 2359300
  420.6 139.2 %all-to-all-start = ((bf16[8,2,54,2048]{3,1,2,0:T(2,128)(2,1)}), bf16[8,2,54,2048]{3,1,2,0:T(2,128)(2,1)}, u32[]{:S(2)}, u32[]{:S(2)}) async-start(bf16[8,2,54,2048]{3,1,2,0:T(2,128)(2,1)} %copy.93), calls=%async_computation | async-start | bytes 7077888 | tf_op jit(solution)/shard_map/all_to_all | solution.py:187
  425.7 231.9 %all-gather.25.cloned.1.call-start = ((), (), s32[]{:S(2)}) async-start(), calls=%async_computation.29 | async-start | bytes 10485760 | tf_op jit(solution)/shard_map/all_gather | solution.py:116
  529.4 258.3 %copy-start.129 = (f32[96]{0:T(128)}, f32[96]{0:T(128)S(1)}, u32[]{:S(2)}) copy-start(f32[96]{0:T(128)S(1)} %fusion.213) | copy-start | bytes 1156
  559.7 86.6 %all-to-all-start.4 = ((bf16[8,2,54,2048]{3,1,2,0:T(2,128)(2,1)}), bf16[8,2,54,2048]{3,1,2,0:T(2,128)(2,1)}, u32[]{:S(2)}, u32[]{:S(2)}) async-start(bf16[8,2,54,2048]{3,1,2,0:T(2,128)(2,1)} %copy.110), calls=%async_computation.4 | async-start | bytes 7077888 | tf_op jit(solution)/shard_map/all_to_all | solution.py:221
  686.2 85.1 %all-to-all-start.1 = ((bf16[8,2,54,2048]{3,1,2,0:T(2,128)(2,1)}), bf16[8,2,54,2048]{3,1,2,0:T(2,128)(2,1)}, u32[]{:S(2)}, u32[]{:S(2)}) async-start(bf16[8,2,54,2048]{3,1,2,0:T(2,128)(2,1)} %copy.96), calls=%async_computation.1 | async-start | bytes 7077888 | tf_op jit(solution)/shard_map/all_to_all | solution.py:200
  692.3 91.9 %all-gather.33.cloned.1.call-start = ((), (), s32[]{:S(2)}) async-start(), calls=%async_computation.33 | async-start | bytes 1966080 | tf_op jit(solution)/shard_map/all_gather | solution.py:142
  719.7 56.5 %copy-start.95 = (f32[96]{0:T(128)S(1)}, f32[96]{0:T(128)}, u32[]{:S(2)}) copy-start(f32[96]{0:T(128)} %copy-done.94) | copy-start | bytes 1156
  771.2 93.4 %all-to-all-start.5 = ((bf16[8,2,54,2048]{3,1,2,0:T(2,128)(2,1)}), bf16[8,2,54,2048]{3,1,2,0:T(2,128)(2,1)}, u32[]{:S(2)}, u32[]{:S(2)}) async-start(bf16[8,2,54,2048]{3,1,2,0:T(2,128)(2,1)} %copy.112), calls=%async_computation.5 | async-start | bytes 7077888 | tf_op jit(solution)/shard_map/all_to_all | solution.py:242
  776.2 25.6 all-gather.31.cloned.1.call-start
  827.9 36.7 %copy-start.111 = (f32[96]{0:T(128)S(1)}, f32[96]{0:T(128)}, u32[]{:S(2)}) copy-start(f32[96]{0:T(128)} %copy-done.110) | copy-start | bytes 1156
  827.9 36.7 %copy-start.152 = (f32[96]{0:T(128)S(1)}, f32[96]{0:T(128)}, u32[]{:S(2)}) copy-start(f32[96]{0:T(128)} %multiply_divide_fusion.1) | copy-start | bytes 1156
  828.0 36.7 %copy-start.130 = (f32[96]{0:T(128)S(1)}, f32[96]{0:T(128)}, u32[]{:S(2)}) copy-start(f32[96]{0:T(128)} %copy-done.129) | copy-start | bytes 1156
  924.3 85.3 %all-to-all-start.2 = ((bf16[8,2,54,2048]{3,1,2,0:T(2,128)(2,1)}), bf16[8,2,54,2048]{3,1,2,0:T(2,128)(2,1)}, u32[]{:S(2)}, u32[]{:S(2)}) async-start(bf16[8,2,54,2048]{3,1,2,0:T(2,128)(2,1)} %copy.105), calls=%async_computation.2 | async-start | bytes 7077888 | tf_op jit(solution)/shard_map/all_to_all | solution.py:187
  1009.6 83.1 %all-to-all-start.6 = ((bf16[8,2,54,2048]{3,1,2,0:T(2,128)(2,1)}), bf16[8,2,54,2048]{3,1,2,0:T(2,128)(2,1)S(1)}, u32[]{:S(2)}, u32[]{:S(2)}) async-start(bf16[8,2,54,2048]{3,1,2,0:T(2,128)(2,1)} %copy.120), calls=%async_computation.8 | async-start | bytes 7077888 | tf_op jit(solution)/shard_map/all_to_all | solution.py:221
  1128.0 82.9 %all-to-all-start.3 = ((bf16[8,2,54,2048]{3,1,2,0:T(2,128)(2,1)}), bf16[8,2,54,2048]{3,1,2,0:T(2,128)(2,1)S(1)}, u32[]{:S(2)}, u32[]{:S(2)}) async-start(bf16[8,2,54,2048]{3,1,2,0:T(2,128)(2,1)} %copy.108), calls=%async_computation.3 | async-start | bytes 7077888 | tf_op jit(solution)/shard_map/all_to_all | solution.py:200
  1210.9 83.1 %all-to-all-start.7 = ((bf16[8,2,54,2048]{3,1,2,0:T(2,128)(2,1)}), bf16[8,2,54,2048]{3,1,2,0:T(2,128)(2,1)}, u32[]{:S(2)}, u32[]{:S(2)}) async-start(bf16[8,2,54,2048]{3,1,2,0:T(2,128)(2,1)} %copy.122), calls=%async_computation.9 | async-start | bytes 7077888 | tf_op jit(solution)/shard_map/all_to_all | solution.py:242
  1215.9 230.6 %reduce-scatter.20.cloned.1.call-start = ((), (), s32[]{:S(2)}) async-start(), calls=%async_computation.35 | async-start | bytes 1966080 | tf_op jit(solution)/shard_map/reduce_scatter | solution.py:280
  1242.0 36.7 %copy-start.83 = (f32[96,16]{0,1:T(8,128)S(1)}, f32[96,16]{0,1:T(8,128)}, u32[]{:S(2)}) copy-start(f32[96,16]{0,1:T(8,128)} %copy-done.82) | copy-start | bytes 18436
  1242.0 36.7 %copy-start.113 = (f32[96]{0:T(128)S(1)}, f32[96]{0:T(128)}, u32[]{:S(2)}) copy-start(f32[96]{0:T(128)} %copy-done.112) | copy-start | bytes 1156
  1242.0 36.7 %copy-start.153 = (f32[96]{0:T(128)S(1)}, f32[96]{0:T(128)}, u32[]{:S(2)}) copy-start(f32[96]{0:T(128)} %multiply_divide_fusion) | copy-start | bytes 1156
  1242.0 36.7 %copy-start.132 = (f32[96]{0:T(128)S(1)}, f32[96]{0:T(128)}, u32[]{:S(2)}) copy-start(f32[96]{0:T(128)} %copy-done.131) | copy-start | bytes 1156
  1242.1 36.8 %copy-start.24 = (bf16[768,2048]{1,0:T(8,128)(2,1)S(1)}, bf16[768,2048]{1,0:T(8,128)(2,1)}, u32[]{:S(2)}) copy-start(bf16[768,2048]{1,0:T(8,128)(2,1)} %gather_fusion.1) | copy-start | bytes 9437188
  1242.1 36.8 %copy-start.79 = (f32[96,8]{1,0:T(8,128)S(1)}, f32[96,8]{1,0:T(8,128)}, u32[]{:S(2)}) copy-start(f32[96,8]{1,0:T(8,128)} %copy-done.78) | copy-start | bytes 9220
  1278.8 32.5 %copy-start.102 = (bf16[96,16]{0,1:T(8,128)(2,1)}, bf16[96,16]{0,1:T(8,128)(2,1)S(1)}, u32[]{:S(2)}) copy-start(bf16[96,16]{0,1:T(8,128)(2,1)S(1)} %multiply_convert_fusion.6) | copy-start | bytes 9220
  1326.1 130.6 %reduce-scatter.24.cloned.1.call-start = ((), (), s32[]{:S(2)}) async-start(), calls=%async_computation.37 | async-start | bytes 1966080 | tf_op jit(solution)/shard_map/reduce_scatter | solution.py:280
  1338.9 136.9 %reduce-scatter.22.cloned.1.call-start = ((), (), s32[]{:S(2)}) async-start(), calls=%async_computation.36 | async-start | bytes 1966080 | tf_op jit(solution)/shard_map/reduce_scatter | solution.py:277
  1346.0 131.8 %reduce-scatter.18.cloned.1.call-start = ((), (), s32[]{:S(2)}) async-start(), calls=%async_computation.34 | async-start | bytes 1966080 | tf_op jit(solution)/shard_map/reduce_scatter | solution.py:277
  1352.5 221.5 %reduce-scatter.46.cloned.1.call-start = ((), (), s32[]{:S(2)}) async-start(), calls=%async_computation.48 | async-start | bytes 1081344
  1354.3 304.3 %reduce-scatter.26.cloned.1.call-start = ((), (), s32[]{:S(2)}) async-start(), calls=%async_computation.38 | async-start | bytes 10485760 | tf_op jit(solution)/shard_map/reduce_scatter | solution.py:315
  1366.2 362.4 %reduce-scatter.28.cloned.1.call-start = ((), (), s32[]{:S(2)}) async-start(), calls=%async_computation.39 | async-start | bytes 10485760 | tf_op jit(solution)/shard_map/reduce_scatter | solution.py:315
  1381.2 421.4 %reduce-scatter.30.cloned.1.call-start = ((), (), s32[]{:S(2)}) async-start(), calls=%async_computation.40 | async-start | bytes 10485760 | tf_op jit(solution)/shard_map/reduce_scatter | solution.py:318
  1396.1 480.4 %reduce-scatter.32.cloned.1.call-start = ((), (), s32[]{:S(2)}) async-start(), calls=%async_computation.41 | async-start | bytes 10485760 | tf_op jit(solution)/shard_map/reduce_scatter | solution.py:318
  1411.0 539.5 %reduce-scatter.34.cloned.1.call-start = ((), (), s32[]{:S(2)}) async-start(), calls=%async_computation.42 | async-start | bytes 10485760 | tf_op jit(solution)/shard_map/reduce_scatter | solution.py:321
  1422.6 601.9 %reduce-scatter.36.cloned.1.call-start = ((), (), s32[]{:S(2)}) async-start(), calls=%async_computation.43 | async-start | bytes 10485760 | tf_op jit(solution)/shard_map/reduce_scatter | solution.py:321
  1434.5 774.2 %reduce-scatter.44.cloned.1.call-start = ((), (), s32[]{:S(2)}) async-start(), calls=%async_computation.47 | async-start | bytes 17301504 | tf_op jit(solution)/shard_map/reduce_scatter | solution.py:303
  1446.3 949.7 %reduce-scatter.42.cloned.1.call-start = ((), (), s32[]{:S(2)}) async-start(), calls=%async_computation.46 | async-start | bytes 17301504 | tf_op jit(solution)/shard_map/reduce_scatter | solution.py:302
  1470.9 1113.0 %reduce-scatter.40.cloned.1.call-start = ((), (), s32[]{:S(2)}) async-start(), calls=%async_computation.45 | async-start | bytes 17301504 | tf_op jit(solution)/shard_map/reduce_scatter | solution.py:301
  1497.1 1273.9 %reduce-scatter.38.cloned.1.call-start = ((), (), s32[]{:S(2)}) async-start(), calls=%async_computation.44 | async-start | bytes 17301504 | tf_op jit(solution)/shard_map/reduce_scatter | solution.py:300
  1513.6 64.3 %copy-start.48 = (bf16[96,2048]{1,0:T(8,128)(2,1)S(1)}, bf16[96,2048]{1,0:T(8,128)(2,1)}, u32[]{:S(2)}) copy-start(bf16[96,2048]{1,0:T(8,128)(2,1)} %copy-done.47) | copy-start | bytes 1179652
  1599.7 56.3 %copy-start.137 = (f32[96]{0:T(128)S(1)}, f32[96]{0:T(128)}, u32[]{:S(2)}) copy-start(f32[96]{0:T(128)} %copy-done.136) | copy-start | bytes 1156
  1599.7 56.3 %copy-start.139 = (f32[96]{0:T(128)S(1)}, f32[96]{0:T(128)}, u32[]{:S(2)}) copy-start(f32[96]{0:T(128)} %copy-done.138) | copy-start | bytes 1156
  (137 other events, 600.0 us)
Sparse Core Ops, SparseCore 0:
  10.8 78.3 all-gather.16
  92.1 75.6 all-gather.18
  170.7 75.6 all-gather.12
  248.4 18.2 all-gather.20
  268.8 19.6 all-gather.14
  291.1 77.0 all-gather.22
  369.7 56.9 all-gather.26
  428.3 58.5 all-gather.28
  488.4 58.9 all-gather.24
  694.9 19.5 all-gather.32
  782.1 19.5 all-gather.30
  1326.2 26.1 reduce-scatter.19
  1354.9 27.9 reduce-scatter.23
  1385.9 27.9 reduce-scatter.21
  1416.9 28.0 reduce-scatter.17
  1447.0 126.8 reduce-scatter.45
  1576.4 78.3 reduce-scatter.25
  1657.2 71.4 reduce-scatter.27
  1731.2 71.3 reduce-scatter.29
  1805.1 71.3 reduce-scatter.31
  1879.1 71.3 reduce-scatter.33
  1953.1 71.3 reduce-scatter.35
  2027.4 181.2 reduce-scatter.43
  2211.4 184.5 reduce-scatter.41
  2398.9 184.9 reduce-scatter.39
  2586.6 184.2 reduce-scatter.37
where the time goes:
time: 2790 us; the launch traced here: 2780 us
  waiting for transfers between devices  1740 us (62%)
  matrix products  369 us (13%)
  local copies, waits for them, and re-layouts  232 us (8%)
  blocking collectives  193 us (7%)
  other arithmetic  179 us (6%)
  starting transfers between devices  46.7 us (2%)
    reduce_scatter x1, waiting for transfers between devices, local(): lax.psum_scatter(grad_key, ('expert', 'shard'), scatter_dimension=0, tile...  188 us
    reduce_scatter x1, waiting for transfers between devices, local(): lax.psum_scatter(grad_value, ('expert', 'shard'), scatter_dimension=0, ti...  187 us
    reduce_scatter x1, waiting for transfers between devices, local(): lax.psum_scatter(grad_query, ('expert', 'shard'), scatter_dimension=0, ti...  187 us
    reduce_scatter x1, waiting for transfers between devices, local(): lax.psum_scatter(grad_out, ('expert', 'shard'), scatter_dimension=0, tile...  179 us
    reduce_scatter x2, waiting for transfers between devices, local(): lax.psum_scatter(grad_down.astype(jnp.bfloat16), 'shard', scatter_dimensi...  143 us
    reduce_scatter x2, waiting for transfers between devices, local(): lax.psum_scatter(grad_up.astype(jnp.bfloat16), 'shard', scatter_dimension...  143 us
    all_to_all x2, waiting for transfers between devices, local(): lax.all_to_all(grad_send, 'expert', split_axis=0, concat_axis=0, tiled=True)  135 us
    all_to_all x2, waiting for transfers between devices, local(): lax.all_to_all(expert_rows, 'expert', split_axis=0, concat_axis=0, tiled=...  104 us
  transfers between devices with their start and end apart: 34, of which 23 were waited for; matrix products, arithmetic and copies ran while one was open for 22% of the time, Pallas kernels for 0%

commit v1 on v0

v1 whole, which is shorter than its diff:
```python
import jax
import jax.numpy as jnp
from jax import lax
from jax.experimental import pallas as pl
from jax.experimental.pallas import tpu as pltpu
from jax.sharding import PartitionSpec as P

HEADS = 16
HEAD_DIM = 128
EPSILON = 1e-05
ROPE_BASE = 10000.0
MASKED = -1e30
BOTH = ("expert", "shard")

f32 = jnp.float32
bf16 = jnp.bfloat16


def dot(left, right, dims):
    return lax.dot_general(left, right, (dims, ((), ())), preferred_element_type=f32)


def nn(left, right):
    return dot(left, right, ((1,), (0,)))


def nt(left, right):
    return dot(left, right, ((1,), (1,)))


def tn(left, right):
    return dot(left, right, ((0,), (0,)))


def swap_core(values):
    return lax.ppermute(values, "shard", [(s, s ^ 1) for s in range(4)])


def swap_side(values):
    return lax.ppermute(values, "shard", [(s, s ^ 2) for s in range(4)])


def gather_shard(values):
    near = swap_core(values)
    far = swap_side(values)
    return [values, near, far, swap_core(far)]


def scatter_shard(parts):
    near = swap_core(jnp.stack([parts[1], parts[3]]).astype(bf16)).astype(f32)
    far = swap_side((parts[2] + near[1]).astype(bf16)).astype(f32)
    return parts[0] + near[0] + far


def tie(*values):
    return lax.optimization_barrier(values)


def sum_rows(values, core, side, tok):
    def reorder(v):
        v = v.reshape(2, -1, 2, 2, tok)
        v = jnp.where(core == 1, jnp.concatenate([v[:, :, :, 1:], v[:, :, :, :1]], axis=3), v)
        v = jnp.where(side == 1, jnp.concatenate([v[:, :, 1:], v[:, :, :1]], axis=2), v)
        return v.reshape(values.shape)

    return reorder(jnp.sum(lax.all_gather(reorder(values), "shard", axis=0), axis=0))


def inverse_rms(values):
    return lax.rsqrt(jnp.mean(values * values, axis=-1, keepdims=True) + EPSILON)


def attend_body(q_ref, k_ref, v_ref, qi_ref, ki_ref, gq_ref, gk_ref, cos_ref, sin_ref, idq_ref, idk_ref,
                qr_ref, kr_ref, vr_ref, o_ref, lse_ref):
    cos = cos_ref[...]
    sin = sin_ref[...]
    half = HEAD_DIM // 2

    def rope(values):
        return (values * cos + pltpu.roll(values, half, 1) * sin).astype(bf16)

    q_r = rope(q_ref[...] * qi_ref[...] * gq_ref[...])
    k_r = rope(k_ref[...] * ki_ref[...] * gk_ref[...])
    v_r = v_ref[...].astype(bf16)
    qr_ref[...] = q_r
    kr_ref[...] = k_r
    vr_ref[...] = v_r
    scores = jnp.where(idk_ref[0] <= idq_ref[...], nt(q_r, k_r) * HEAD_DIM ** (-0.5), MASKED)
    peak = jnp.max(scores, axis=-1, keepdims=True)
    weight = jnp.exp(scores - peak)
    total = jnp.sum(weight, axis=-1, keepdims=True)
    o_ref[...] = nn((weight / total).astype(bf16), v_r).astype(bf16)
    lse_ref[0] = peak + jnp.log(total)


def attend(linear, q_inv, k_inv, gain_q, gain_k, cos, sin, ids, heads):
    micro, length = ids.shape
    cols = heads * HEAD_DIM
    total = micro * length
    head = lambda base: pl.BlockSpec((length, HEAD_DIM), lambda m, h: (m, base + h))
    column = pl.BlockSpec((length, 1), lambda m, h: (m, 0))
    gain = pl.BlockSpec((1, HEAD_DIM), lambda m, h: (0, h))
    angle = pl.BlockSpec((length, HEAD_DIM), lambda m, h: (0, 0))
    keys = pl.BlockSpec((1, 1, length), lambda m, h: (m, 0, 0))
    low = jax.ShapeDtypeStruct((total, cols), bf16)
    return pl.pallas_call(
        attend_body,
        grid=(micro, heads),
        in_specs=[head(0), head(heads), head(2 * heads), column, column, gain, gain, angle, angle, column, keys],
        out_specs=[head(0)] * 4 + [pl.BlockSpec((1, length, 1), lambda m, h: (m * heads + h, 0, 0))],
        out_shape=[low] * 4 + [jax.ShapeDtypeStruct((micro * heads, length, 1), f32)],
    )(linear, linear, linear, q_inv, k_inv, gain_q, gain_k, cos, sin, ids.reshape(total, 1), ids[:, None, :])


def attend_back_body(dh_ref, wo_ref, q_ref, k_ref, qr_ref, kr_ref, vr_ref, lse_ref, qi_ref, ki_ref, gq_ref, gk_ref,
                     cos_ref, sin_ref, idq_ref, idk_ref, wq_ref, wk_ref, dv_ref, pq_ref, pk_ref, sum_ref):
    cos = cos_ref[...]
    sin = sin_ref[...]
    half = HEAD_DIM // 2
    scale = HEAD_DIM ** (-0.5)
    q_r = qr_ref[...]
    k_r = kr_ref[...]
    d_o = nt(dh_ref[...], wo_ref[...]).astype(bf16)
    scores = jnp.where(idk_ref[0] <= idq_ref[...], nt(q_r, k_r) * scale, MASKED)
    prob = jnp.exp(scores - lse_ref[0])
    d_prob = nt(d_o, vr_ref[...])
    delta = jnp.sum(prob * d_prob, axis=-1, keepdims=True)
    d_s = (prob * (d_prob - delta)).astype(bf16)
    dv_ref[...] = tn(prob.astype(bf16), d_o).astype(bf16)
    ones = jnp.ones((8, HEAD_DIM), f32)

    def finish(grad, linear, inverse, gain, out_ref, part_ref, at):
        grad = grad * scale
        grad = grad * cos - pltpu.roll(grad, half, 1) * sin
        normed = linear * inverse
        part_ref[...] = jnp.sum(grad * normed, axis=0, keepdims=True)
        grad = grad * gain
        out_ref[...] = grad
        rows = lax.dot_general(
            ones, grad * normed, (((1,), (1,)), ((), ())), precision=lax.Precision.HIGHEST, preferred_element_type=f32
        )

        @pl.when(pl.program_id(0) == 0)
        def _():
            sum_ref[at] = rows

        @pl.when(pl.program_id(0) > 0)
        def _():
            sum_ref[at] = sum_ref[at] + rows

    finish(nn(d_s, k_r), q_ref[...], qi_ref[...], gq_ref[...], wq_ref, pq_ref, 0)
    finish(tn(d_s, q_r), k_ref[...], ki_ref[...], gk_ref[...], wk_ref, pk_ref, 1)


def attend_back(m, dh, w_o, linear, q_r, k_r, v_r, lse, q_inv, k_inv, gain_q, gain_k, cos, sin, ids, heads):
    micro, length = ids.shape
    cols = heads * HEAD_DIM
    width = dh.shape[1]
    head = lambda base: pl.BlockSpec((length, HEAD_DIM), lambda h: (m, base + h))
    column = pl.BlockSpec((length, 1), lambda h: (m, 0))
    gain = pl.BlockSpec((1, HEAD_DIM), lambda h: (0, h))
    angle = pl.BlockSpec((length, HEAD_DIM), lambda h: (0, 0))
    keys = pl.BlockSpec((1, 1, length), lambda h: (m, 0, 0))
    out = pl.BlockSpec((length, HEAD_DIM), lambda h: (0, h))
    return pl.pallas_call(
        attend_back_body,
        grid=(heads,),
        in_specs=[
            pl.BlockSpec((length, width), lambda h: (0, 0)),
            pl.BlockSpec((HEAD_DIM, width), lambda h: (h, 0)),
            head(0), head(heads), head(0), head(0), head(0),
            pl.BlockSpec((1, length, 1), lambda h: (m * heads + h, 0, 0)),
            column, column, gain, gain, angle, angle, column, keys,
        ],
        out_specs=[out, out, out, gain, gain, pl.BlockSpec((2, 8, length), lambda h: (0, 0, 0))],
        out_shape=[
            jax.ShapeDtypeStruct((length, cols), f32),
            jax.ShapeDtypeStruct((length, cols), f32),
            jax.ShapeDtypeStruct((length, cols), bf16),
            jax.ShapeDtypeStruct((1, cols), f32),
            jax.ShapeDtypeStruct((1, cols), f32),
            jax.ShapeDtypeStruct((2, 8, length), f32),
        ],
    )(dh, w_o, linear, linear, q_r, k_r, v_r, lse, q_inv, k_inv, gain_q, gain_k, cos, sin,
      ids.reshape(micro * length, 1), ids[:, None, :])


def project_back_body(wq_ref, wk_ref, dv_ref, q_ref, k_ref, qi_ref, ki_ref, sq_ref, sk_ref, out_ref):
    cols = wq_ref.shape[1]
    q_inv = qi_ref[...]
    k_inv = ki_ref[...]
    out_ref[:, :cols] = (q_inv * (wq_ref[...] - q_ref[...] * (q_inv * sq_ref[...]))).astype(bf16)
    out_ref[:, cols : 2 * cols] = (k_inv * (wk_ref[...] - k_ref[...] * (k_inv * sk_ref[...]))).astype(bf16)
    out_ref[:, 2 * cols :] = dv_ref[...]


def project_back(m, w_q, w_k, d_v, linear, q_inv, k_inv, s_q, s_k):
    length, cols = w_q.shape
    rows = length // 2
    full = pl.BlockSpec((rows, cols), lambda i: (i, 0))
    column = pl.BlockSpec((rows, 1), lambda i: (2 * m + i, 0))
    own = pl.BlockSpec((rows, 1), lambda i: (i, 0))
    return pl.pallas_call(
        project_back_body,
        grid=(2,),
        in_specs=[full, full, full]
        + [pl.BlockSpec((rows, cols), lambda i, b=b: (2 * m + i, b)) for b in range(2)]
        + [column, column, own, own],
        out_specs=pl.BlockSpec((rows, 3 * cols), lambda i: (i, 0)),
        out_shape=jax.ShapeDtypeStruct((length, 3 * cols), bf16),
    )(w_q, w_k, d_v, linear, linear, q_inv, k_inv, s_q, s_k)


def half_expert(weight, core):
    other = lax.dynamic_index_in_dim(weight, 1 - core, 0, keepdims=True)
    return lax.dynamic_update_slice(weight, swap_core(other), (1 - core, 0, 0))


def whole_expert(half, side):
    far = swap_side(half)
    whole = jnp.concatenate([half, half], axis=0)
    whole = lax.dynamic_update_slice(whole, far, (2 * (1 - side), 0, 0))
    return whole.reshape(4 * half.shape[1], half.shape[2])


def send_side(grad, side):
    grad = grad.reshape(4, grad.shape[0] // 4, grad.shape[1])
    return swap_side(lax.dynamic_slice_in_dim(grad, 2 * (1 - side), 2, 0).astype(bf16))


def share_expert_grad(grad, far, core, side):
    grad = grad.reshape(4, grad.shape[0] // 4, grad.shape[1])
    mine = lax.dynamic_slice_in_dim(grad, 2 * side, 2, 0) + far.astype(f32)
    near = swap_core(lax.dynamic_index_in_dim(mine, 1 - core, 0, keepdims=True).astype(bf16))
    return lax.dynamic_update_slice(mine, near.astype(f32), (1 - core, 0, 0))


def local(
    tokens,
    cotangent,
    block_ids,
    routes,
    w_query,
    w_key,
    w_value,
    w_out,
    router,
    attention_gain,
    query_gain,
    key_gain,
    mixture_gain,
    w_gate,
    w_up,
    w_down,
):
    micro, tok, width = tokens.shape
    owners = lax.axis_size("expert")
    experts = router.shape[1]
    capacity = (tok * routes.shape[2] * 9 + 8 * experts - 1) // (8 * experts)
    pack = (2 * capacity + 15) // 16 * 16
    rows = w_query.shape[0]
    cols = width // 4
    heads = HEADS // 4
    length = 4 * tok
    s_index = lax.axis_index("shard")
    e_index = lax.axis_index("expert")
    core = s_index % 2
    side = s_index // 2
    my_expert = 2 * e_index + core

    top = routes.shape[2]
    route_cols = micro * tok * top // rows
    used = 4 + experts + route_cols
    aux_cols = (used + 127) // 128 * 128
    aux = jnp.concatenate(
        [
            jnp.stack([attention_gain, query_gain, key_gain, mixture_gain], axis=1),
            router,
            routes.astype(bf16).transpose(0, 2, 1).reshape(rows, route_cols),
            jnp.zeros((rows, aux_cols - used), bf16),
        ],
        axis=1,
    )
    blocks = [w.reshape(rows, 4, cols) for w in (w_query, w_key, w_value)]
    blocks.append(jnp.broadcast_to(aux[:, None, :], (rows, 4, aux_cols)))
    payload = jnp.concatenate(blocks, axis=2).transpose(1, 0, 2)
    half_gate = half_expert(w_gate, core)
    half_up = half_expert(w_up, core)
    payload, half_gate, half_up = tie(payload, half_gate, half_up)
    payload = lax.all_to_all(payload, "shard", split_axis=0, concat_axis=0, tiled=True)
    front = lax.all_gather(payload.reshape(4 * rows, 3 * cols + aux_cols), "expert", axis=0, tiled=True)
    devices = 4 * owners
    moves = [(b, (b % owners) * 4 + b // owners) for b in range(devices)]
    w_o = lax.all_gather(lax.ppermute(w_out, BOTH, moves), "expert", axis=0, tiled=True)

    gate_w = whole_expert(half_gate, side)
    up_w = whole_expert(half_up, side)
    down_w = whole_expert(half_expert(w_down, core), side)
    chunks = gather_shard(tokens)
    front, gate_w, up_w, *chunks = tie(front, gate_w, up_w, *chunks)
    w_qkv = front[:, : 3 * cols]
    aux_rows = front[:, 3 * cols :].T.astype(f32)
    gain_attention = aux_rows[0]
    gain_query = lax.dynamic_slice_in_dim(aux_rows[1], s_index * cols, cols)
    gain_key = lax.dynamic_slice_in_dim(aux_rows[2], s_index * cols, cols)
    gain_mixture = aux_rows[3]
    router_all = front[:, 3 * cols + 4 : 3 * cols + 4 + experts]


    all_routes = front[:, 3 * cols + 4 + experts : 3 * cols + used].astype(jnp.int32)
    all_routes = all_routes.reshape(owners, 4, micro, top, tok)
    mine = all_routes == my_expert
    mine = jnp.any(mine, axis=3)
    pair = [lax.dynamic_index_in_dim(mine, s_index ^ j, 1, keepdims=False) for j in range(2)]
    mask = jnp.concatenate(pair, axis=2).transpose(1, 0, 2)
    order = jnp.arange(2 * tok)
    earlier = (order[:, None] < order[None, :]).astype(bf16)
    slot = jnp.einsum("met,tu->meu", mask.astype(bf16), earlier, preferred_element_type=f32)
    slot = jnp.where(mask, slot.astype(jnp.int32), -1)
    chosen = (slot[:, :, None, :] == jnp.arange(pack)[None, None, :, None]).astype(bf16)

    x_all = jnp.concatenate(chunks, axis=1).reshape(micro * length, width).astype(f32)
    x_scale = inverse_rms(x_all)
    a_all = (x_all * x_scale * gain_attention).astype(bf16)
    linear = nn(a_all, w_qkv)
    q_lin = linear[:, :cols]
    k_lin = linear[:, cols : 2 * cols]
    sums = jnp.stack([jnp.sum(q_lin * q_lin, axis=1), jnp.sum(k_lin * k_lin, axis=1)])
    sums = sum_rows(sums, core, side, tok)
    inv = lax.rsqrt(sums / width + EPSILON)
    q_inv = inv[0][:, None]
    k_inv = inv[1][:, None]
    chunk_ids = [jnp.bitwise_xor(s_index, j) for j in range(4)]
    positions = jnp.concatenate([c * tok + jnp.arange(tok, dtype=jnp.int32) for c in chunk_ids])
    rate = ROPE_BASE ** (-2.0 * jnp.arange(HEAD_DIM // 2, dtype=f32) / HEAD_DIM)
    angles = positions.astype(f32)[:, None] * rate[None, :]
    cosine = jnp.cos(angles)
    sine = jnp.sin(angles)
    cosine = jnp.concatenate([cosine, cosine], axis=1)
    sine = jnp.concatenate([-sine, sine], axis=1)
    ids = block_ids[:, 0, :]
    ids = jnp.concatenate(
        [lax.dynamic_slice_in_dim(ids, c * tok, tok, axis=1) for c in chunk_ids], axis=1
    )
    gain_query = gain_query[None, :]
    gain_key = gain_key[None, :]
    q_r, k_r, v_r, o_all, lse = attend(
        linear, q_inv, k_inv, gain_query, gain_key, cosine, sine, ids, heads
    )
    branch = nn(o_all, w_o).reshape(micro, 4, tok, width)
    branch = scatter_shard([branch[:, j] for j in range(4)])
    hidden = tokens.astype(f32) + branch
    h_scale = inverse_rms(hidden)
    h_n = hidden * h_scale
    b_own = (h_n * gain_mixture).astype(bf16)

    def gather_pair(own):
        got = lax.all_gather(own, "expert", axis=0, tiled=True).reshape(owners, tok, width)
        return got

    def with_near(got):
        return jnp.concatenate([got, swap_core(got)], axis=1)

    do_first = gather_pair(cotangent[0])
    b_own, do_first = tie(b_own, do_first)
    b_got = [gather_pair(b_own[0]), gather_pair(b_own[1])]
    b_first, down_w, second = tie(b_got[0], down_w, cotangent[1])
    b_got[0] = b_first
    do_got = [do_first, gather_pair(second)]
    out_parts = []
    db_list = []
    kept = []
    router_part = jnp.zeros((width, experts), f32)
    for m in range(micro):
        b_now, do_now = b_got[m], do_got[m]
        if m > 0:
            b_now, do_now, _ = tie(b_now, do_now, db_half)
        b_pair = with_near(b_now)
        do_pair = with_near(do_now)
        pick = chosen[m]
        x_p = jnp.einsum("ert,etd->erd", pick, b_pair, preferred_element_type=f32)
        x_p = x_p.astype(bf16).reshape(owners * pack, width)
        b_flat = b_pair.reshape(owners * 2 * tok, width)
        logits = nn(b_flat, router_all)
        pi = jax.nn.softmax(logits, axis=-1)
        is_mine = (jnp.arange(experts) == my_expert).astype(f32)[None, :]
        gate = jnp.sum(pi * is_mine, axis=1)
        gate_p = jnp.einsum(
            "ert,et->er", chosen[m].astype(f32), gate.reshape(owners, 2 * tok), precision=lax.Precision.HIGHEST
        ).reshape(-1, 1)
        gl = nn(x_p, gate_w)
        ul = nn(x_p, up_w)
        sg = 1.0 / (1.0 + jnp.exp(-gl))
        silu = gl * sg
        act = (silu * ul).astype(bf16)
        y = nn(act, down_w).astype(bf16).astype(f32)
        weighted = (gate_p * y).astype(bf16).reshape(owners, pack, width)
        out_part = jnp.einsum("ert,erd->etd", pick, weighted, preferred_element_type=f32).astype(bf16)
        out_half = out_part[:, :tok].astype(f32) + swap_core(out_part[:, tok:]).astype(f32)
        out_parts.append(out_half.astype(bf16))
        do_p = jnp.einsum("ert,etd->erd", pick, do_pair, preferred_element_type=f32)
        do_p = do_p.reshape(owners * pack, width)
        dgate_p = jnp.sum(y * do_p, axis=1)
        dy = (gate_p * do_p).astype(bf16)
        dact = nt(dy, down_w)
        dgl = (dact * ul * sg * (1.0 + gl * (1.0 - sg))).astype(bf16)
        dul = (dact * silu).astype(bf16)
        drow = (nt(dgl, gate_w) + nt(dul, up_w)).astype(bf16).reshape(owners, pack, width)
        dgate = jnp.einsum(
            "ert,er->et", chosen[m].astype(f32), dgate_p.reshape(owners, pack), precision=lax.Precision.HIGHEST
        ).reshape(-1, 1)
        dz = (dgate * gate[:, None] * (is_mine - pi)).astype(bf16)
        router_part = router_part + tn(b_flat, dz)
        db_part = jnp.einsum("ert,erd->etd", pick, drow, preferred_element_type=f32)
        db_part = db_part + nt(dz, router_all).reshape(owners, 2 * tok, width)
        db_half = (db_part[:, :tok] + swap_core(db_part[:, tok:].astype(bf16)).astype(f32)).astype(bf16)
        db_list.append(lax.psum_scatter(db_half, "expert", scatter_dimension=0, tiled=True)[0])
        kept.append((x_p, act, dy, dgl, dul))
    x_k, act_k, dy_k, dgl_k, dul_k = [jnp.concatenate(group, axis=0) for group in zip(*kept)]
    full_gate = tn(x_k, dgl_k)
    full_up = tn(x_k, dul_k)
    full_down = tn(act_k, dy_k)
    mixture_part = jnp.zeros((width,), f32)
    attention_part = jnp.zeros((width,), f32)
    query_part = jnp.zeros((cols,), f32)
    key_part = jnp.zeros((cols,), f32)
    x_own = tokens.astype(f32)
    own_scale = inverse_rms(x_own)
    dh_rows = []
    dqkv_rows = []
    input_grads = []
    for m in range(micro):
        rows_m = slice(m * length, (m + 1) * length)
        db = db_list[m].astype(f32)
        mixture_part = mixture_part + jnp.sum(db * h_n[m], axis=0)
        w_g = db * gain_mixture
        d_hidden = cotangent[m].astype(f32) + h_scale[m] * (
            w_g - h_n[m] * jnp.mean(w_g * h_n[m], axis=-1, keepdims=True)
        )
        dh_m = jnp.concatenate(gather_shard(d_hidden.astype(bf16)), axis=0)
        dh_m, full_gate, full_up, full_down = tie(dh_m, full_gate, full_up, full_down)
        if m > 0:
            sent = [send_side(full, side) for full in (full_gate, full_up, full_down)]
        dh_rows.append(dh_m)
        w_q, w_k, d_v, part_q, part_k, sums = attend_back(
            m, dh_m, w_o, linear, q_r, k_r, v_r, lse, q_inv, k_inv, gain_query, gain_key, cosine, sine, ids, heads
        )
        query_part = query_part + part_q[0]
        key_part = key_part + part_k[0]
        sums = sum_rows(sums[:, 0], core, side, tok) / width
        d_qkv = project_back(m, w_q, w_k, d_v, linear, q_inv, k_inv, sums[0][:, None], sums[1][:, None])
        if m + 1 < micro:
            db_list[m + 1], d_qkv, *out_parts = tie(db_list[m + 1], d_qkv, *out_parts)
            out_own = lax.psum_scatter(jnp.stack(out_parts), "expert", scatter_dimension=1, tiled=True)
        dqkv_rows.append(d_qkv)
        da_part = nt(d_qkv, w_qkv)
        attention_part = attention_part + jnp.sum(da_part * (x_all * x_scale)[rows_m], axis=0)
        da_part = da_part.reshape(4, tok, width)
        da = scatter_shard([da_part[j] for j in range(4)])
        x_n = x_own[m] * own_scale[m]
        a_g = da * gain_attention
        grad = d_hidden + own_scale[m] * (a_g - x_n * jnp.mean(a_g * x_n, axis=-1, keepdims=True))
        input_grads.append(grad.astype(bf16))
    input_grad = jnp.stack(input_grads)
    dh_all = jnp.concatenate(dh_rows, axis=0)
    d_qkv = jnp.concatenate(dqkv_rows, axis=0)
    grad_wo = tn(o_all, dh_all).astype(bf16)
    grad_wo = grad_wo.reshape(owners, rows, 4, cols).transpose(0, 2, 1, 3).reshape(width, cols)

    blank = jnp.zeros((width,), f32)
    gains = jnp.stack(
        [
            attention_part,
            lax.dynamic_update_slice(blank, query_part, (s_index * cols,)),
            lax.dynamic_update_slice(blank, key_part, (s_index * cols,)),
            mixture_part,
        ],
        axis=1,
    )
    (aux_grad,) = tie(
        jnp.concatenate([gains, router_part, jnp.zeros((width, aux_cols - 4 - experts), f32)], axis=1).astype(bf16)
    )
    grad_payload = jnp.concatenate([tn(a_all, d_qkv).astype(bf16), grad_wo, aux_grad], axis=1)
    grad_payload, out_own = tie(grad_payload, out_own)
    output = (hidden + out_own[:, 0].astype(f32)).astype(bf16)
    grad_gate = share_expert_grad(full_gate, sent[0], core, side)
    grad_up = share_expert_grad(full_up, sent[1], core, side)
    grad_down = share_expert_grad(full_down, sent[2], core, side)
    grad_own = lax.psum_scatter(grad_payload, "expert", scatter_dimension=0, tiled=True)
    grad_own = grad_own.reshape(4, rows, 4 * cols + aux_cols)
    grad_wo = grad_own[:, :, 3 * cols : 4 * cols].transpose(1, 0, 2).reshape(rows, width)
    grad_wo = lax.ppermute(grad_wo, BOTH, [(d, b) for b, d in moves]).astype(f32)
    grad_own = jnp.concatenate([grad_own[:, :, : 3 * cols], grad_own[:, :, 4 * cols :]], axis=2)
    grad_own = lax.all_to_all(grad_own, "shard", split_axis=0, concat_axis=0, tiled=True).astype(f32)
    grad_q, grad_k, grad_v = [
        grad_own[:, :, i * cols : (i + 1) * cols].transpose(1, 0, 2).reshape(rows, width)
        for i in range(3)
    ]
    aux_sum = jnp.sum(grad_own[:, :, 3 * cols :], axis=0)
    return (
        output,
        input_grad,
        grad_q,
        grad_k,
        grad_v,
        grad_wo,
        aux_sum[:, 4 : 4 + experts],
        aux_sum[:, 0],
        aux_sum[:, 1],
        aux_sum[:, 2],
        aux_sum[:, 3],
        grad_gate,
        grad_up,
        grad_down,
    )


def solution(mesh):
    tokens_spec = P(None, BOTH, None)
    rows_spec = P(BOTH, None)
    gain_spec = P(BOTH)
    expert_spec = P("expert", "shard", None)
    return jax.shard_map(
        local,
        mesh=mesh,
        in_specs=(tokens_spec, tokens_spec, P(None, "expert", None), tokens_spec)
        + (rows_spec,) * 5
        + (gain_spec,) * 4
        + (expert_spec,) * 3,
        out_specs=(tokens_spec, tokens_spec)
        + (rows_spec,) * 5
        + (gain_spec,) * 4
        + (expert_spec,) * 3,
        check_vma=False,
    )
```

time: 2790 us -> 990 us (0.35)
  waiting for transfers between devices: 1740 us -> 417 us
  blocking collectives: 193 us -> 31.5 us
  matrix products: 369 us -> 223 us
  local copies, waits for them, and re-layouts: 232 us -> 108 us
  other arithmetic: 179 us -> 89.4 us
  Pallas kernels: 0 us -> 45.3 us
    reduce_scatter x14 -> x4, waiting for transfers between devices: 1100 us -> 35.8 us  [the longest x1 26.4 us: local(): lax.psum_scatter(jnp.stack(out_parts), 'expert', scatter_dimension=1, til...]
    ppermute x0 -> x37, waiting for transfers between devices: none -> 323 us  [the longest x12 292 us: swap_side(): return lax.ppermute(values, 'shard', [(s, s ^ 2) for s in range(4)])]
    all_to_all x8 -> x1, waiting for transfers between devices: 300 us -> 0.01 us  [local(): lax.all_to_all(grad_own, 'shard', split_axis=0, concat_axis=0, tiled=True)]
    all_gather x11 -> x6, waiting for transfers between devices: 281 us -> 57.3 us  [the longest x4 57.3 us: gather_pair(): lax.all_gather(own, 'expert', axis=0, tiled=True)]
    dot_general x64 -> x40, matrix products: 369 us -> 223 us  [the longest x27 183 us: dot(): lax.dot_general(left, right, (dims, ((), ())), preferred_element_type=f32)]
    unnamed x2 -> x0, blocking collectives: 92.1 us -> none
    all_gather x1 -> x3, blocking collectives: 101 us -> 16 us  [sum_rows(): lax.all_gather(reorder(values), 'shard', axis=0)]
    scatter-add x4 -> x0, other arithmetic: 73.9 us -> none  [gate_piece(): jnp.take_along_axis(jax.nn.softmax(logit_rows, axis=-1), route_now, axis=1)]
  transfers between devices with their start and end apart: 34 -> 48, of which waited for: 23 -> 19; matrix products, arithmetic and copies ran while one was open for 22% -> 38% of each run, Pallas kernels for 0% -> 5%
where the time goes in v1:
time: 990 us; the launch traced here: 980 us
  waiting for transfers between devices  417 us (42%)
  matrix products  223 us (23%)
  local copies, waits for them, and re-layouts  108 us (11%)
  other arithmetic  89.4 us (9%)
  starting transfers between devices  49 us (5%)
  Pallas kernels  45.3 us (5%)
  blocking collectives  31.5 us (3%)
  between operations  16.9 us (2%)
    ppermute x12, waiting for transfers between devices, swap_side(): return lax.ppermute(values, 'shard', [(s, s ^ 2) for s in range(4)])  292 us
    dot_general x27, matrix products, dot(): lax.dot_general(left, right, (dims, ((), ())), preferred_element_type=f32)  183 us
    all_gather x4, waiting for transfers between devices, gather_pair(): lax.all_gather(own, 'expert', axis=0, tiled=True)  57.3 us
    ppermute x12, starting transfers between devices, swap_side(): return lax.ppermute(values, 'shard', [(s, s ^ 2) for s in range(4)])  33.8 us
    unnamed x232, local copies, waits for them, and re-layouts  30.6 us
    pallas_call x2, Pallas kernels, attend_back(): pl.pallas_call(attend_back_body, grid=(heads,), in_specs=[pl.BlockSpec((l...  27.3 us
    reduce_scatter x1, waiting for transfers between devices, local(): lax.psum_scatter(jnp.stack(out_parts), 'expert', scatter_dimension=1, til...  26.4 us
  transfers between devices with their start and end apart: 48, of which 19 were waited for; matrix products, arithmetic and copies ran while one was open for 38% of the time, Pallas kernels for 5%

profile of v1, /device:TPU:2, one launch (start us, length us, event | category | flops | bytes accessed | tf_op | source)
XLA Modules:
  0.0 979.7 jit_solution(4329441714079668140)
XLA Ops:
  27.6 15.4 %all_to_all.10 = bf16[4,64,1664]{2,1,0:T(8,128)(2,1)} all-to-all(bf16[4,64,1664]{2,1,0:T(8,128)(2,1)S(1)} %copy.152), channel_id=1, replica_groups=mesh['expert'=8,'shard'=4] {'shard'}, dimensions={0} | all-to-all | bytes 1703936 | tf_op jit(solution)/shard_map/all_to_all | solution.py:290
  45.4 4.5 collective-permute-start.7
  49.8 7.5 collective-permute-done.7
  58.2 20.9 %collective-permute-start.2 = (bf16[2,512,1024]{2,1,0:T(8,128)(2,1)}, bf16[2,512,1024]{2,1,0:T(8,128)(2,1)}, u32[]{:S(2)}, u32[]{:S(2)}) collective-permute-start(bf16[2,512,1024]{2,1,0:T(8,128)(2,1)} %constant_dynamic-update-slice_fusion.13), channel_id=1, source_target_pairs={{0,2},{1,3},{2,0},{3,1},{4,6},{5,7},{6,4},{7,5},{8,10},{9,11},{10,... | collective-permute-start | bytes 6291464 | tf_op jit(solution)/shard_map/ppermute | solution.py:40
  86.8 55.9 %collective-permute-done.5 = bf16[2,96,2048]{2,1,0:T(8,128)(2,1)} collective-permute-done((bf16[2,96,2048]{2,1,0:T(8,128)(2,1)S(1)}, bf16[2,96,2048]{2,1,0:T(8,128)(2,1)}, u32[]{:S(2)}, u32[]{:S(2)}) %collective-permute-start.5) | collective-permute-done | bytes 786464 | tf_op jit(solution)/shard_map/ppermute | solution.py:40
  143.6 3.9 pad_maximum_fusion.5
  149.4 36.9 %collective-permute-done.3 = bf16[2,512,1024]{2,1,0:T(8,128)(2,1)} collective-permute-done((bf16[2,512,1024]{2,1,0:T(8,128)(2,1)}, bf16[2,512,1024]{2,1,0:T(8,128)(2,1)}, u32[]{:S(2)}, u32[]{:S(2)}) %collective-permute-start.3) | collective-permute-done | bytes 2097184 | tf_op jit(solution)/shard_map/ppermute | solution.py:40
  192.2 4.2 maximum_convert_fusion
  201.7 5.1 fusion.24.q_ref.k_ref.v_ref
  209.7 5.7 all_gather.28
  218.8 11.2 %shard_map.263 = (bf16[768,512]{1,0:T(8,128)(2,1)}, bf16[768,512]{1,0:T(8,128)(2,1)}, bf16[768,512]{1,0:T(8,128)(2,1)}, bf16[768,512]{1,0:T(8,128)(2,1)}, f32[8,384,1]{2,1,0:T(8,128)}) custom-call(f32[768,1536]{1,0:T(8,128)} %copy-done, f32[768,1536]{1,0:T(8,128)} %copy-done, f32[768,1536]{1,0:T(8,128)} %copy-done, f32[768,1]{1,0:T(8,128)} %copy.154.qi_ref, ...), custom_call_target="tpu_custom_call" | custom-call | tf_op jit(solution)/shard_map/pallas_call | solution.py:106
  230.0 3.6 fusion.137
  238.8 19.3 %collective-permute-done.9 = bf16[2,96,2048]{2,1,0:T(8,128)(2,1)S(1)} collective-permute-done((bf16[2,96,2048]{2,1,0:T(8,128)(2,1)S(1)}, bf16[2,96,2048]{2,1,0:T(8,128)(2,1)S(1)}, u32[]{:S(2)}, u32[]{:S(2)}) %collective-permute-start.9) | collective-permute-done | bytes 786464 | tf_op jit(solution)/shard_map/ppermute | solution.py:40
  261.7 10.6 %all-gather.16.cloned.1.call-done = bf16[1,768,2048]{2,1,0:T(8,128)(2,1)} async-done(((bf16[1,96,2048]{2,1,0:T(8,128)(2,1)}), bf16[1,768,2048]{2,1,0:T(8,128)(2,1)}) %all-gather.16.cloned.1.call-update) | async-done | bytes 3145744 | tf_op jit(solution)/shard_map/all_gather | solution.py:358
  281.4 43.8 %collective-permute-done.11 = bf16[2,256,2048]{2,1,0:T(8,128)(2,1)S(1)} collective-permute-done((bf16[2,256,2048]{2,1,0:T(8,128)(2,1)S(1)}, bf16[2,256,2048]{2,1,0:T(8,128)(2,1)S(1)}, u32[]{:S(2)}, u32[]{:S(2)}) %collective-permute-start.11) | collective-permute-done | bytes 2097184 | tf_op jit(solution)/shard_map/ppermute | solution.py:40
  326.8 6.9 all-gather.20.cloned.1.call-done
  336.4 7.1 fusion.12
  355.1 3.6 fusion.9
  358.7 7.4 fusion.138
  366.2 4.0 fusion.139
  370.2 7.3 multiply_convert_fusion.6
  377.4 8.7 fusion.1
  386.3 6.7 fusion.140
  393.0 5.7 add_convert_fusion.1
  402.4 4.0 convolution_add_fusion.1
  407.4 5.3 collective-permute-done.14
  415.5 39.7 %all-gather.14.cloned.1.call-done = bf16[768,2048]{1,0:T(8,128)(2,1)} async-done(((bf16[96,2048]{1,0:T(8,128)(2,1)}), bf16[768,2048]{1,0:T(8,128)(2,1)}) %all-gather.14.cloned.1.call-update) | async-done | bytes 3145744 | tf_op jit(solution)/shard_map/all_gather | solution.py:358
  455.7 3.8 convolution_convert_fusion.2
  475.2 4.2 convolution_convert_fusion.4
  479.4 4.1 fusion.16
  484.0 7.2 fusion.141
  491.3 4.0 fusion.142
  495.3 7.0 multiply_convert_fusion.3
  502.3 9.4 fusion.3
  512.6 8.3 fusion.143
  523.9 8.5 add_convert_fusion
  532.4 8.6 convolution_add_fusion
  545.4 5.0 add_convert_fusion.3
  556.7 12.5 %fusion.27 = f32[2048,1024]{1,0:T(8,128)} fusion(bf16[896,2048]{1,0:T(8,128)(2,1)S(1)} %bitcast.381, bf16[896,2048]{1,0:T(8,128)(2,1)S(1)} %bitcast.377, bf16[896,1024]{1,0:T(8,128)(2,1)} %get-tuple-element.156, bf16[896,1024]{1,0:T(8,128)(2,1)} %get-tuple-element.159), kind=kOutput, calls=%fused_computation.50 | convolution fusion | flops 7538212864 | bytes 19398656 | tf_op jit(solution)/shard_map/dot_general | solution.py:20
  569.3 4.9 fusion.10
  574.2 13.9 %fusion.26 = f32[2048,1024]{1,0:T(8,128)} fusion(bf16[896,2048]{1,0:T(8,128)(2,1)} %bitcast.380, bf16[896,2048]{1,0:T(8,128)(2,1)} %bitcast.374, bf16[896,1024]{1,0:T(8,128)(2,1)} %copy-done.91, bf16[896,1024]{1,0:T(8,128)(2,1)} %get-tuple-element.161), kind=kOutput, calls=%fused_computation.49 | convolution fusion | flops 7538212864 | bytes 19398656 | tf_op jit(solution)/shard_map/dot_general | solution.py:20
  592.9 13.3 %fusion.4 = f32[1024,2048]{1,0:T(8,128)} fusion(bf16[896,2048]{1,0:T(8,128)(2,1)} %copy-done.30, bf16[896,2048]{1,0:T(8,128)(2,1)} %copy-done.29, bf16[896,1024]{1,0:T(8,128)(2,1)} %copy-done.90, bf16[896,1024]{1,0:T(8,128)(2,1)} %copy-done.89), kind=kOutput, calls=%fused_computation.11 | convolution fusion | flops 7538212864 | bytes 19398656 | tf_op jit(solution)/shard_map/dot_general | solution.py:20
  606.7 4.9 add_convert_fusion.2
  612.9 13.7 %shard_map.264 = (f32[384,512]{1,0:T(8,128)}, f32[384,512]{1,0:T(8,128)}, bf16[384,512]{1,0:T(8,128)(2,1)}, f32[1,512]{1,0:T(1,128)}, f32[1,512]{1,0:T(1,128)}, /*index=5*/f32[2,8,384]{2,1,0:T(8,128)}) custom-call(bf16[384,2048]{1,0:T(8,128)(2,1)} %pad_maximum_fusion.9.dh_ref, bf16[512,2048]{1,0:T(8,128)(2,1)} %all-gather.12.cloned.1.call-done.wo_ref, ...), custom_call_target="tpu_custom_call" | custom-call | tf_op jit(solution)/shard_map/pallas_call | solution.py:165
  628.4 5.2 all_gather.34
  638.9 9.4 reduce-scatter.5.cloned.1.call-done
  648.3 6.0 pad_maximum_fusion.2
  655.1 3.7 fusion.113
  661.4 4.4 fusion.51
  666.5 3.7 collective-permute-done.24
  670.2 7.1 fusion.22
  680.6 4.5 reshape.764
  688.5 4.0 copy.180
  692.5 13.7 %shard_map.266 = (f32[384,512]{1,0:T(8,128)}, f32[384,512]{1,0:T(8,128)}, bf16[384,512]{1,0:T(8,128)(2,1)}, f32[1,512]{1,0:T(1,128)}, f32[1,512]{1,0:T(1,128)}, /*index=5*/f32[2,8,384]{2,1,0:T(8,128)}) custom-call(bf16[384,2048]{1,0:T(8,128)(2,1)} %copy-done.20, bf16[512,2048]{1,0:T(8,128)(2,1)} %all-gather.12.cloned.1.call-done.wo_ref, ...), custom_call_target="tpu_custom_call" | custom-call | tf_op jit(solution)/shard_map/pallas_call | solution.py:165
  708.0 5.2 all_gather.35
  718.7 12.9 %fusion.39 = (f32[2048]{0:T(1024)S(1)}, f32[2048]{0:T(1024)S(1)}, bf16[384,2048]{1,0:T(8,128)(2,1)}, bf16[384,2048]{1,0:T(8,128)(2,1)}, f32[384,2048]{1,0:T(8,128)}) fusion(f32[768,2048]{1,0:T(8,128)} %copy-done.18, f32[384,2048]{1,0:T(8,128)} %fusion.22, bf16[384,1536]{1,0:T(8,128)(2,1)} %shard_map.267, bf16[2048,1664]{0,1:T(8,128)(2,1)} %all-gather.10.cloned.1.call-done), kind=kOutput, calls=%fused_computation.86 | convolution fusion | flops 2420633600 | bytes 23216128 | tf_op jit(solution)/shard_map/dot_general | solution.py:20
  732.6 8.2 convolution_convert_fusion
  740.9 4.6 pad_maximum_fusion
  745.4 26.4 %reduce-scatter.9.cloned.1.call-done = bf16[2,1,96,2048]{3,2,0,1:T(8,128)(2,1)} async-done(((bf16[2,8,96,2048]{3,2,0,1:T(8,128)(2,1)}), bf16[2,1,96,2048]{3,2,0,1:T(8,128)(2,1)}) %reduce-scatter.9.cloned.1.call-update) | async-done | bytes 786448 | tf_op jit(solution)/shard_map/reduce_scatter | solution.py:454
  788.8 46.5 %collective-permute-done.27 = bf16[96,2048]{1,0:T(8,128)(2,1)S(1)} collective-permute-done((bf16[96,2048]{1,0:T(8,128)(2,1)S(1)}, bf16[96,2048]{1,0:T(8,128)(2,1)S(1)}, u32[]{:S(2)}, u32[]{:S(2)}) %collective-permute-start.27) | collective-permute-done | bytes 393248 | tf_op jit(solution)/shard_map/ppermute | solution.py:40
  835.3 8.4 collective-permute-done.29
  851.8 37.0 %collective-permute-done.31 = bf16[2,512,1024]{2,1,0:T(8,128)(2,1)} collective-permute-done((bf16[2,512,1024]{2,1,0:T(8,128)(2,1)S(1)}, bf16[2,512,1024]{2,1,0:T(8,128)(2,1)}, u32[]{:S(2)}, u32[]{:S(2)}) %collective-permute-start.31) | collective-permute-done | bytes 2097184 | tf_op jit(solution)/shard_map/ppermute | solution.py:40
  892.0 40.6 %collective-permute-done.33 = bf16[2,512,1024]{2,1,0:T(8,128)(2,1)} collective-permute-done((bf16[2,512,1024]{2,1,0:T(8,128)(2,1)S(1)}, bf16[2,512,1024]{2,1,0:T(8,128)(2,1)}, u32[]{:S(2)}, u32[]{:S(2)}) %collective-permute-start.33) | collective-permute-done | bytes 2097184 | tf_op jit(solution)/shard_map/ppermute | solution.py:40
  954.6 12.7 %collective-permute-done.30 = bf16[64,2048]{1,0:T(8,128)(2,1)S(1)} collective-permute-done((bf16[64,2048]{1,0:T(8,128)(2,1)S(1)}, bf16[64,2048]{1,0:T(8,128)(2,1)S(1)}, u32[]{:S(2)}, u32[]{:S(2)}) %collective-permute-start.30) | collective-permute-done | bytes 262176 | tf_op jit(solution)/shard_map/ppermute | solution.py:492
  (559 shorter events, 210.5 us)
Async XLA Ops:
  7.2 183.0 %all-gather.10.cloned.1.call-start = ((), (), s32[]{:S(2)}) async-start(), calls=%async_computation.6 | async-start | bytes 7667712 | tf_op jit(solution)/shard_map/all_gather | solution.py:291
  14.3 9.8 %collective-permute-start = (bf16[1,512,1024]{2,1,0:T(8,128)(2,1)}, bf16[1,512,1024]{2,1,0:T(8,128)(2,1)S(1)}, u32[]{:S(2)}, u32[]{:S(2)}) collective-permute-start(bf16[1,512,1024]{2,1,0:T(8,128)(2,1)} %constant_dynamic-slice_fusion.10), channel_id=1, source_target_pairs={{0,1},{1,0},{2,3},{3,2},{4,5},{5,4},{6,7},{7,6},{8,9},{9,8},{10,11... | collective-permute-start | bytes 3145736 | tf_op jit(solution)/shard_map/ppermute | solution.py:36
  16.6 8.6 collective-permute-start.1
  25.2 53.9 %copy-start.8 = (bf16[2,96,2048]{2,1,0:T(8,128)(2,1)S(1)}, bf16[2,96,2048]{2,1,0:T(8,128)(2,1)}, u32[]{:S(2)}) copy-start(bf16[2,96,2048]{2,1,0:T(8,128)(2,1)} %param.16) | copy-start | bytes 2359300
  27.6 55.7 %copy-start.69 = (s32[2,1,384]{2,1,0:T(1,128)S(1)}, s32[2,1,384]{2,1,0:T(1,128)}, u32[]{:S(2)}) copy-start(s32[2,1,384]{2,1,0:T(1,128)} %param.18) | copy-start | bytes 9220
  45.3 184.7 %all-gather.12.cloned.1.call-start = ((), (), s32[]{:S(2)}) async-start(), calls=%async_computation.7 | async-start | bytes 2359296 | tf_op jit(solution)/shard_map/all_gather | solution.py:294
  45.4 12.0 %collective-permute-start.7 = (bf16[64,2048]{1,0:T(8,128)(2,1)S(1)}, bf16[64,2048]{1,0:T(8,128)(2,1)S(1)}, u32[]{:S(2)}, u32[]{:S(2)}) collective-permute-start(bf16[64,2048]{1,0:T(8,128)(2,1)S(1)} %copy-done.88), channel_id=1, source_target_pairs={{0,0},{1,4},{2,8},{3,12},{4,16},{5,20},{6,24},{7,28},{8,1},{9,5},{... | collective-permute-start | bytes 786440 | tf_op jit(solution)/shard_map/ppermute | solution.py:294
  58.1 214.3 %all-gather.16.cloned.1.call-start = ((), (), s32[]{:S(2)}) async-start(), calls=%async_computation.13 | async-start | bytes 3538944 | tf_op jit(solution)/shard_map/all_gather | solution.py:358
  58.2 89.3 %collective-permute-start.2 = (bf16[2,512,1024]{2,1,0:T(8,128)(2,1)}, bf16[2,512,1024]{2,1,0:T(8,128)(2,1)}, u32[]{:S(2)}, u32[]{:S(2)}) collective-permute-start(bf16[2,512,1024]{2,1,0:T(8,128)(2,1)} %constant_dynamic-update-slice_fusion.13), channel_id=1, source_target_pairs={{0,2},{1,3},{2,0},{3,1},{4,6},{5,7},{6,4},{7,5},{8,10},{9,11},{10,... | collective-permute-start | bytes 6291464 | tf_op jit(solution)/shard_map/ppermute | solution.py:40
  79.1 109.1 %collective-permute-start.4 = (bf16[2,96,2048]{2,1,0:T(8,128)(2,1)S(1)}, bf16[2,96,2048]{2,1,0:T(8,128)(2,1)}, u32[]{:S(2)}, u32[]{:S(2)}) collective-permute-start(bf16[2,96,2048]{2,1,0:T(8,128)(2,1)S(1)} %copy-done.8), channel_id=1, source_target_pairs={{0,1},{1,0},{2,3},{3,2},{4,5},{5,4},{6,7},{7,6},{8,9},{9,8},{10,11... | collective-permute-start | bytes 2359304 | tf_op jit(solution)/shard_map/ppermute | solution.py:36
  79.1 63.6 %collective-permute-start.5 = (bf16[2,96,2048]{2,1,0:T(8,128)(2,1)S(1)}, bf16[2,96,2048]{2,1,0:T(8,128)(2,1)}, u32[]{:S(2)}, u32[]{:S(2)}) collective-permute-start(bf16[2,96,2048]{2,1,0:T(8,128)(2,1)S(1)} %copy-done.8), channel_id=1, source_target_pairs={{0,2},{1,3},{2,0},{3,1},{4,6},{5,7},{6,4},{7,5},{8,10},{9,11},{10,... | collective-permute-start | bytes 2359304 | tf_op jit(solution)/shard_map/ppermute | solution.py:40
  79.2 107.0 %collective-permute-start.3 = (bf16[2,512,1024]{2,1,0:T(8,128)(2,1)}, bf16[2,512,1024]{2,1,0:T(8,128)(2,1)}, u32[]{:S(2)}, u32[]{:S(2)}) collective-permute-start(bf16[2,512,1024]{2,1,0:T(8,128)(2,1)} %constant_dynamic-update-slice_fusion.12), channel_id=1, source_target_pairs={{0,2},{1,3},{2,0},{3,1},{4,6},{5,7},{6,4},{7,5},{8,10},{9,11},{10,... | collective-permute-start | bytes 6291464 | tf_op jit(solution)/shard_map/ppermute | solution.py:40
  83.2 250.5 %all-gather.20.cloned.1.call-start = ((), (), s32[]{:S(2)}) async-start(), calls=%async_computation.15 | async-start | bytes 3538944 | tf_op jit(solution)/shard_map/all_gather | solution.py:358
  142.7 47.4 %collective-permute-start.6 = (bf16[2,96,2048]{2,1,0:T(8,128)(2,1)}, bf16[2,96,2048]{2,1,0:T(8,128)(2,1)}, u32[]{:S(2)}, u32[]{:S(2)}) collective-permute-start(bf16[2,96,2048]{2,1,0:T(8,128)(2,1)} %collective-permute-done.5), channel_id=1, source_target_pairs={{0,1},{1,0},{2,3},{3,2},{4,5},{5,4},{6,7},{7,6},{8,9},{9,8},{10,11... | collective-permute-start | bytes 2359304 | tf_op jit(solution)/shard_map/ppermute | solution.py:36
  197.8 61.5 %copy-start.45 = (f32[1,2048]{1,0:T(1,128)}, f32[1,2048]{1,0:T(1,128)S(1)}, u32[]{:S(2)}) copy-start(f32[1,2048]{1,0:T(1,128)S(1)} %get-tuple-element.177) | copy-start | bytes 24580
  234.1 3.6 collective-permute-start.8
  238.2 19.9 %collective-permute-start.9 = (bf16[2,96,2048]{2,1,0:T(8,128)(2,1)S(1)}, bf16[2,96,2048]{2,1,0:T(8,128)(2,1)S(1)}, u32[]{:S(2)}, u32[]{:S(2)}) collective-permute-start(bf16[2,96,2048]{2,1,0:T(8,128)(2,1)S(1)} %fusion.53), channel_id=1, source_target_pairs={{0,2},{1,3},{2,0},{3,1},{4,6},{5,7},{6,4},{7,5},{8,10},{9,11},{10,... | collective-permute-start | bytes 2359304 | tf_op jit(solution)/shard_map/ppermute | solution.py:40
  273.4 142.1 %all-gather.18.cloned.1.call-start = ((), (), s32[]{:S(2)}) async-start(), calls=%async_computation.14 | async-start | bytes 3538944 | tf_op jit(solution)/shard_map/all_gather | solution.py:358
  274.5 2.9 collective-permute-start.10
  274.5 180.7 %all-gather.14.cloned.1.call-start = ((), (), s32[]{:S(2)}) async-start(), calls=%async_computation.8 | async-start | bytes 3538944 | tf_op jit(solution)/shard_map/all_gather | solution.py:358
  277.5 47.7 %collective-permute-start.11 = (bf16[2,256,2048]{2,1,0:T(8,128)(2,1)S(1)}, bf16[2,256,2048]{2,1,0:T(8,128)(2,1)S(1)}, u32[]{:S(2)}, u32[]{:S(2)}) collective-permute-start(bf16[2,256,2048]{2,1,0:T(8,128)(2,1)S(1)} %constant_dynamic-update-slice_fusion.9), channel_id=1, source_target_pairs={{0,2},{1,3},{2,0},{3,1},{4,6},{5,7},{6,4},{7,5},{8,10},{9,11},{10,... | collective-permute-start | bytes 6291464 | tf_op jit(solution)/shard_map/ppermute | solution.py:40
  279.0 57.4 %collective-permute-start.13 = (bf16[8,96,2048]{2,1,0:T(8,128)(2,1)}, bf16[8,96,2048]{2,1,0:T(8,128)(2,1)}, u32[]{:S(2)}, u32[]{:S(2)}) collective-permute-start(bf16[8,96,2048]{2,1,0:T(8,128)(2,1)} %bitcast.421), channel_id=1, source_target_pairs={{0,1},{1,0},{2,3},{3,2},{4,5},{5,4},{6,7},{7,6},{8,9},{9,8},{10,11... | collective-permute-start | bytes 9437192 | tf_op jit(solution)/shard_map/ppermute | solution.py:36
  333.7 12.1 %collective-permute-start.12 = (bf16[8,96,2048]{2,1,0:T(8,128)(2,1)}, bf16[8,96,2048]{2,1,0:T(8,128)(2,1)}, u32[]{:S(2)}, u32[]{:S(2)}) collective-permute-start(bf16[8,96,2048]{2,1,0:T(8,128)(2,1)} %bitcast.419), channel_id=1, source_target_pairs={{0,1},{1,0},{2,3},{3,2},{4,5},{5,4},{6,7},{7,6},{8,9},{9,8},{10,11... | collective-permute-start | bytes 9437192 | tf_op jit(solution)/shard_map/ppermute | solution.py:36
  333.7 187.2 %copy-start.64 = (f32[16]{0:T(128)}, f32[16]{0:T(128)S(1)}, u32[]{:S(2)}) copy-start(f32[16]{0:T(128)S(1)} %compare_convert_fusion) | copy-start | bytes 196
  343.5 244.6 %reduce-scatter.7.cloned.1.call-start = ((), (), s32[]{:S(2)}) async-start(), calls=%async_computation.10 | async-start | bytes 3538944 | tf_op jit(solution)/shard_map/reduce_scatter | solution.py:417
  354.3 45.2 %copy-start.35 = (f32[1536,16]{0,1:T(8,128)}, f32[1536,16]{0,1:T(8,128)S(1)}, u32[]{:S(2)}) copy-start(f32[1536,16]{0,1:T(8,128)S(1)} %get-tuple-element.242) | copy-start | bytes 294916
  354.3 45.2 %copy-start.50 = (f32[1536]{0:T(1024)}, f32[1536]{0:T(1024)S(1)}, u32[]{:S(2)}) copy-start(f32[1536]{0:T(1024)S(1)} %get-tuple-element.241) | copy-start | bytes 18436
  354.4 45.2 %copy-start.54 = (f32[1536]{0:T(1024)}, f32[1536]{0:T(1024)S(1)}, u32[]{:S(2)}) copy-start(f32[1536]{0:T(1024)S(1)} %fusion.90) | copy-start | bytes 18436
  406.9 5.8 collective-permute-start.14
  455.2 11.6 %collective-permute-start.15 = (bf16[8,96,2048]{2,1,0:T(8,128)(2,1)}, bf16[8,96,2048]{2,1,0:T(8,128)(2,1)}, u32[]{:S(2)}, u32[]{:S(2)}) collective-permute-start(bf16[8,96,2048]{2,1,0:T(8,128)(2,1)} %bitcast.417), channel_id=1, source_target_pairs={{0,1},{1,0},{2,3},{3,2},{4,5},{5,4},{6,7},{7,6},{8,9},{9,8},{10,11... | collective-permute-start | bytes 9437192 | tf_op jit(solution)/shard_map/ppermute | solution.py:36
  455.2 24.2 %collective-permute-start.16 = (bf16[8,96,2048]{2,1,0:T(8,128)(2,1)}, bf16[8,96,2048]{2,1,0:T(8,128)(2,1)}, u32[]{:S(2)}, u32[]{:S(2)}) collective-permute-start(bf16[8,96,2048]{2,1,0:T(8,128)(2,1)} %bitcast.423), channel_id=1, source_target_pairs={{0,1},{1,0},{2,3},{3,2},{4,5},{5,4},{6,7},{7,6},{8,9},{9,8},{10,11... | collective-permute-start | bytes 9437192 | tf_op jit(solution)/shard_map/ppermute | solution.py:36
  464.0 81.3 %collective-permute-start.21 = (bf16[8,96,2048]{2,1,0:T(8,128)(2,1)}, bf16[8,96,2048]{2,1,0:T(8,128)(2,1)}, u32[]{:S(2)}, u32[]{:S(2)}) collective-permute-start(bf16[8,96,2048]{2,1,0:T(8,128)(2,1)} %slice.468), channel_id=1, source_target_pairs={{0,1},{1,0},{2,3},{3,2},{4,5},{5,4},{6,7},{7,6},{8,9},{9,8},{10,11... | collective-permute-start | bytes 9437192 | tf_op jit(solution)/shard_map/ppermute | solution.py:36
  464.1 184.3 %reduce-scatter.5.cloned.1.call-start = ((), (), s32[]{:S(2)}) async-start(), calls=%async_computation.9 | async-start | bytes 3538944 | tf_op jit(solution)/shard_map/reduce_scatter | solution.py:417
  474.5 46.4 %copy-start.56 = (f32[1536]{0:T(1024)}, f32[1536]{0:T(1024)S(1)}, u32[]{:S(2)}) copy-start(f32[1536]{0:T(1024)S(1)} %fusion.92) | copy-start | bytes 18436
  544.3 25.0 %collective-permute-start.17 = (bf16[8,96,2048]{2,1,0:T(8,128)(2,1)S(1)}, bf16[8,96,2048]{2,1,0:T(8,128)(2,1)}, u32[]{:S(2)}, u32[]{:S(2)}) collective-permute-start(bf16[8,96,2048]{2,1,0:T(8,128)(2,1)S(1)} %slice.705), channel_id=1, source_target_pairs={{0,1},{1,0},{2,3},{3,2},{4,5},{5,4},{6,7},{7,6},{8,9},{9,8},{10,11... | collective-permute-start | bytes 9437192 | tf_op jit(solution)/shard_map/ppermute | solution.py:36
  545.4 44.6 %copy-start.72 = (f32[96]{0:T(128)}, f32[96]{0:T(128)S(1)}, u32[]{:S(2)}) copy-start(f32[96]{0:T(128)S(1)} %get-tuple-element.240) | copy-start | bytes 1156
  556.7 50.0 %collective-permute-start.22 = (bf16[8,96,2048]{2,1,0:T(8,128)(2,1)}, bf16[8,96,2048]{2,1,0:T(8,128)(2,1)}, u32[]{:S(2)}, u32[]{:S(2)}) collective-permute-start(bf16[8,96,2048]{2,1,0:T(8,128)(2,1)} %slice.470), channel_id=1, source_target_pairs={{0,1},{1,0},{2,3},{3,2},{4,5},{5,4},{6,7},{7,6},{8,9},{9,8},{10,11... | collective-permute-start | bytes 9437192 | tf_op jit(solution)/shard_map/ppermute | solution.py:36
  574.2 197.6 %reduce-scatter.9.cloned.1.call-start = ((), (), s32[]{:S(2)}) async-start(), calls=%async_computation.11 | async-start | bytes 7077888 | tf_op jit(solution)/shard_map/reduce_scatter | solution.py:454
  591.4 15.3 %collective-permute-start.19 = (bf16[96,2048]{1,0:T(8,128)(2,1)S(1)}, bf16[96,2048]{1,0:T(8,128)(2,1)S(1)}, u32[]{:S(2)}, u32[]{:S(2)}) collective-permute-start(bf16[96,2048]{1,0:T(8,128)(2,1)S(1)} %fusion.119), channel_id=1, source_target_pairs={{0,2},{1,3},{2,0},{3,1},{4,6},{5,7},{6,4},{7,5},{8,10},{9,11},{10,... | collective-permute-start | bytes 1179656 | tf_op jit(solution)/shard_map/ppermute | solution.py:40
  606.2 5.4 collective-permute-start.18
  606.6 5.0 collective-permute-start.20
  654.5 289.0 %reduce-scatter.11.cloned.1.call-start = ((), (), s32[]{:S(2)}) async-start(), calls=%async_computation.12 | async-start | bytes 10027008 | tf_op jit(solution)/shard_map/reduce_scatter | solution.py:489
  659.9 10.3 %collective-permute-start.24 = (bf16[96,2048]{1,0:T(8,128)(2,1)S(1)}, bf16[96,2048]{1,0:T(8,128)(2,1)S(1)}, u32[]{:S(2)}, u32[]{:S(2)}) collective-permute-start(bf16[96,2048]{1,0:T(8,128)(2,1)S(1)} %fusion.118), channel_id=1, source_target_pairs={{0,2},{1,3},{2,0},{3,1},{4,6},{5,7},{6,4},{7,5},{8,10},{9,11},{10,... | collective-permute-start | bytes 1179656 | tf_op jit(solution)/shard_map/ppermute | solution.py:40
  665.9 11.4 %collective-permute-start.23 = (bf16[96,2048]{1,0:T(8,128)(2,1)S(1)}, bf16[96,2048]{1,0:T(8,128)(2,1)S(1)}, u32[]{:S(2)}, u32[]{:S(2)}) collective-permute-start(bf16[96,2048]{1,0:T(8,128)(2,1)S(1)} %fusion.118), channel_id=1, source_target_pairs={{0,1},{1,0},{2,3},{3,2},{4,5},{5,4},{6,7},{7,6},{8,9},{9,8},{10,11... | collective-permute-start | bytes 1179656 | tf_op jit(solution)/shard_map/ppermute | solution.py:36
  670.1 7.1 collective-permute-start.25
  774.5 5.3 collective-permute-start.26
  774.9 5.8 collective-permute-start.28
  778.3 68.8 %collective-permute-start.35 = (bf16[2,256,2048]{2,1,0:T(8,128)(2,1)S(1)}, bf16[2,256,2048]{2,1,0:T(8,128)(2,1)S(1)}, u32[]{:S(2)}, u32[]{:S(2)}) collective-permute-start(bf16[2,256,2048]{2,1,0:T(8,128)(2,1)S(1)} %dynamic-slice_convert_fusion), channel_id=1, source_target_pairs={{0,2},{1,3},{2,0},{3,1},{4,6},{5,7},{6,4},{7,5},{8,10},{9,11},{10,... | collective-permute-start | bytes 6291464 | tf_op jit(solution)/shard_map/ppermute | solution.py:40
  780.1 55.2 %collective-permute-start.27 = (bf16[96,2048]{1,0:T(8,128)(2,1)S(1)}, bf16[96,2048]{1,0:T(8,128)(2,1)S(1)}, u32[]{:S(2)}, u32[]{:S(2)}) collective-permute-start(bf16[96,2048]{1,0:T(8,128)(2,1)S(1)} %fusion.81), channel_id=1, source_target_pairs={{0,2},{1,3},{2,0},{3,1},{4,6},{5,7},{6,4},{7,5},{8,10},{9,11},{10,... | collective-permute-start | bytes 1179656 | tf_op jit(solution)/shard_map/ppermute | solution.py:40
  782.2 61.5 %collective-permute-start.29 = (bf16[96,2048]{1,0:T(8,128)(2,1)S(1)}, bf16[96,2048]{1,0:T(8,128)(2,1)S(1)}, u32[]{:S(2)}, u32[]{:S(2)}) collective-permute-start(bf16[96,2048]{1,0:T(8,128)(2,1)S(1)} %fusion.75), channel_id=1, source_target_pairs={{0,2},{1,3},{2,0},{3,1},{4,6},{5,7},{6,4},{7,5},{8,10},{9,11},{10,... | collective-permute-start | bytes 1179656 | tf_op jit(solution)/shard_map/ppermute | solution.py:40
  783.8 63.3 %slice-start.13 = ((s8[8388608]{0:T(1024)(128)(4,1)}), s8[4194304]{0:T(1024)(128)(4,1)S(1)}, s32[]{:S(2)}) async-start(s8[8388608]{0:T(1024)(128)(4,1)} %bitcast.395), calls=%async_computation.29 | async-start | bytes 8388608
  784.1 104.7 %collective-permute-start.31 = (bf16[2,512,1024]{2,1,0:T(8,128)(2,1)S(1)}, bf16[2,512,1024]{2,1,0:T(8,128)(2,1)}, u32[]{:S(2)}, u32[]{:S(2)}) collective-permute-start(bf16[2,512,1024]{2,1,0:T(8,128)(2,1)S(1)} %dynamic-slice_convert_fusion.2), channel_id=1, source_target_pairs={{0,2},{1,3},{2,0},{3,1},{4,6},{5,7},{6,4},{7,5},{8,10},{9,11},{10,... | collective-permute-start | bytes 6291464 | tf_op jit(solution)/shard_map/ppermute | solution.py:40
  787.5 58.2 %copy-start.15 = (bf16[2,96,2048]{2,1,0:T(8,128)(2,1)S(1)}, bf16[2,96,2048]{2,1,0:T(8,128)(2,1)}, u32[]{:S(2)}) copy-start(bf16[2,96,2048]{2,1,0:T(8,128)(2,1)} %param.17) | copy-start | bytes 2359300
  787.6 58.2 %copy-start.32 = (bf16[1,96,2048]{2,1,0:T(8,128)(2,1)S(1)}, bf16[1,96,2048]{2,1,0:T(8,128)(2,1)}, u32[]{:S(2)}) copy-start(bf16[1,96,2048]{2,1,0:T(8,128)(2,1)} %reduce-scatter.7.cloned.1.call-done) | copy-start | bytes 1179652
  787.6 58.2 %copy-start.73 = (f32[96]{0:T(128)S(1)}, f32[96]{0:T(128)}, u32[]{:S(2)}) copy-start(f32[96]{0:T(128)} %copy-done.72) | copy-start | bytes 1156
  787.6 58.2 %copy-start.77 = (f32[96]{0:T(128)S(1)}, f32[96]{0:T(128)}, u32[]{:S(2)}) copy-start(f32[96]{0:T(128)} %copy-done.76) | copy-start | bytes 1156
  787.6 145.0 %collective-permute-start.33 = (bf16[2,512,1024]{2,1,0:T(8,128)(2,1)S(1)}, bf16[2,512,1024]{2,1,0:T(8,128)(2,1)}, u32[]{:S(2)}, u32[]{:S(2)}) collective-permute-start(bf16[2,512,1024]{2,1,0:T(8,128)(2,1)S(1)} %dynamic-slice_convert_fusion.1), channel_id=1, source_target_pairs={{0,2},{1,3},{2,0},{3,1},{4,6},{5,7},{6,4},{7,5},{8,10},{9,11},{10,... | collective-permute-start | bytes 6291464 | tf_op jit(solution)/shard_map/ppermute | solution.py:40
  847.1 85.5 %slice-start.11 = ((s8[8388608]{0:T(1024)(128)(4,1)}), s8[4194304]{0:T(1024)(128)(4,1)S(1)}, s32[]{:S(2)}) async-start(s8[8388608]{0:T(1024)(128)(4,1)} %bitcast.391), calls=%async_computation.27 | async-start | bytes 8388608
  851.7 81.0 %slice-start.12 = ((s8[8388608]{0:T(1024)(128)(4,1)}), s8[4194304]{0:T(1024)(128)(4,1)S(1)}, s32[]{:S(2)}) async-start(s8[8388608]{0:T(1024)(128)(4,1)} %bitcast.391), calls=%async_computation.28 | async-start | bytes 8388608
  851.7 87.1 %collective-permute-start.36 = (bf16[1,256,2048]{2,1,0:T(8,128)(2,1)S(1)}, bf16[1,256,2048]{2,1,0:T(8,128)(2,1)S(1)}, u32[]{:S(2)}, u32[]{:S(2)}) collective-permute-start(bf16[1,256,2048]{2,1,0:T(8,128)(2,1)S(1)} %dynamic-slice_convert_fusion.3), channel_id=1, source_target_pairs={{0,1},{1,0},{2,3},{3,2},{4,5},{5,4},{6,7},{7,6},{8,9},{9,8},{10,11... | collective-permute-start | bytes 3145736 | tf_op jit(solution)/shard_map/ppermute | solution.py:36
  891.9 46.3 %collective-permute-start.32 = (bf16[1,512,1024]{2,1,0:T(8,128)(2,1)S(1)}, bf16[1,512,1024]{2,1,0:T(8,128)(2,1)S(1)}, u32[]{:S(2)}, u32[]{:S(2)}) collective-permute-start(bf16[1,512,1024]{2,1,0:T(8,128)(2,1)S(1)} %dynamic-slice_convert_fusion.5), channel_id=1, source_target_pairs={{0,1},{1,0},{2,3},{3,2},{4,5},{5,4},{6,7},{7,6},{8,9},{9,8},{10,11... | collective-permute-start | bytes 3145736 | tf_op jit(solution)/shard_map/ppermute | solution.py:36
  935.5 3.0 collective-permute-start.34
  946.3 21.8 %all-to-all-start.1 = ((bf16[4,64,1664]{2,1,0:T(8,128)(2,1)}), bf16[4,64,1664]{2,1,0:T(8,128)(2,1)S(1)}, u32[]{:S(2)}, u32[]{:S(2)}) async-start(bf16[4,64,1664]{2,1,0:T(8,128)(2,1)} %pad_maximum_fusion.11), calls=%async_computation.5 | async-start | bytes 1703936 | tf_op jit(solution)/shard_map/all_to_all | solution.py:494
  949.9 17.4 %collective-permute-start.30 = (bf16[64,2048]{1,0:T(8,128)(2,1)S(1)}, bf16[64,2048]{1,0:T(8,128)(2,1)S(1)}, u32[]{:S(2)}, u32[]{:S(2)}) collective-permute-start(bf16[64,2048]{1,0:T(8,128)(2,1)S(1)} %bitcast.435), channel_id=1, source_target_pairs={{0,0},{4,1},{8,2},{12,3},{16,4},{20,5},{24,6},{28,7},{1,8},{5,9},{... | collective-permute-start | bytes 786440 | tf_op jit(solution)/shard_map/ppermute | solution.py:492
  (94 other events, 837.9 us)
Sparse Core Ops, SparseCore 0:
  45.4 117.0 all-gather.9
  164.6 46.3 all-gather.11
  213.8 58.5 all-gather.15
  275.0 58.6 all-gather.19
  335.7 58.6 all-gather.17
  396.5 58.6 all-gather.13
  464.2 74.3 reduce-scatter.6
  574.3 74.0 reduce-scatter.4
  654.5 117.2 reduce-scatter.8
  775.3 154.4 reduce-scatter.10

commit v2 on v1

--- a/solution.py
+++ b/solution.py
@@ -54,6 +54,16 @@
 
 def tie(*values):
     return lax.optimization_barrier(values)
+
+
+def low_groups():
+    count = lax.axis_size("expert")
+    return [[2 * h + low for h in range(count // 2)] for low in range(2)]
+
+
+def swap_low(values):
+    count = lax.axis_size("expert")
+    return lax.ppermute(values, "expert", [(e, e ^ 1) for e in range(count)])
 
 
 def sum_rows(values, core, side, tok):
@@ -112,8 +122,13 @@
     )(linear, linear, linear, q_inv, k_inv, gain_q, gain_k, cos, sin, ids.reshape(total, 1), ids[:, None, :])
 
 
+def exact(left, right, at):
+    dims = (((1,), (at,)), ((), ()))
+    return lax.dot_general(left, right, dims, precision=lax.Precision.HIGHEST, preferred_element_type=f32)
+
+
 def attend_back_body(dh_ref, wo_ref, q_ref, k_ref, qr_ref, kr_ref, vr_ref, lse_ref, qi_ref, ki_ref, gq_ref, gk_ref,
-                     cos_ref, sin_ref, idq_ref, idk_ref, wq_ref, wk_ref, dv_ref, pq_ref, pk_ref, sum_ref):
+                     cos_ref, sin_ref, idq_ref, idk_ref, order_ref, wq_ref, wk_ref, dv_ref, pq_ref, pk_ref, sum_ref):
     cos = cos_ref[...]
     sin = sin_ref[...]
     half = HEAD_DIM // 2
@@ -136,23 +151,23 @@
         part_ref[...] = jnp.sum(grad * normed, axis=0, keepdims=True)
         grad = grad * gain
         out_ref[...] = grad
-        rows = lax.dot_general(
-            ones, grad * normed, (((1,), (1,)), ((), ())), precision=lax.Precision.HIGHEST, preferred_element_type=f32
-        )
+        rows = exact(ones, grad * normed, 1)
+
+        rows = exact(rows, order_ref[...], 0)[:1]
 
         @pl.when(pl.program_id(0) == 0)
         def _():
-            sum_ref[at] = rows
+            sum_ref[at : at + 1] = rows
 
         @pl.when(pl.program_id(0) > 0)
         def _():
-            sum_ref[at] = sum_ref[at] + rows
+            sum_ref[at : at + 1] = sum_ref[at : at + 1] + rows
 
     finish(nn(d_s, k_r), q_ref[...], qi_ref[...], gq_ref[...], wq_ref, pq_ref, 0)
     finish(tn(d_s, q_r), k_ref[...], ki_ref[...], gk_ref[...], wk_ref, pk_ref, 1)
 
 
-def attend_back(m, dh, w_o, linear, q_r, k_r, v_r, lse, q_inv, k_inv, gain_q, gain_k, cos, sin, ids, heads):
+def attend_back(m, dh, w_o, linear, q_r, k_r, v_r, lse, q_inv, k_inv, gain_q, gain_k, cos, sin, ids, order, heads):
     micro, length = ids.shape
     cols = heads * HEAD_DIM
     width = dh.shape[1]
@@ -171,44 +186,151 @@
             head(0), head(heads), head(0), head(0), head(0),
             pl.BlockSpec((1, length, 1), lambda h: (m * heads + h, 0, 0)),
             column, column, gain, gain, angle, angle, column, keys,
+            pl.BlockSpec((length, length), lambda h: (0, 0)),
         ],
-        out_specs=[out, out, out, gain, gain, pl.BlockSpec((2, 8, length), lambda h: (0, 0, 0))],
+        out_specs=[out, out, out, gain, gain, pl.BlockSpec((2, length), lambda h: (0, 0))],
         out_shape=[
             jax.ShapeDtypeStruct((length, cols), f32),
             jax.ShapeDtypeStruct((length, cols), f32),
             jax.ShapeDtypeStruct((length, cols), bf16),
             jax.ShapeDtypeStruct((1, cols), f32),
             jax.ShapeDtypeStruct((1, cols), f32),
-            jax.ShapeDtypeStruct((2, 8, length), f32),
+            jax.ShapeDtypeStruct((2, length), f32),
         ],
     )(dh, w_o, linear, linear, q_r, k_r, v_r, lse, q_inv, k_inv, gain_q, gain_k, cos, sin,
-      ids.reshape(micro * length, 1), ids[:, None, :])
-
-
-def project_back_body(wq_ref, wk_ref, dv_ref, q_ref, k_ref, qi_ref, ki_ref, sq_ref, sk_ref, out_ref):
+      ids.reshape(micro * length, 1), ids[:, None, :], order)
+
+
+def project_back_body(wq_ref, wk_ref, dv_ref, q_ref, k_ref, qi_ref, ki_ref, sum_ref, order_ref, out_ref):
     cols = wq_ref.shape[1]
     q_inv = qi_ref[...]
     k_inv = ki_ref[...]
-    out_ref[:, :cols] = (q_inv * (wq_ref[...] - q_ref[...] * (q_inv * sq_ref[...]))).astype(bf16)
-    out_ref[:, cols : 2 * cols] = (k_inv * (wk_ref[...] - k_ref[...] * (k_inv * sk_ref[...]))).astype(bf16)
+    total = sum_ref[0] + sum_ref[1] + sum_ref[2] + sum_ref[3]
+    total = exact(order_ref[...], total, 1) * (1.0 / (4 * cols))
+    out_ref[:, :cols] = (q_inv * (wq_ref[...] - q_ref[...] * (q_inv * total[:, :1]))).astype(bf16)
+    out_ref[:, cols : 2 * cols] = (k_inv * (wk_ref[...] - k_ref[...] * (k_inv * total[:, 1:]))).astype(bf16)
     out_ref[:, 2 * cols :] = dv_ref[...]
 
 
-def project_back(m, w_q, w_k, d_v, linear, q_inv, k_inv, s_q, s_k):
+def project_back(m, w_q, w_k, d_v, linear, q_inv, k_inv, sums, order):
     length, cols = w_q.shape
     rows = length // 2
     full = pl.BlockSpec((rows, cols), lambda i: (i, 0))
     column = pl.BlockSpec((rows, 1), lambda i: (2 * m + i, 0))
-    own = pl.BlockSpec((rows, 1), lambda i: (i, 0))
     return pl.pallas_call(
         project_back_body,
         grid=(2,),
         in_specs=[full, full, full]
         + [pl.BlockSpec((rows, cols), lambda i, b=b: (2 * m + i, b)) for b in range(2)]
-        + [column, column, own, own],
+        + [column, column, pl.BlockSpec(sums.shape, lambda i: (0, 0, 0)), pl.BlockSpec((rows, length), lambda i: (i, 0))],
         out_specs=pl.BlockSpec((rows, 3 * cols), lambda i: (i, 0)),
         out_shape=jax.ShapeDtypeStruct((length, 3 * cols), bf16),
-    )(w_q, w_k, d_v, linear, linear, q_inv, k_inv, s_q, s_k)
+    )(w_q, w_k, d_v, linear, linear, q_inv, k_inv, sums, order)
+
+
+def expert_body(slot_ref, bo_ref, bn_ref, do_ref, dn_ref, wg_ref, wu_ref, wd_ref, router_ref, mine_ref,
+                x_ref, act_ref, dy_ref, dgl_ref, dul_ref, oo_ref, on_ref, go_ref, gn_ref, part_ref):
+    group = slot_ref.shape[0]
+    pack = x_ref.shape[1]
+    tok, width = bo_ref.shape[-2:]
+    router = router_ref[...]
+    mine = mine_ref[...]
+    picks, gates, xs, dos, pis, bs = [], [], [], [], [], []
+    for g in range(group):
+        both = lambda own, near: jnp.concatenate([own[g].reshape(tok, width), near[g].reshape(tok, width)], axis=0)
+        b = both(bo_ref, bn_ref)
+        logits = nt(router, b)
+        weight = jnp.exp(logits - jnp.max(logits, axis=0, keepdims=True))
+        pi = weight / jnp.sum(weight, axis=0, keepdims=True)
+        slots = lax.broadcasted_iota(jnp.int32, (pack, 2 * tok), 0)
+        pick = jnp.where(slots == slot_ref[g], 1.0, 0.0)
+        gate = jnp.sum(pi * mine, axis=0, keepdims=True)
+        gates.append((gate, jnp.sum(pick * gate, axis=1, keepdims=True)))
+        low = pick.astype(bf16)
+        picks.append((pick, low))
+        xs.append(nn(low, b).astype(bf16))
+        dos.append(nn(low, both(do_ref, dn_ref)))
+        pis.append(pi)
+        bs.append(b)
+    x = jnp.concatenate(xs, axis=0)
+    gate_p = jnp.concatenate([g[1] for g in gates], axis=0)
+    gl = nn(x, wg_ref[...])
+    ul = nn(x, wu_ref[...])
+    sg = 1.0 / (1.0 + jnp.exp(-gl))
+    silu = gl * sg
+    act = (silu * ul).astype(bf16)
+    do_p = jnp.concatenate(dos, axis=0)
+    dy = (gate_p * do_p).astype(bf16)
+    y = nn(act, wd_ref[...]).astype(bf16).astype(f32)
+    dgate_p = jnp.sum(y * do_p, axis=1, keepdims=True)
+    weighted = (gate_p * y).astype(bf16)
+    dact = nt(dy, wd_ref[...])
+    dgl = (dact * ul * sg * (1.0 + gl * (1.0 - sg))).astype(bf16)
+    dul = (dact * silu).astype(bf16)
+    drow = (nt(dgl, wg_ref[...]) + nt(dul, wu_ref[...])).astype(bf16)
+    total = None
+    for g in range(group):
+        rows = slice(g * pack, (g + 1) * pack)
+        pick, low = picks[g]
+        x_ref[g] = x[rows]
+        act_ref[g] = act[rows]
+        dy_ref[g] = dy[rows]
+        dgl_ref[g] = dgl[rows]
+        dul_ref[g] = dul[rows]
+        out = tn(low, weighted[rows]).astype(bf16)
+        oo_ref[g] = out[:tok]
+        on_ref[g] = out[tok:]
+        dgate = jnp.sum(pick * dgate_p[rows], axis=0, keepdims=True)
+        dz = (dgate * gates[g][0] * (mine - pis[g])).astype(bf16)
+        grad = (tn(low, drow[rows]) + tn(dz, router)).astype(bf16)
+        go_ref[g] = grad[:tok]
+        gn_ref[g] = grad[tok:]
+        part = nn(dz, bs[g])
+        total = part if total is None else total + part
+
+    @pl.when(pl.program_id(0) == 0)
+    def _():
+        part_ref[...] = total
+
+    @pl.when(pl.program_id(0) > 0)
+    def _():
+        part_ref[...] = part_ref[...] + total
+
+
+def expert_step(slot, b_own, b_near, do_own, do_near, gate_w, up_w, down_w, router_t, mine, pack):
+    group = 2
+    owners = slot.shape[0]
+    width, hidden = gate_w.shape
+    tok = slot.shape[2] // 2
+    experts = router_t.shape[0]
+
+    def rows_spec(value):
+        if isinstance(value, tuple):
+            at = value[1]
+            return pl.BlockSpec((group, 1, tok, width), lambda i: (i, at, 0, 0))
+        return pl.BlockSpec((group, tok, width), lambda i: (i, 0, 0))
+
+    def fixed(shape):
+        return pl.BlockSpec(shape, lambda i: (0, 0), pipeline_mode=pl.Buffered(1))
+
+    def packed(cols):
+        return pl.BlockSpec((group, pack, cols), lambda i: (i, 0, 0))
+
+    token = pl.BlockSpec((group, tok, width), lambda i: (i, 0, 0))
+    values = (b_own, b_near, do_own, do_near)
+    widths = (width, hidden, width, hidden, hidden)
+    return pl.pallas_call(
+        expert_body,
+        grid=(owners // group,),
+        in_specs=[pl.BlockSpec((group, 1, 2 * tok), lambda i: (i, 0, 0))]
+        + [rows_spec(v) for v in values]
+        + [fixed(gate_w.shape), fixed(up_w.shape), fixed(down_w.shape), fixed(router_t.shape), fixed(mine.shape)],
+        out_specs=[packed(c) for c in widths] + [token] * 4 + [pl.BlockSpec((experts, width), lambda i: (0, 0))],
+        out_shape=[jax.ShapeDtypeStruct((owners, pack, c), bf16) for c in widths]
+        + [jax.ShapeDtypeStruct((owners, tok, width), bf16)] * 4
+        + [jax.ShapeDtypeStruct((experts, width), f32)],
+        compiler_params=pltpu.CompilerParams(vmem_limit_bytes=60 * 1024 * 1024),
+    )(slot, *[v[0] if isinstance(v, tuple) else v for v in values], gate_w, up_w, down_w, router_t, mine)
 
 
 def half_expert(weight, core):
@@ -284,27 +406,41 @@
     blocks = [w.reshape(rows, 4, cols) for w in (w_query, w_key, w_value)]
     blocks.append(jnp.broadcast_to(aux[:, None, :], (rows, 4, aux_cols)))
     payload = jnp.concatenate(blocks, axis=2).transpose(1, 0, 2)
-    half_gate = half_expert(w_gate, core)
-    half_up = half_expert(w_up, core)
-    payload, half_gate, half_up = tie(payload, half_gate, half_up)
     payload = lax.all_to_all(payload, "shard", split_axis=0, concat_axis=0, tiled=True)
+    do_got = lax.all_gather(cotangent[0], "expert", axis=0, axis_index_groups=low_groups())
+    payload, do_got = tie(payload, do_got)
     front = lax.all_gather(payload.reshape(4 * rows, 3 * cols + aux_cols), "expert", axis=0, tiled=True)
+
+    gate_w = whole_expert(half_expert(w_gate, core), side)
+    down_w = whole_expert(half_expert(w_down, core), side)
+    chunks = gather_shard(tokens)
     devices = 4 * owners
     moves = [(b, (b % owners) * 4 + b // owners) for b in range(devices)]
-    w_o = lax.all_gather(lax.ppermute(w_out, BOTH, moves), "expert", axis=0, tiled=True)
-
-    gate_w = whole_expert(half_gate, side)
-    up_w = whole_expert(half_up, side)
-    down_w = whole_expert(half_expert(w_down, core), side)
-    chunks = gather_shard(tokens)
-    front, gate_w, up_w, *chunks = tie(front, gate_w, up_w, *chunks)
+    w_o_block = lax.ppermute(w_out, BOTH, moves)
+    x_all = jnp.concatenate(chunks, axis=1).reshape(micro * length, width)
+    x_scale = inverse_rms(x_all.astype(f32))
+    chunk_ids = [jnp.bitwise_xor(s_index, j) for j in range(4)]
+    positions = jnp.concatenate([c * tok + jnp.arange(tok, dtype=jnp.int32) for c in chunk_ids])
+    order = (positions[:, None] == jnp.arange(length)[None, :]).astype(f32)
+    rate = ROPE_BASE ** (-2.0 * jnp.arange(HEAD_DIM // 2, dtype=f32) / HEAD_DIM)
+    angles = positions.astype(f32)[:, None] * rate[None, :]
+    cosine = jnp.cos(angles)
+    sine = jnp.sin(angles)
+    cosine = jnp.concatenate([cosine, cosine], axis=1)
+    sine = jnp.concatenate([-sine, sine], axis=1)
+    up_w = whole_expert(half_expert(w_up, core), side)
+    front, gate_w, up_w, w_o_block, x_all, x_scale, cosine, sine = tie(
+        front, gate_w, up_w, w_o_block, x_all, x_scale, cosine, sine
+    )
+    do_got, _ = tie(do_got, front)
+    do_other = swap_low(do_got)
+    w_o = lax.all_gather(w_o_block, "expert", axis=0, tiled=True)
     w_qkv = front[:, : 3 * cols]
     aux_rows = front[:, 3 * cols :].T.astype(f32)
     gain_attention = aux_rows[0]
     gain_query = lax.dynamic_slice_in_dim(aux_rows[1], s_index * cols, cols)
     gain_key = lax.dynamic_slice_in_dim(aux_rows[2], s_index * cols, cols)
     gain_mixture = aux_rows[3]
-    router_all = front[:, 3 * cols + 4 : 3 * cols + 4 + experts]
 
 
     all_routes = front[:, 3 * cols + 4 + experts : 3 * cols + used].astype(jnp.int32)
@@ -313,15 +449,13 @@
     mine = jnp.any(mine, axis=3)
     pair = [lax.dynamic_index_in_dim(mine, s_index ^ j, 1, keepdims=False) for j in range(2)]
     mask = jnp.concatenate(pair, axis=2).transpose(1, 0, 2)
-    order = jnp.arange(2 * tok)
-    earlier = (order[:, None] < order[None, :]).astype(bf16)
+    places = jnp.arange(2 * tok)
+    earlier = (places[:, None] < places[None, :]).astype(bf16)
     slot = jnp.einsum("met,tu->meu", mask.astype(bf16), earlier, preferred_element_type=f32)
     slot = jnp.where(mask, slot.astype(jnp.int32), -1)
-    chosen = (slot[:, :, None, :] == jnp.arange(pack)[None, None, :, None]).astype(bf16)
-
-    x_all = jnp.concatenate(chunks, axis=1).reshape(micro * length, width).astype(f32)
-    x_scale = inverse_rms(x_all)
-    a_all = (x_all * x_scale * gain_attention).astype(bf16)
+    slot = slot[:, :, None, :]
+
+    a_all = (x_all.astype(f32) * x_scale * gain_attention).astype(bf16)
     linear = nn(a_all, w_qkv)
     q_lin = linear[:, :cols]
     k_lin = linear[:, cols : 2 * cols]
@@ -330,14 +464,6 @@
     inv = lax.rsqrt(sums / width + EPSILON)
     q_inv = inv[0][:, None]
     k_inv = inv[1][:, None]
-    chunk_ids = [jnp.bitwise_xor(s_index, j) for j in range(4)]
-    positions = jnp.concatenate([c * tok + jnp.arange(tok, dtype=jnp.int32) for c in chunk_ids])
-    rate = ROPE_BASE ** (-2.0 * jnp.arange(HEAD_DIM // 2, dtype=f32) / HEAD_DIM)
-    angles = positions.astype(f32)[:, None] * rate[None, :]
-    cosine = jnp.cos(angles)
-    sine = jnp.sin(angles)
-    cosine = jnp.concatenate([cosine, cosine], axis=1)
-    sine = jnp.concatenate([-sine, sine], axis=1)
     ids = block_ids[:, 0, :]
     ids = jnp.concatenate(
         [lax.dynamic_slice_in_dim(ids, c * tok, tok, axis=1) for c in chunk_ids], axis=1
@@ -354,83 +480,57 @@
     h_n = hidden * h_scale
     b_own = (h_n * gain_mixture).astype(bf16)
 
-    def gather_pair(own):
-        got = lax.all_gather(own, "expert", axis=0, tiled=True).reshape(owners, tok, width)
-        return got
-
-    def with_near(got):
-        return jnp.concatenate([got, swap_core(got)], axis=1)
-
-    do_first = gather_pair(cotangent[0])
-    b_own, do_first = tie(b_own, do_first)
-    b_got = [gather_pair(b_own[0]), gather_pair(b_own[1])]
-    b_first, down_w, second = tie(b_got[0], down_w, cotangent[1])
-    b_got[0] = b_first
-    do_got = [do_first, gather_pair(second)]
+    def gather_expert(own):
+        return lax.all_gather(own, "expert", axis=0, tiled=True)
+
+    my_expert = 2 * e_index + core
+    low = e_index % 2
+    do_first = jnp.stack(
+        [jnp.where(low == 0, do_got, do_other), jnp.where(low == 0, do_other, do_got)], axis=1
+    ).reshape(owners, tok, width)
+    b_first = gather_expert(b_own[0][None])
+    second = gather_expert(jnp.stack([b_own[1], cotangent[1]])[None])
+    b_first, down_w = tie(b_first, down_w)
     out_parts = []
     db_list = []
     kept = []
-    router_part = jnp.zeros((width, experts), f32)
+    router_t = front[:, 3 * cols + 4 : 3 * cols + 4 + experts].T
+    is_mine = (jnp.arange(experts) == my_expert).astype(f32)[:, None]
+    router_part = jnp.zeros((experts, width), f32)
     for m in range(micro):
-        b_now, do_now = b_got[m], do_got[m]
-        if m > 0:
-            b_now, do_now, _ = tie(b_now, do_now, db_half)
-        b_pair = with_near(b_now)
-        do_pair = with_near(do_now)
-        pick = chosen[m]
-        x_p = jnp.einsum("ert,etd->erd", pick, b_pair, preferred_element_type=f32)
-        x_p = x_p.astype(bf16).reshape(owners * pack, width)
-        b_flat = b_pair.reshape(owners * 2 * tok, width)
-        logits = nn(b_flat, router_all)
-        pi = jax.nn.softmax(logits, axis=-1)
-        is_mine = (jnp.arange(experts) == my_expert).astype(f32)[None, :]
-        gate = jnp.sum(pi * is_mine, axis=1)
-        gate_p = jnp.einsum(
-            "ert,et->er", chosen[m].astype(f32), gate.reshape(owners, 2 * tok), precision=lax.Precision.HIGHEST
-        ).reshape(-1, 1)
-        gl = nn(x_p, gate_w)
-        ul = nn(x_p, up_w)
-        sg = 1.0 / (1.0 + jnp.exp(-gl))
-        silu = gl * sg
-        act = (silu * ul).astype(bf16)
-        y = nn(act, down_w).astype(bf16).astype(f32)
-        weighted = (gate_p * y).astype(bf16).reshape(owners, pack, width)
-        out_part = jnp.einsum("ert,erd->etd", pick, weighted, preferred_element_type=f32).astype(bf16)
-        out_half = out_part[:, :tok].astype(f32) + swap_core(out_part[:, tok:]).astype(f32)
-        out_parts.append(out_half.astype(bf16))
-        do_p = jnp.einsum("ert,etd->erd", pick, do_pair, preferred_element_type=f32)
-        do_p = do_p.reshape(owners * pack, width)
-        dgate_p = jnp.sum(y * do_p, axis=1)
-        dy = (gate_p * do_p).astype(bf16)
-        dact = nt(dy, down_w)
-        dgl = (dact * ul * sg * (1.0 + gl * (1.0 - sg))).astype(bf16)
-        dul = (dact * silu).astype(bf16)
-        drow = (nt(dgl, gate_w) + nt(dul, up_w)).astype(bf16).reshape(owners, pack, width)
-        dgate = jnp.einsum(
-            "ert,er->et", chosen[m].astype(f32), dgate_p.reshape(owners, pack), precision=lax.Precision.HIGHEST
-        ).reshape(-1, 1)
-        dz = (dgate * gate[:, None] * (is_mine - pi)).astype(bf16)
-        router_part = router_part + tn(b_flat, dz)
-        db_part = jnp.einsum("ert,erd->etd", pick, drow, preferred_element_type=f32)
-        db_part = db_part + nt(dz, router_all).reshape(owners, 2 * tok, width)
-        db_half = (db_part[:, :tok] + swap_core(db_part[:, tok:].astype(bf16)).astype(f32)).astype(bf16)
+        if m == 0:
+            values = (b_first, swap_core(b_first), do_first, swap_core(do_first))
+        else:
+            second, _ = tie(second, db_half)
+            near = swap_core(second)
+            values = ((second, 0), (near, 0), (second, 1), (near, 1))
+        *saved, out_mine, out_near, db_mine, db_near, part = expert_step(
+            slot[m], *values, gate_w, up_w, down_w, router_t, is_mine, pack
+        )
+        router_part = router_part + part
+        db_half = (db_mine.astype(f32) + swap_core(db_near).astype(f32)).astype(bf16)
         db_list.append(lax.psum_scatter(db_half, "expert", scatter_dimension=0, tiled=True)[0])
-        kept.append((x_p, act, dy, dgl, dul))
+        out_parts.append((out_mine, out_near))
+        kept.append([v.reshape(owners * pack, v.shape[2]) for v in saved])
     x_k, act_k, dy_k, dgl_k, dul_k = [jnp.concatenate(group, axis=0) for group in zip(*kept)]
+    outs = [v for pair in out_parts for v in pair]
+    _, db_list[0], x_k, act_k, *outs = tie(db_half, db_list[0], x_k, act_k, *outs)
+    out_parts = [
+        (outs[2 * m].astype(f32) + swap_core(outs[2 * m + 1]).astype(f32)).astype(bf16) for m in range(micro)
+    ]
     full_gate = tn(x_k, dgl_k)
     full_up = tn(x_k, dul_k)
     full_down = tn(act_k, dy_k)
     mixture_part = jnp.zeros((width,), f32)
-    attention_part = jnp.zeros((width,), f32)
     query_part = jnp.zeros((cols,), f32)
     key_part = jnp.zeros((cols,), f32)
     x_own = tokens.astype(f32)
     own_scale = inverse_rms(x_own)
     dh_rows = []
     dqkv_rows = []
+    d_hiddens = []
     input_grads = []
     for m in range(micro):
-        rows_m = slice(m * length, (m + 1) * length)
         db = db_list[m].astype(f32)
         mixture_part = mixture_part + jnp.sum(db * h_n[m], axis=0)
         w_g = db * gain_mixture
@@ -438,39 +538,32 @@
             w_g - h_n[m] * jnp.mean(w_g * h_n[m], axis=-1, keepdims=True)
         )
         dh_m = jnp.concatenate(gather_shard(d_hidden.astype(bf16)), axis=0)
-        dh_m, full_gate, full_up, full_down = tie(dh_m, full_gate, full_up, full_down)
-        if m > 0:
-            sent = [send_side(full, side) for full in (full_gate, full_up, full_down)]
+        if m == 0:
+            out_part = jnp.stack(out_parts, axis=1)
+            dh_m, full_gate, full_up, full_down, out_part = tie(dh_m, full_gate, full_up, full_down, out_part)
         dh_rows.append(dh_m)
         w_q, w_k, d_v, part_q, part_k, sums = attend_back(
-            m, dh_m, w_o, linear, q_r, k_r, v_r, lse, q_inv, k_inv, gain_query, gain_key, cosine, sine, ids, heads
+            m, dh_m, w_o, linear, q_r, k_r, v_r, lse, q_inv, k_inv, gain_query, gain_key, cosine, sine, ids, order, heads
         )
         query_part = query_part + part_q[0]
         key_part = key_part + part_k[0]
-        sums = sum_rows(sums[:, 0], core, side, tok) / width
-        d_qkv = project_back(m, w_q, w_k, d_v, linear, q_inv, k_inv, sums[0][:, None], sums[1][:, None])
+        sums = lax.all_gather(sums, "shard", axis=0)
+        d_qkv = project_back(m, w_q, w_k, d_v, linear, q_inv, k_inv, sums, order)
         if m + 1 < micro:
-            db_list[m + 1], d_qkv, *out_parts = tie(db_list[m + 1], d_qkv, *out_parts)
-            out_own = lax.psum_scatter(jnp.stack(out_parts), "expert", scatter_dimension=1, tiled=True)
+            db_list[m + 1], d_qkv, out_part = tie(db_list[m + 1], d_qkv, out_part)
+            out_own = lax.psum_scatter(out_part, "expert", scatter_dimension=0, tiled=True)[0]
         dqkv_rows.append(d_qkv)
-        da_part = nt(d_qkv, w_qkv)
-        attention_part = attention_part + jnp.sum(da_part * (x_all * x_scale)[rows_m], axis=0)
-        da_part = da_part.reshape(4, tok, width)
-        da = scatter_shard([da_part[j] for j in range(4)])
-        x_n = x_own[m] * own_scale[m]
-        a_g = da * gain_attention
-        grad = d_hidden + own_scale[m] * (a_g - x_n * jnp.mean(a_g * x_n, axis=-1, keepdims=True))
-        input_grads.append(grad.astype(bf16))
-    input_grad = jnp.stack(input_grads)
+        d_hiddens.append(d_hidden)
     dh_all = jnp.concatenate(dh_rows, axis=0)
-    d_qkv = jnp.concatenate(dqkv_rows, axis=0)
-    grad_wo = tn(o_all, dh_all).astype(bf16)
-    grad_wo = grad_wo.reshape(owners, rows, 4, cols).transpose(0, 2, 1, 3).reshape(width, cols)
+    grad_wo = jnp.stack(
+        [tn(o_all, dh_all[:, i * cols : (i + 1) * cols]).astype(bf16).reshape(owners, rows, cols) for i in range(4)],
+        axis=1,
+    ).reshape(width, cols)
 
     blank = jnp.zeros((width,), f32)
     gains = jnp.stack(
         [
-            attention_part,
+            blank,
             lax.dynamic_update_slice(blank, query_part, (s_index * cols,)),
             lax.dynamic_update_slice(blank, key_part, (s_index * cols,)),
             mixture_part,
@@ -478,15 +571,28 @@
         axis=1,
     )
     (aux_grad,) = tie(
-        jnp.concatenate([gains, router_part, jnp.zeros((width, aux_cols - 4 - experts), f32)], axis=1).astype(bf16)
-    )
-    grad_payload = jnp.concatenate([tn(a_all, d_qkv).astype(bf16), grad_wo, aux_grad], axis=1)
-    grad_payload, out_own = tie(grad_payload, out_own)
-    output = (hidden + out_own[:, 0].astype(f32)).astype(bf16)
-    grad_gate = share_expert_grad(full_gate, sent[0], core, side)
-    grad_up = share_expert_grad(full_up, sent[1], core, side)
-    grad_down = share_expert_grad(full_down, sent[2], core, side)
+        jnp.concatenate([gains, router_part.T, jnp.zeros((width, aux_cols - 4 - experts), f32)], axis=1).astype(bf16)
+    )
+    grad_payload = jnp.concatenate([tn(a_all, jnp.concatenate(dqkv_rows, axis=0)).astype(bf16), grad_wo, aux_grad], axis=1)
+    grad_payload, out_own, *dqkv_rows = tie(grad_payload, out_own, *dqkv_rows)
     grad_own = lax.psum_scatter(grad_payload, "expert", scatter_dimension=0, tiled=True)
+    output = (hidden + out_own.astype(f32)).astype(bf16)
+    for m in range(micro):
+        da_part = nt(dqkv_rows[m], w_qkv)
+        da_part = da_part.reshape(4, tok, width)
+        da = scatter_shard([da_part[j] for j in range(4)])
+        da, full_gate, full_up, full_down = tie(da, full_gate, full_up, full_down)
+        x_n = x_own[m] * own_scale[m]
+        a_g = da * gain_attention
+        grad = d_hiddens[m] + own_scale[m] * (a_g - x_n * jnp.mean(a_g * x_n, axis=-1, keepdims=True))
+        input_grads.append(grad.astype(bf16))
+    input_grad = jnp.stack(input_grads)
+    sent_gate = send_side(full_gate, side)
+    sent_up = send_side(full_up, side)
+    sent_down = send_side(full_down, side)
+    grad_gate = share_expert_grad(full_gate, sent_gate, core, side)
+    grad_up = share_expert_grad(full_up, sent_up, core, side)
+    grad_down = share_expert_grad(full_down, sent_down, core, side)
     grad_own = grad_own.reshape(4, rows, 4 * cols + aux_cols)
     grad_wo = grad_own[:, :, 3 * cols : 4 * cols].transpose(1, 0, 2).reshape(rows, width)
     grad_wo = lax.ppermute(grad_wo, BOTH, [(d, b) for b, d in moves]).astype(f32)
@@ -497,6 +603,10 @@
         for i in range(3)
     ]
     aux_sum = jnp.sum(grad_own[:, :, 3 * cols :], axis=0)
+    grad_gain = sum(
+        jnp.sum(w.astype(f32) * g, axis=1) for w, g in ((w_query, grad_q), (w_key, grad_k), (w_value, grad_v))
+    )
+    grad_gain = grad_gain / attention_gain.astype(f32)
     return (
         output,
         input_grad,
@@ -505,7 +615,7 @@
         grad_v,
         grad_wo,
         aux_sum[:, 4 : 4 + experts],
-        aux_sum[:, 0],
+        grad_gain,
         aux_sum[:, 1],
         aux_sum[:, 2],
         aux_sum[:, 3],

time: 990 us -> 926 us (0.935)
  matrix products: 223 us -> 74.5 us
  Pallas kernels: 45.3 us -> 142 us
  local copies, waits for them, and re-layouts: 108 us -> 84.8 us
  waiting for transfers between devices: 417 us -> 438 us
  starting transfers between devices: 49 us -> 30.1 us
  other arithmetic: 89.4 us -> 99.7 us
    dot_general x27 -> x12, matrix products: 183 us -> 74.4 us  [dot(): lax.dot_general(left, right, (dims, ((), ())), preferred_element_type=f32)]
    pallas_call x0 -> x2, Pallas kernels: none -> 89.6 us  [expert_step(): pl.pallas_call(expert_body, grid=(owners // group,), in_specs=[pl.BlockSp...]
    dot_general x12 -> x0, matrix products: 39.1 us -> none  [the longest x2 12.6 us: local(): db_part = jnp.einsum('ert,erd->etd', pick, drow, preferred_element_type=f32)]
    reduce_scatter x1, waiting for transfers between devices: 26.4 us -> 47.2 us  [local(): lax.psum_scatter(out_part, 'expert', scatter_dimension=0, tiled=True)[0]]
    ppermute x12, starting transfers between devices: 33.8 us -> 16.1 us  [swap_side(): return lax.ppermute(values, 'shard', [(s, s ^ 2) for s in range(4)])]
    convert_element_type x10 -> x5, other arithmetic: 28.1 us -> 13.7 us  [the longest x2 11.1 us: local(): (db_mine.astype(f32) + swap_core(db_near).astype(f32)).astype(bf16)]
    ppermute x12, waiting for transfers between devices: 292 us -> 280 us  [swap_side(): return lax.ppermute(values, 'shard', [(s, s ^ 2) for s in range(4)])]
    all_gather x5 -> x4, waiting for transfers between devices: 57.3 us -> 69.4 us  [the longest x2 47.5 us: gather_expert(): return lax.all_gather(own, 'expert', axis=0, tiled=True)]
  transfers between devices with their start and end apart: 48 -> 47, of which waited for: 19 -> 25; matrix products, arithmetic and copies ran while one was open for 38% -> 25% of each run, Pallas kernels for 5% -> 15%
where the time goes in v2:
time: 926 us; the launch traced here: 917 us
  waiting for transfers between devices  438 us (47%)
  Pallas kernels  142 us (15%)
  other arithmetic  99.7 us (11%)
  local copies, waits for them, and re-layouts  84.8 us (9%)
  matrix products  74.5 us (8%)
  blocking collectives  32.8 us (4%)
  starting transfers between devices  30.1 us (3%)
  between operations  15.4 us (2%)
    ppermute x12, waiting for transfers between devices, swap_side(): return lax.ppermute(values, 'shard', [(s, s ^ 2) for s in range(4)])  280 us
    pallas_call x2, Pallas kernels, expert_step(): pl.pallas_call(expert_body, grid=(owners // group,), in_specs=[pl.BlockSp...  89.6 us
    dot_general x12, matrix products, dot(): lax.dot_general(left, right, (dims, ((), ())), preferred_element_type=f32)  74.4 us
    all_gather x2, waiting for transfers between devices, gather_expert(): return lax.all_gather(own, 'expert', axis=0, tiled=True)  47.5 us
    reduce_scatter x1, waiting for transfers between devices, local(): lax.psum_scatter(out_part, 'expert', scatter_dimension=0, tiled=True)[0]  47.2 us
    pallas_call x2, Pallas kernels, attend_back(): pl.pallas_call(attend_back_body, grid=(heads,), in_specs=[pl.BlockSpec((l...  34 us
    unnamed x144, local copies, waits for them, and re-layouts  25.9 us
    ppermute x22, waiting for transfers between devices, swap_core(): return lax.ppermute(values, 'shard', [(s, s ^ 1) for s in range(4)])  22.6 us
  transfers between devices with their start and end apart: 47, of which 25 were waited for; matrix products, arithmetic and copies ran while one was open for 25% of the time, Pallas kernels for 15%

profile of v2, /device:TPU:2, one launch (start us, length us, event | category | flops | bytes accessed | tf_op | source)
XLA Modules:
  0.0 917.3 jit_solution(12400489098793833180)
XLA Ops:
  28.3 15.5 %all_to_all.10 = bf16[4,64,1664]{2,1,0:T(8,128)(2,1)} all-to-all(bf16[4,64,1664]{2,1,0:T(8,128)(2,1)S(1)} %copy.159), channel_id=1, replica_groups=mesh['expert'=8,'shard'=4] {'shard'}, dimensions={0} | all-to-all | bytes 1703936 | tf_op jit(solution)/shard_map/all_to_all | solution.py:409
  43.8 7.6 all-gather.11.cloned.1.call-done
  55.3 3.2 collective-permute-start.4
  59.7 2.4 constant_dynamic-slice_fusion.7
  64.1 3.0 fusion.78
  81.9 4.6 pad_maximum_fusion.4
  86.5 2.5 pad_maximum_fusion.3
  90.7 33.4 %collective-permute-done.3 = bf16[2,512,1024]{2,1,0:T(8,128)(2,1)} collective-permute-done((bf16[2,512,1024]{2,1,0:T(8,128)(2,1)}, bf16[2,512,1024]{2,1,0:T(8,128)(2,1)}, u32[]{:S(2)}, u32[]{:S(2)}) %collective-permute-start.3) | collective-permute-done | bytes 2097184 | tf_op jit(solution)/shard_map/ppermute | solution.py:40
  124.1 3.1 constant_dynamic-update-slice_fusion.15
  127.2 41.2 %collective-permute-done.1 = bf16[2,512,1024]{2,1,0:T(8,128)(2,1)} collective-permute-done((bf16[2,512,1024]{2,1,0:T(8,128)(2,1)S(1)}, bf16[2,512,1024]{2,1,0:T(8,128)(2,1)}, u32[]{:S(2)}, u32[]{:S(2)}) %collective-permute-start.1) | collective-permute-done | bytes 2097184 | tf_op jit(solution)/shard_map/ppermute | solution.py:40
  168.4 3.1 constant_dynamic-update-slice_fusion.17
  173.4 8.2 fusion.8.q_ref.k_ref.v_ref
  184.4 6.3 all_gather.32
  194.1 11.0 %shard_map.263 = (bf16[768,512]{1,0:T(8,128)(2,1)}, bf16[768,512]{1,0:T(8,128)(2,1)}, bf16[768,512]{1,0:T(8,128)(2,1)}, bf16[768,512]{1,0:T(8,128)(2,1)}, f32[8,384,1]{2,1,0:T(8,128)}) custom-call(f32[768,1536]{1,0:T(8,128)} %copy-done, f32[768,1536]{1,0:T(8,128)} %copy-done, f32[768,1536]{1,0:T(8,128)} %copy-done, f32[768,1]{1,0:T(8,128)} %copy.161.qi_ref, ...), custom_call_target="tpu_custom_call" | custom-call | tf_op jit(solution)/shard_map/pallas_call | solution.py:116
  205.2 14.3 %all-gather.15.cloned.1.call-done.wo_ref = bf16[512,2048]{1,0:T(8,128)(2,1)} async-done(((bf16[64,2048]{1,0:T(8,128)(2,1)}), bf16[512,2048]{1,0:T(8,128)(2,1)}) %all-gather.15.cloned.1.call-update) | async-done | bytes 2097168 | tf_op jit(solution)/shard_map/all_gather | solution.py:437
  219.4 3.6 fusion.87
  223.5 3.4 collective-permute-done.8
  229.0 18.1 %collective-permute-done.9 = bf16[2,96,2048]{2,1,0:T(8,128)(2,1)S(1)} collective-permute-done((bf16[2,96,2048]{2,1,0:T(8,128)(2,1)S(1)}, bf16[2,96,2048]{2,1,0:T(8,128)(2,1)S(1)}, u32[]{:S(2)}, u32[]{:S(2)}) %collective-permute-start.9) | collective-permute-done | bytes 786464 | tf_op jit(solution)/shard_map/ppermute | solution.py:40
  250.5 2.3 constant_dynamic-slice_fusion
  255.8 2.3 constant_dynamic-update-slice_fusion.14
  261.1 2.6 pad_maximum_fusion.5
  263.7 42.5 %collective-permute-done.11 = bf16[2,256,2048]{2,1,0:T(8,128)(2,1)} collective-permute-done((bf16[2,256,2048]{2,1,0:T(8,128)(2,1)}, bf16[2,256,2048]{2,1,0:T(8,128)(2,1)}, u32[]{:S(2)}, u32[]{:S(2)}) %collective-permute-start.11) | collective-permute-done | bytes 2097184 | tf_op jit(solution)/shard_map/ppermute | solution.py:40
  308.1 4.4 collective-permute-done.13
  316.1 10.6 %all-gather.17.cloned.1.call-done.bo_ref = bf16[8,96,2048]{2,1,0:T(8,128)(2,1)} async-done(((bf16[1,96,2048]{2,1,0:T(8,128)(2,1)}), bf16[8,96,2048]{2,1,0:T(8,128)(2,1)}) %all-gather.17.cloned.1.call-update) | async-done | bytes 3145744 | tf_op jit(solution)/shard_map/all_gather | solution.py:484
  332.7 45.4 %shard_map.264 = (bf16[8,112,2048]{2,1,0:T(8,128)(2,1)}, bf16[8,112,1024]{2,1,0:T(8,128)(2,1)}, bf16[8,112,2048]{2,1,0:T(8,128)(2,1)}, bf16[8,112,1024]{2,1,0:T(...) custom-call(s32[8,1,192]{2,1,0:T(1,128)} %get-tuple-element.237.slot, ...), custom_call_target="tpu_custom_call" | custom-call | tf_op jit(solution)/shard_map/pallas_call | solution.py:322
  378.4 5.7 collective-permute-done.15
  384.1 5.0 add_convert_fusion.3
  389.1 36.9 %all-gather.19.cloned.1.call-done = bf16[16,96,2048]{2,1,0:T(8,128)(2,1)} async-done(((bf16[2,96,2048]{2,1,0:T(8,128)(2,1)}), bf16[16,96,2048]{2,1,0:T(8,128)(2,1)}) %all-gather.19.cloned.1.call-update) | async-done | bytes 6291472 | tf_op jit(solution)/shard_map/all_gather | solution.py:484
  426.3 10.3 %collective-permute-done.16.bn_ref.dn_ref = bf16[8,2,96,2048]{3,2,1,0:T(8,128)(2,1)} collective-permute-done((bf16[8,2,96,2048]{3,2,1,0:T(8,128)(2,1)}, bf16[8,2,96,2048]{3,2,1,0:T(8,128)(2,1)}, u32[]{:S(2)}, u32[]{:S(2)}) %collective-permute-start.16) | collective-permute-done | bytes 6291488 | tf_op jit(solution)/shard_map/ppermute | solution.py:36
  436.6 44.2 %shard_map.265 = (bf16[8,112,2048]{2,1,0:T(8,128)(2,1)}, bf16[8,112,1024]{2,1,0:T(8,128)(2,1)}, bf16[8,112,2048]{2,1,0:T(8,128)(2,1)}, bf16[8,112,1024]{2,1,0:T(...) custom-call(s32[8,1,192]{2,1,0:T(1,128)} %get-tuple-element.238.slot, ...), custom_call_target="tpu_custom_call" | custom-call | tf_op jit(solution)/shard_map/pallas_call | solution.py:322
  482.4 4.3 pad_maximum_fusion.6
  486.7 7.5 pad_maximum_fusion.1
  494.2 6.1 add_convert_fusion.2
  500.6 2.5 reduce-scatter.7.cloned.1.call-done
  509.0 13.3 %fusion.14 = f32[2048,1024]{1,0:T(8,128)} fusion(bf16[1792,2048]{1,0:T(8,128)(2,1)} %pad_maximum_fusion.1, bf16[896,1024]{1,0:T(8,128)(2,1)} %bitcast.349, bf16[896,1024]{1,0:T(8,128)(2,1)} %bitcast.347), kind=kOutput, calls=%fused_computation.34 | convolution fusion | flops 7523532800 | bytes 19398656 | tf_op jit(solution)/shard_map/dot_general | solution.py:20
  522.4 11.9 %fusion.10 = f32[2048,1024]{1,0:T(8,128)} fusion(bf16[1792,2048]{1,0:T(8,128)(2,1)S(1)} %bitcast.272, bf16[896,1024]{1,0:T(8,128)(2,1)} %bitcast.348, bf16[896,1024]{1,0:T(8,128)(2,1)S(1)} %bitcast.346), kind=kOutput, calls=%fused_computation.30 | convolution fusion | flops 7523532800 | bytes 19398656 | tf_op jit(solution)/shard_map/dot_general | solution.py:20
  534.8 12.2 %fusion = f32[1024,2048]{1,0:T(8,128)} fusion(bf16[1792,1024]{1,0:T(8,128)(2,1)S(1)} %copy-done.13, bf16[896,2048]{1,0:T(8,128)(2,1)} %bitcast.345, bf16[896,2048]{1,0:T(8,128)(2,1)S(1)} %bitcast.344), kind=kOutput, calls=%fused_computation.3 | convolution fusion | flops 7530872832 | bytes 19398656 | tf_op jit(solution)/shard_map/dot_general | solution.py:20
  552.3 3.3 pad_maximum_fusion.2
  555.6 16.9 %shard_map.266 = (f32[384,512]{1,0:T(8,128)}, f32[384,512]{1,0:T(8,128)}, bf16[384,512]{1,0:T(8,128)(2,1)}, f32[1,512]{1,0:T(1,128)}, f32[1,512]{1,0:T(1,128)}, /*index=5*/f32[2,384]{1,0:T(2,128)}) custom-call(bf16[384,2048]{1,0:T(8,128)(2,1)} %pad_maximum_fusion.10.dh_ref, bf16[512,2048]{1,0:T(8,128)(2,1)} %all-gather.15.cloned.1.call-done.wo_ref, ...), custom_call_target="tpu_custom_call" | custom-call | tf_op jit(solution)/shard_map/pallas_call | solution.py:180
  572.5 5.8 all-gather.3.sum_ref
  578.3 3.7 shard_map.267
  587.4 10.0 %collective-permute-done.24 = bf16[96,2048]{1,0:T(8,128)(2,1)S(1)} collective-permute-done((bf16[96,2048]{1,0:T(8,128)(2,1)S(1)}, bf16[96,2048]{1,0:T(8,128)(2,1)S(1)}, u32[]{:S(2)}, u32[]{:S(2)}) %collective-permute-start.24) | collective-permute-done | bytes 393248 | tf_op jit(solution)/shard_map/ppermute | solution.py:40
  600.3 17.1 %shard_map.268 = (f32[384,512]{1,0:T(8,128)}, f32[384,512]{1,0:T(8,128)}, bf16[384,512]{1,0:T(8,128)(2,1)}, f32[1,512]{1,0:T(1,128)}, f32[1,512]{1,0:T(1,128)}, /*index=5*/f32[2,384]{1,0:T(2,128)}) custom-call(bf16[384,2048]{1,0:T(8,128)(2,1)} %pad_maximum_fusion.11.dh_ref, bf16[512,2048]{1,0:T(8,128)(2,1)} %all-gather.15.cloned.1.call-done.wo_ref, ...), custom_call_target="tpu_custom_call" | custom-call | tf_op jit(solution)/shard_map/pallas_call | solution.py:180
  629.4 3.9 copy.185
  633.3 5.2 all-gather.4.sum_ref
  638.5 3.9 shard_map.269
  642.4 7.9 convolution_convert_fusion
  650.4 4.2 pad_maximum_fusion
  654.6 47.2 %reduce-scatter.9.cloned.1.call-done = bf16[1,2,96,2048]{3,2,1,0:T(8,128)(2,1)} async-done(((bf16[8,2,96,2048]{3,2,1,0:T(8,128)(2,1)}), bf16[1,2,96,2048]{3,2,1,0:T(8,128)(2,1)}) %reduce-scatter.9.cloned.1.call-update) | async-done | bytes 786448 | tf_op jit(solution)/shard_map/reduce_scatter | solution.py:554
  703.1 4.7 fusion.86
  709.1 5.2 fusion.85
  718.6 8.7 collective-permute-done.27
  727.5 7.4 collective-permute-done.29
  743.4 40.6 %collective-permute-done.35 = bf16[2,256,2048]{2,1,0:T(8,128)(2,1)} collective-permute-done((bf16[2,256,2048]{2,1,0:T(8,128)(2,1)S(1)}, bf16[2,256,2048]{2,1,0:T(8,128)(2,1)}, u32[]{:S(2)}, u32[]{:S(2)}) %collective-permute-start.35) | collective-permute-done | bytes 2097184 | tf_op jit(solution)/shard_map/ppermute | solution.py:40
  784.0 4.3 convert_add_fusion
  791.1 37.9 %collective-permute-done.31 = bf16[2,512,1024]{2,1,0:T(8,128)(2,1)} collective-permute-done((bf16[2,512,1024]{2,1,0:T(8,128)(2,1)S(1)}, bf16[2,512,1024]{2,1,0:T(8,128)(2,1)}, u32[]{:S(2)}, u32[]{:S(2)}) %collective-permute-start.31) | collective-permute-done | bytes 2097184 | tf_op jit(solution)/shard_map/ppermute | solution.py:40
  828.9 2.6 convert_add_fusion.2
  832.9 39.4 %collective-permute-done.33 = bf16[2,512,1024]{2,1,0:T(8,128)(2,1)} collective-permute-done((bf16[2,512,1024]{2,1,0:T(8,128)(2,1)}, bf16[2,512,1024]{2,1,0:T(8,128)(2,1)}, u32[]{:S(2)}, u32[]{:S(2)}) %collective-permute-start.33) | collective-permute-done | bytes 2097184 | tf_op jit(solution)/shard_map/ppermute | solution.py:40
  872.3 4.4 convert_add_fusion.1
  882.8 3.5 all-to-all-start.1
  886.3 2.8 convert_dynamic-update-slice_fusion.2
  889.1 2.5 collective-permute-start.30
  891.7 2.8 convert_dynamic-update-slice_fusion.1
  894.5 12.1 %collective-permute-done.30 = bf16[64,2048]{1,0:T(8,128)(2,1)S(1)} collective-permute-done((bf16[64,2048]{1,0:T(8,128)(2,1)S(1)}, bf16[64,2048]{1,0:T(8,128)(2,1)S(1)}, u32[]{:S(2)}, u32[]{:S(2)}) %collective-permute-start.30) | collective-permute-done | bytes 262176 | tf_op jit(solution)/shard_map/ppermute | solution.py:598
  (384 shorter events, 139.4 us)
Async XLA Ops:
  7.2 44.2 %all-gather.11.cloned.1.call-start = ((), (), s32[]{:S(2)}) async-start(), calls=%async_computation.6 | async-start | bytes 1966080 | tf_op jit(solution)/shard_map/all_gather | solution.py:410
  10.8 14.1 %copy-start.27 = (bf16[64,2048]{1,0:T(8,128)(2,1)S(1)}, bf16[64,2048]{1,0:T(8,128)(2,1)}, u32[]{:S(2)}) copy-start(bf16[64,2048]{1,0:T(8,128)(2,1)} %param.22) | copy-start | bytes 786436
  13.0 158.5 %all-gather.13.cloned.1.call-start = ((), (), s32[]{:S(2)}) async-start(), calls=%async_computation.7 | async-start | bytes 7667712 | tf_op jit(solution)/shard_map/all_gather | solution.py:412
  53.6 165.8 %all-gather.15.cloned.1.call-start = ((), (), s32[]{:S(2)}) async-start(), calls=%async_computation.8 | async-start | bytes 2359296 | tf_op jit(solution)/shard_map/all_gather | solution.py:437
  53.7 24.0 %collective-permute-start.5 = (bf16[2,96,2048]{2,1,0:T(8,128)(2,1)}, bf16[2,96,2048]{2,1,0:T(8,128)(2,1)}, u32[]{:S(2)}, u32[]{:S(2)}) collective-permute-start(bf16[2,96,2048]{2,1,0:T(8,128)(2,1)} %param.16), channel_id=1, source_target_pairs={{0,1},{1,0},{2,3},{3,2},{4,5},{5,4},{6,7},{7,6},{8,9},{9,8},{10,11... | collective-permute-start | bytes 2359304 | tf_op jit(solution)/shard_map/ppermute | solution.py:36
  53.8 23.9 %collective-permute-start.6 = (bf16[2,96,2048]{2,1,0:T(8,128)(2,1)}, bf16[2,96,2048]{2,1,0:T(8,128)(2,1)}, u32[]{:S(2)}, u32[]{:S(2)}) collective-permute-start(bf16[2,96,2048]{2,1,0:T(8,128)(2,1)} %param.16), channel_id=1, source_target_pairs={{0,2},{1,3},{2,0},{3,1},{4,6},{5,7},{6,4},{7,5},{8,10},{9,11},{10,... | collective-permute-start | bytes 2359304 | tf_op jit(solution)/shard_map/ppermute | solution.py:40
  55.3 116.2 %collective-permute-start.4 = (bf16[64,2048]{1,0:T(8,128)(2,1)}, bf16[64,2048]{1,0:T(8,128)(2,1)}, u32[]{:S(2)}, u32[]{:S(2)}) collective-permute-start(bf16[64,2048]{1,0:T(8,128)(2,1)} %param.23), channel_id=1, source_target_pairs={{0,0},{1,4},{2,8},{3,12},{4,16},{5,20},{6,24},{7,28},{8,1},{9,5},{... | collective-permute-start | bytes 786440 | tf_op jit(solution)/shard_map/ppermute | solution.py:419
  59.6 13.1 %collective-permute-start = (bf16[1,512,1024]{2,1,0:T(8,128)(2,1)}, bf16[1,512,1024]{2,1,0:T(8,128)(2,1)}, u32[]{:S(2)}, u32[]{:S(2)}) collective-permute-start(bf16[1,512,1024]{2,1,0:T(8,128)(2,1)} %constant_dynamic-slice_fusion.8), channel_id=1, source_target_pairs={{0,1},{1,0},{2,3},{3,2},{4,5},{5,4},{6,7},{7,6},{8,9},{9,8},{10,11... | collective-permute-start | bytes 3145736 | tf_op jit(solution)/shard_map/ppermute | solution.py:36
  62.1 5.2 collective-permute-start.2
  69.6 54.5 %collective-permute-start.3 = (bf16[2,512,1024]{2,1,0:T(8,128)(2,1)}, bf16[2,512,1024]{2,1,0:T(8,128)(2,1)}, u32[]{:S(2)}, u32[]{:S(2)}) collective-permute-start(bf16[2,512,1024]{2,1,0:T(8,128)(2,1)} %constant_dynamic-update-slice_fusion.16), channel_id=1, source_target_pairs={{0,2},{1,3},{2,0},{3,1},{4,6},{5,7},{6,4},{7,5},{8,10},{9,11},{10,... | collective-permute-start | bytes 6291464 | tf_op jit(solution)/shard_map/ppermute | solution.py:40
  74.0 94.4 %collective-permute-start.1 = (bf16[2,512,1024]{2,1,0:T(8,128)(2,1)S(1)}, bf16[2,512,1024]{2,1,0:T(8,128)(2,1)}, u32[]{:S(2)}, u32[]{:S(2)}) collective-permute-start(bf16[2,512,1024]{2,1,0:T(8,128)(2,1)S(1)} %constant_dynamic-update-slice_fusion.18), channel_id=1, source_target_pairs={{0,2},{1,3},{2,0},{3,1},{4,6},{5,7},{6,4},{7,5},{8,10},{9,11},{10,... | collective-permute-start | bytes 6291464 | tf_op jit(solution)/shard_map/ppermute | solution.py:40
  77.7 11.3 %collective-permute-start.7 = (bf16[2,96,2048]{2,1,0:T(8,128)(2,1)}, bf16[2,96,2048]{2,1,0:T(8,128)(2,1)S(1)}, u32[]{:S(2)}, u32[]{:S(2)}) collective-permute-start(bf16[2,96,2048]{2,1,0:T(8,128)(2,1)} %collective-permute-done.6), channel_id=1, source_target_pairs={{0,1},{1,0},{2,3},{3,2},{4,5},{5,4},{6,7},{7,6},{8,9},{9,8},{10,11... | collective-permute-start | bytes 2359304 | tf_op jit(solution)/shard_map/ppermute | solution.py:36
  90.0 37.3 %copy-start.12 = (bf16[2,384,2048]{2,1,0:T(8,128)(2,1)}, bf16[2,384,2048]{2,1,0:T(8,128)(2,1)S(1)}, u32[]{:S(2)}) copy-start(bf16[2,384,2048]{2,1,0:T(8,128)(2,1)S(1)} %constant_dynamic-update-slice_fusion) | copy-start | bytes 9437188
  171.5 155.2 %all-gather.17.cloned.1.call-start = ((), (), s32[]{:S(2)}) async-start(), calls=%async_computation.9 | async-start | bytes 3538944 | tf_op jit(solution)/shard_map/all_gather | solution.py:484
  223.4 3.5 collective-permute-start.8
  227.3 19.8 %copy-start.18 = (bf16[2,96,2048]{2,1,0:T(8,128)(2,1)S(1)}, bf16[2,96,2048]{2,1,0:T(8,128)(2,1)}, u32[]{:S(2)}) copy-start(bf16[2,96,2048]{2,1,0:T(8,128)(2,1)} %param.16) | copy-start | bytes 2359300
  227.5 19.6 %collective-permute-start.9 = (bf16[2,96,2048]{2,1,0:T(8,128)(2,1)S(1)}, bf16[2,96,2048]{2,1,0:T(8,128)(2,1)S(1)}, u32[]{:S(2)}, u32[]{:S(2)}) collective-permute-start(bf16[2,96,2048]{2,1,0:T(8,128)(2,1)S(1)} %fusion.24), channel_id=1, source_target_pairs={{0,2},{1,3},{2,0},{3,1},{4,6},{5,7},{6,4},{7,5},{8,10},{9,11},{10,... | collective-permute-start | bytes 2359304 | tf_op jit(solution)/shard_map/ppermute | solution.py:40
  250.5 175.6 %all-gather.19.cloned.1.call-start = ((), (), s32[]{:S(2)}) async-start(), calls=%async_computation.14 | async-start | bytes 7077888 | tf_op jit(solution)/shard_map/all_gather | solution.py:484
  252.8 3.0 collective-permute-start.10
  253.8 249.3 %reduce-scatter.7.cloned.1.call-start = ((), (), s32[]{:S(2)}) async-start(), calls=%async_computation.11 | async-start | bytes 3538944 | tf_op jit(solution)/shard_map/reduce_scatter | solution.py:512
  258.2 48.0 %collective-permute-start.11 = (bf16[2,256,2048]{2,1,0:T(8,128)(2,1)}, bf16[2,256,2048]{2,1,0:T(8,128)(2,1)}, u32[]{:S(2)}, u32[]{:S(2)}) collective-permute-start(bf16[2,256,2048]{2,1,0:T(8,128)(2,1)} %constant_dynamic-update-slice_fusion.14), channel_id=1, source_target_pairs={{0,2},{1,3},{2,0},{3,1},{4,6},{5,7},{6,4},{7,5},{8,10},{9,11},{10,... | collective-permute-start | bytes 6291464 | tf_op jit(solution)/shard_map/ppermute | solution.py:40
  259.6 52.8 %collective-permute-start.13 = (bf16[4,96,2048]{2,1,0:T(8,128)(2,1)}, bf16[4,96,2048]{2,1,0:T(8,128)(2,1)}, u32[]{:S(2)}, u32[]{:S(2)}) collective-permute-start(bf16[4,96,2048]{2,1,0:T(8,128)(2,1)} %all-gather.11.cloned.1.call-done), channel_id=1, source_target_pairs={{0,4},{4,0},{8,12},{12,8},{16,20},{20,16},{24,28},{28,24},{1,5},{5... | collective-permute-start | bytes 4718600 | tf_op jit(solution)/shard_map/ppermute | solution.py:66
  263.7 48.7 %copy-start.24 = (bf16[4,96,2048]{2,1,0:T(8,128)(2,1)S(1)}, bf16[4,96,2048]{2,1,0:T(8,128)(2,1)}, u32[]{:S(2)}) copy-start(bf16[4,96,2048]{2,1,0:T(8,128)(2,1)} %all-gather.11.cloned.1.call-done) | copy-start | bytes 4718596
  316.1 15.6 %collective-permute-start.14 = (bf16[8,96,2048]{2,1,0:T(8,128)(2,1)}, bf16[8,96,2048]{2,1,0:T(8,128)(2,1)}, u32[]{:S(2)}, u32[]{:S(2)}) collective-permute-start(bf16[8,96,2048]{2,1,0:T(8,128)(2,1)} %bitcast.37.do_ref), channel_id=1, source_target_pairs={{0,1},{1,0},{2,3},{3,2},{4,5},{5,4},{6,7},{7,6},{8,9},{9,8},{10,11... | collective-permute-start | bytes 9437192 | tf_op jit(solution)/shard_map/ppermute | solution.py:36
  326.7 6.0 collective-permute-start.12
  378.2 5.9 collective-permute-start.15
  426.1 10.5 %collective-permute-start.16 = (bf16[8,2,96,2048]{3,2,1,0:T(8,128)(2,1)}, bf16[8,2,96,2048]{3,2,1,0:T(8,128)(2,1)}, u32[]{:S(2)}, u32[]{:S(2)}) collective-permute-start(bf16[8,2,96,2048]{3,2,1,0:T(8,128)(2,1)} %bitcast.264), channel_id=1, source_target_pairs={{0,1},{1,0},{2,3},{3,2},{4,5},{5,4},{6,7},{7,6},{8,9},{9,8},{10,11... | collective-permute-start | bytes 18874376 | tf_op jit(solution)/shard_map/ppermute | solution.py:36
  426.1 155.9 %reduce-scatter.5.cloned.1.call-start = ((), (), s32[]{:S(2)}) async-start(), calls=%async_computation.10 | async-start | bytes 3538944 | tf_op jit(solution)/shard_map/reduce_scatter | solution.py:512
  480.7 13.5 %collective-permute-start.17 = (bf16[8,96,2048]{2,1,0:T(8,128)(2,1)}, bf16[8,96,2048]{2,1,0:T(8,128)(2,1)}, u32[]{:S(2)}, u32[]{:S(2)}) collective-permute-start(bf16[8,96,2048]{2,1,0:T(8,128)(2,1)} %get-tuple-element.110), channel_id=1, source_target_pairs={{0,1},{1,0},{2,3},{3,2},{4,5},{5,4},{6,7},{7,6},{8,9},{9,8},{10,11... | collective-permute-start | bytes 9437192 | tf_op jit(solution)/shard_map/ppermute | solution.py:36
  482.4 22.6 %copy-start.40 = (f32[96]{0:T(128)}, f32[96]{0:T(128)S(1)}, u32[]{:S(2)}) copy-start(f32[96]{0:T(128)S(1)} %get-tuple-element.267) | copy-start | bytes 1156
  500.4 201.5 %reduce-scatter.9.cloned.1.call-start = ((), (), s32[]{:S(2)}) async-start(), calls=%async_computation.12 | async-start | bytes 7077888 | tf_op jit(solution)/shard_map/reduce_scatter | solution.py:554
  505.5 16.8 %slice-start = ((s8[7340032]{0:T(1024)(128)(4,1)}), s8[4194304]{0:T(1024)(128)(4,1)S(1)}, s32[]{:S(2)}) async-start(s8[7340032]{0:T(1024)(128)(4,1)} %bitcast.271), calls=%async_computation.15 | async-start | bytes 8388608
  506.9 27.4 %collective-permute-start.19 = (bf16[96,2048]{1,0:T(8,128)(2,1)S(1)}, bf16[96,2048]{1,0:T(8,128)(2,1)S(1)}, u32[]{:S(2)}, u32[]{:S(2)}) collective-permute-start(bf16[96,2048]{1,0:T(8,128)(2,1)S(1)} %fusion.73), channel_id=1, source_target_pairs={{0,2},{1,3},{2,0},{3,1},{4,6},{5,7},{6,4},{7,5},{8,10},{9,11},{10,... | collective-permute-start | bytes 1179656 | tf_op jit(solution)/shard_map/ppermute | solution.py:40
  508.5 38.5 %collective-permute-start.18 = (bf16[96,2048]{1,0:T(8,128)(2,1)S(1)}, bf16[96,2048]{1,0:T(8,128)(2,1)S(1)}, u32[]{:S(2)}, u32[]{:S(2)}) collective-permute-start(bf16[96,2048]{1,0:T(8,128)(2,1)S(1)} %fusion.73), channel_id=1, source_target_pairs={{0,1},{1,0},{2,3},{3,2},{4,5},{5,4},{6,7},{7,6},{8,9},{9,8},{10,11... | collective-permute-start | bytes 1179656 | tf_op jit(solution)/shard_map/ppermute | solution.py:36
  508.5 39.8 %collective-permute-start.21 = (bf16[8,96,2048]{2,1,0:T(8,128)(2,1)S(1)}, bf16[8,96,2048]{2,1,0:T(8,128)(2,1)S(1)}, u32[]{:S(2)}, u32[]{:S(2)}) collective-permute-start(bf16[8,96,2048]{2,1,0:T(8,128)(2,1)S(1)} %copy-done.54), channel_id=1, source_target_pairs={{0,1},{1,0},{2,3},{3,2},{4,5},{5,4},{6,7},{7,6},{8,9},{9,8},{10,11... | collective-permute-start | bytes 9437192 | tf_op jit(solution)/shard_map/ppermute | solution.py:36
  509.0 41.9 %collective-permute-start.22 = (bf16[8,96,2048]{2,1,0:T(8,128)(2,1)}, bf16[8,96,2048]{2,1,0:T(8,128)(2,1)S(1)}, u32[]{:S(2)}, u32[]{:S(2)}) collective-permute-start(bf16[8,96,2048]{2,1,0:T(8,128)(2,1)} %get-tuple-element.131), channel_id=1, source_target_pairs={{0,1},{1,0},{2,3},{3,2},{4,5},{5,4},{6,7},{7,6},{8,9},{9,8},{10,11... | collective-permute-start | bytes 9437192 | tf_op jit(solution)/shard_map/ppermute | solution.py:36
  509.0 13.4 %slice-start.1 = ((s8[7340032]{0:T(1024)(128)(4,1)}), s8[3145728]{0:T(1024)(128)(4,1)S(1)}, s32[]{:S(2)}) async-start(s8[7340032]{0:T(1024)(128)(4,1)} %bitcast.271), calls=%async_computation.16 | async-start | bytes 6291456
  509.0 13.4 %copy-start.55 = (bf16[8,112,1024]{2,1,0:T(8,128)(2,1)S(1)}, bf16[8,112,1024]{2,1,0:T(8,128)(2,1)}, u32[]{:S(2)}) copy-start(bf16[8,112,1024]{2,1,0:T(8,128)(2,1)} %get-tuple-element.121) | copy-start | bytes 5505028
  522.4 12.5 %copy-start.13 = (bf16[1792,1024]{1,0:T(8,128)(2,1)S(1)}, bf16[1792,1024]{1,0:T(8,128)(2,1)}, u32[]{:S(2)}) copy-start(bf16[1792,1024]{1,0:T(8,128)(2,1)} %pad_maximum_fusion.6) | copy-start | bytes 11010052
  534.3 12.7 %collective-permute-start.20 = (bf16[96,2048]{1,0:T(8,128)(2,1)S(1)}, bf16[96,2048]{1,0:T(8,128)(2,1)S(1)}, u32[]{:S(2)}, u32[]{:S(2)}) collective-permute-start(bf16[96,2048]{1,0:T(8,128)(2,1)S(1)} %collective-permute-done.19), channel_id=1, source_target_pairs={{0,1},{1,0},{2,3},{3,2},{4,5},{5,4},{6,7},{7,6},{8,9},{9,8},{10,11... | collective-permute-start | bytes 1179656 | tf_op jit(solution)/shard_map/ppermute | solution.py:36
  582.1 298.0 %reduce-scatter.11.cloned.1.call-start = ((), (), s32[]{:S(2)}) async-start(), calls=%async_computation.13 | async-start | bytes 10027008 | tf_op jit(solution)/shard_map/reduce_scatter | solution.py:578
  586.0 11.4 %collective-permute-start.24 = (bf16[96,2048]{1,0:T(8,128)(2,1)S(1)}, bf16[96,2048]{1,0:T(8,128)(2,1)S(1)}, u32[]{:S(2)}, u32[]{:S(2)}) collective-permute-start(bf16[96,2048]{1,0:T(8,128)(2,1)S(1)} %get-tuple-element.210), channel_id=1, source_target_pairs={{0,2},{1,3},{2,0},{3,1},{4,6},{5,7},{6,4},{7,5},{8,10},{9,11},{10,... | collective-permute-start | bytes 1179656 | tf_op jit(solution)/shard_map/ppermute | solution.py:40
  587.2 10.1 %collective-permute-start.23 = (bf16[96,2048]{1,0:T(8,128)(2,1)S(1)}, bf16[96,2048]{1,0:T(8,128)(2,1)S(1)}, u32[]{:S(2)}, u32[]{:S(2)}) collective-permute-start(bf16[96,2048]{1,0:T(8,128)(2,1)S(1)} %get-tuple-element.210), channel_id=1, source_target_pairs={{0,1},{1,0},{2,3},{3,2},{4,5},{5,4},{6,7},{7,6},{8,9},{9,8},{10,11... | collective-permute-start | bytes 1179656 | tf_op jit(solution)/shard_map/ppermute | solution.py:36
  597.3 1.7 collective-permute-start.25
  600.3 17.1 %copy-start.52 = (f32[1,512]{1,0:T(1,128)S(1)}, f32[1,512]{1,0:T(1,128)}, u32[]{:S(2)}) copy-start(f32[1,512]{1,0:T(1,128)} %get-tuple-element.150) | copy-start | bytes 6148
  600.3 17.8 %copy-start.51 = (f32[1,512]{1,0:T(1,128)S(1)}, f32[1,512]{1,0:T(1,128)}, u32[]{:S(2)}) copy-start(f32[1,512]{1,0:T(1,128)} %get-tuple-element.148) | copy-start | bytes 6148
  708.0 7.0 collective-permute-start.26
  709.1 25.9 %slice-start.6 = ((s8[8388608]{0:T(1024)(128)(4,1)}), s8[4194304]{0:T(1024)(128)(4,1)S(1)}, s32[]{:S(2)}) async-start(s8[8388608]{0:T(1024)(128)(4,1)} %bitcast.286), calls=%async_computation.21 | async-start | bytes 8388608
  709.1 28.8 %slice-start.4 = ((s8[8388608]{0:T(1024)(128)(4,1)}), s8[4194304]{0:T(1024)(128)(4,1)S(1)}, s32[]{:S(2)}) async-start(s8[8388608]{0:T(1024)(128)(4,1)} %bitcast.282), calls=%async_computation.19 | async-start | bytes 8388608
  714.3 20.7 %slice-start.7 = ((s8[8388608]{0:T(1024)(128)(4,1)}), s8[4194304]{0:T(1024)(128)(4,1)S(1)}, s32[]{:S(2)}) async-start(s8[8388608]{0:T(1024)(128)(4,1)} %bitcast.286), calls=%async_computation.22 | async-start | bytes 8388608
  714.4 2.4 collective-permute-start.28
  715.0 23.0 %slice-start.5 = ((s8[8388608]{0:T(1024)(128)(4,1)}), s8[4194304]{0:T(1024)(128)(4,1)S(1)}, s32[]{:S(2)}) async-start(s8[8388608]{0:T(1024)(128)(4,1)} %bitcast.282), calls=%async_computation.20 | async-start | bytes 8388608
  715.2 12.1 %collective-permute-start.27 = (bf16[96,2048]{1,0:T(8,128)(2,1)S(1)}, bf16[96,2048]{1,0:T(8,128)(2,1)S(1)}, u32[]{:S(2)}, u32[]{:S(2)}) collective-permute-start(bf16[96,2048]{1,0:T(8,128)(2,1)S(1)} %fusion.49), channel_id=1, source_target_pairs={{0,2},{1,3},{2,0},{3,1},{4,6},{5,7},{6,4},{7,5},{8,10},{9,11},{10,... | collective-permute-start | bytes 1179656 | tf_op jit(solution)/shard_map/ppermute | solution.py:40
  717.0 21.9 %slice-start.2 = ((s8[8388608]{0:T(1024)(128)(4,1)}), s8[4194304]{0:T(1024)(128)(4,1)S(1)}, s32[]{:S(2)}) async-start(s8[8388608]{0:T(1024)(128)(4,1)} %bitcast.278), calls=%async_computation.17 | async-start | bytes 8388608
  717.1 17.8 %collective-permute-start.29 = (bf16[96,2048]{1,0:T(8,128)(2,1)S(1)}, bf16[96,2048]{1,0:T(8,128)(2,1)S(1)}, u32[]{:S(2)}, u32[]{:S(2)}) collective-permute-start(bf16[96,2048]{1,0:T(8,128)(2,1)S(1)} %fusion.44), channel_id=1, source_target_pairs={{0,2},{1,3},{2,0},{3,1},{4,6},{5,7},{6,4},{7,5},{8,10},{9,11},{10,... | collective-permute-start | bytes 1179656 | tf_op jit(solution)/shard_map/ppermute | solution.py:40
  735.3 48.7 %collective-permute-start.35 = (bf16[2,256,2048]{2,1,0:T(8,128)(2,1)S(1)}, bf16[2,256,2048]{2,1,0:T(8,128)(2,1)}, u32[]{:S(2)}, u32[]{:S(2)}) collective-permute-start(bf16[2,256,2048]{2,1,0:T(8,128)(2,1)S(1)} %dynamic-slice_convert_fusion), channel_id=1, source_target_pairs={{0,2},{1,3},{2,0},{3,1},{4,6},{5,7},{6,4},{7,5},{8,10},{9,11},{10,... | collective-permute-start | bytes 6291464 | tf_op jit(solution)/shard_map/ppermute | solution.py:40
  738.3 90.7 %collective-permute-start.31 = (bf16[2,512,1024]{2,1,0:T(8,128)(2,1)S(1)}, bf16[2,512,1024]{2,1,0:T(8,128)(2,1)}, u32[]{:S(2)}, u32[]{:S(2)}) collective-permute-start(bf16[2,512,1024]{2,1,0:T(8,128)(2,1)S(1)} %dynamic-slice_convert_fusion.2), channel_id=1, source_target_pairs={{0,2},{1,3},{2,0},{3,1},{4,6},{5,7},{6,4},{7,5},{8,10},{9,11},{10,... | collective-permute-start | bytes 6291464 | tf_op jit(solution)/shard_map/ppermute | solution.py:40
  740.6 131.7 %collective-permute-start.33 = (bf16[2,512,1024]{2,1,0:T(8,128)(2,1)}, bf16[2,512,1024]{2,1,0:T(8,128)(2,1)}, u32[]{:S(2)}, u32[]{:S(2)}) collective-permute-start(bf16[2,512,1024]{2,1,0:T(8,128)(2,1)} %dynamic-slice_convert_fusion.1), channel_id=1, source_target_pairs={{0,2},{1,3},{2,0},{3,1},{4,6},{5,7},{6,4},{7,5},{8,10},{9,11},{10,... | collective-permute-start | bytes 6291464 | tf_op jit(solution)/shard_map/ppermute | solution.py:40
  790.1 88.4 %collective-permute-start.36 = (bf16[1,256,2048]{2,1,0:T(8,128)(2,1)S(1)}, bf16[1,256,2048]{2,1,0:T(8,128)(2,1)S(1)}, u32[]{:S(2)}, u32[]{:S(2)}) collective-permute-start(bf16[1,256,2048]{2,1,0:T(8,128)(2,1)S(1)} %dynamic-slice_convert_fusion.3), channel_id=1, source_target_pairs={{0,1},{1,0},{2,3},{3,2},{4,5},{5,4},{6,7},{7,6},{8,9},{9,8},{10,11... | collective-permute-start | bytes 3145736 | tf_op jit(solution)/shard_map/ppermute | solution.py:36
  831.6 45.0 %copy-start.10 = (f32[2,512,1024]{2,1,0:T(8,128)}, f32[2,512,1024]{2,1,0:T(8,128)S(1)}, u32[]{:S(2)}) copy-start(f32[2,512,1024]{2,1,0:T(8,128)S(1)} %convert_add_fusion.2) | copy-start | bytes 12582916
  832.9 53.4 %collective-permute-start.32 = (bf16[1,512,1024]{2,1,0:T(8,128)(2,1)}, bf16[1,512,1024]{2,1,0:T(8,128)(2,1)}, u32[]{:S(2)}, u32[]{:S(2)}) collective-permute-start(bf16[1,512,1024]{2,1,0:T(8,128)(2,1)} %dynamic-slice_convert_fusion.5), channel_id=1, source_target_pairs={{0,1},{1,0},{2,3},{3,2},{4,5},{5,4},{6,7},{7,6},{8,9},{9,8},{10,11... | collective-permute-start | bytes 3145736 | tf_op jit(solution)/shard_map/ppermute | solution.py:36
  878.4 13.3 %collective-permute-start.34 = (bf16[1,512,1024]{2,1,0:T(8,128)(2,1)S(1)}, bf16[1,512,1024]{2,1,0:T(8,128)(2,1)}, u32[]{:S(2)}, u32[]{:S(2)}) collective-permute-start(bf16[1,512,1024]{2,1,0:T(8,128)(2,1)S(1)} %dynamic-slice_convert_fusion.4), channel_id=1, source_target_pairs={{0,1},{1,0},{2,3},{3,2},{4,5},{5,4},{6,7},{7,6},{8,9},{9,8},{10,11... | collective-permute-start | bytes 3145736 | tf_op jit(solution)/shard_map/ppermute | solution.py:36
  882.8 24.6 %all-to-all-start.1 = ((bf16[4,64,1664]{2,1,0:T(8,128)(2,1)}), bf16[4,64,1664]{2,1,0:T(8,128)(2,1)S(1)}, u32[]{:S(2)}, u32[]{:S(2)}) async-start(bf16[4,64,1664]{2,1,0:T(8,128)(2,1)} %pad_maximum_fusion.12), calls=%async_computation.5 | async-start | bytes 1703936 | tf_op jit(solution)/shard_map/all_to_all | solution.py:600
  889.1 17.4 %collective-permute-start.30 = (bf16[64,2048]{1,0:T(8,128)(2,1)S(1)}, bf16[64,2048]{1,0:T(8,128)(2,1)S(1)}, u32[]{:S(2)}, u32[]{:S(2)}) collective-permute-start(bf16[64,2048]{1,0:T(8,128)(2,1)S(1)} %bitcast.322), channel_id=1, source_target_pairs={{0,0},{4,1},{8,2},{12,3},{16,4},{20,5},{24,6},{28,7},{1,8},{5,9},{... | collective-permute-start | bytes 786440 | tf_op jit(solution)/shard_map/ppermute | solution.py:598
  (47 other events, 151.6 us)
Sparse Core Ops, SparseCore 0:
  13.1 38.2 all-gather.10
  53.8 116.2 all-gather.12
  172.2 47.1 all-gather.14
  250.6 76.0 all-gather.16
  328.8 97.2 all-gather.18
  429.5 73.5 reduce-scatter.6
  507.3 73.7 reduce-scatter.4
  584.6 117.1 reduce-scatter.8
  705.5 154.4 reduce-scatter.10

commit v3 on v2

--- a/solution.py
+++ b/solution.py
@@ -432,7 +432,7 @@
     front, gate_w, up_w, w_o_block, x_all, x_scale, cosine, sine = tie(
         front, gate_w, up_w, w_o_block, x_all, x_scale, cosine, sine
     )
-    do_got, _ = tie(do_got, front)
+    do_got, more_own, _ = tie(do_got, cotangent[1], front)
     do_other = swap_low(do_got)
     w_o = lax.all_gather(w_o_block, "expert", axis=0, tiled=True)
     w_qkv = front[:, : 3 * cols]
@@ -488,8 +488,10 @@
     do_first = jnp.stack(
         [jnp.where(low == 0, do_got, do_other), jnp.where(low == 0, do_other, do_got)], axis=1
     ).reshape(owners, tok, width)
+    more = lax.all_gather(more_own, "expert", axis=0, axis_index_groups=low_groups())
+    b_own, more = tie(b_own, more)
     b_first = gather_expert(b_own[0][None])
-    second = gather_expert(jnp.stack([b_own[1], cotangent[1]])[None])
+    second = gather_expert(b_own[1][None])
     b_first, down_w = tie(b_first, down_w)
     out_parts = []
     db_list = []
@@ -501,9 +503,12 @@
         if m == 0:
             values = (b_first, swap_core(b_first), do_first, swap_core(do_first))
         else:
-            second, _ = tie(second, db_half)
-            near = swap_core(second)
-            values = ((second, 0), (near, 0), (second, 1), (near, 1))
+            second, more, _ = tie(second, more, db_half)
+            more_other = swap_low(more)
+            do_second = jnp.stack(
+                [jnp.where(low == 0, more, more_other), jnp.where(low == 0, more_other, more)], axis=1
+            ).reshape(owners, tok, width)
+            values = (second, swap_core(second), do_second, swap_core(do_second))
         *saved, out_mine, out_near, db_mine, db_near, part = expert_step(
             slot[m], *values, gate_w, up_w, down_w, router_t, is_mine, pack
         )

time: 926 us -> 939 us (1.014)
  waiting for transfers between devices: 438 us -> 452 us
    ppermute x1 -> x2, waiting for transfers between devices: 4.38 us -> 42.4 us  [swap_low(): return lax.ppermute(values, 'expert', [(e, e ^ 1) for e in range(count)])]
    all_gather x2, waiting for transfers between devices: 47.5 us -> 10 us  [gather_expert(): return lax.all_gather(own, 'expert', axis=0, tiled=True)]
    all_gather x1, waiting for transfers between devices: 7.6 us -> 17.6 us  [local(): lax.all_gather(cotangent[0], 'expert', axis=0, axis_index_groups=low_grou...]
    ppermute x22 -> x23, waiting for transfers between devices: 22.6 us -> 18.4 us  [swap_core(): return lax.ppermute(values, 'shard', [(s, s ^ 1) for s in range(4)])]
    unnamed x144 -> x156, local copies, waits for them, and re-layouts: 25.9 us -> 26.8 us
  transfers between devices with their start and end apart: 47 -> 50, of which waited for: 25 -> 26; matrix products, arithmetic and copies ran while one was open for 25% -> 24% of each run, Pallas kernels for 15% -> 15%
where the time goes in v3:
time: 939 us; the launch traced here: 930 us
  waiting for transfers between devices  452 us (48%)
  Pallas kernels  142 us (15%)
  other arithmetic  104 us (11%)
  local copies, waits for them, and re-layouts  78.8 us (8%)
  matrix products  74.4 us (8%)
  blocking collectives  33 us (4%)
  starting transfers between devices  30.1 us (3%)
  between operations  15.9 us (2%)
    ppermute x12, waiting for transfers between devices, swap_side(): return lax.ppermute(values, 'shard', [(s, s ^ 2) for s in range(4)])  282 us
    pallas_call x2, Pallas kernels, expert_step(): pl.pallas_call(expert_body, grid=(owners // group,), in_specs=[pl.BlockSp...  89.7 us
    dot_general x12, matrix products, dot(): lax.dot_general(left, right, (dims, ((), ())), preferred_element_type=f32)  74.3 us
    reduce_scatter x1, waiting for transfers between devices, local(): lax.psum_scatter(out_part, 'expert', scatter_dimension=0, tiled=True)[0]  46.5 us
    ppermute x2, waiting for transfers between devices, swap_low(): return lax.ppermute(values, 'expert', [(e, e ^ 1) for e in range(count)])  42.4 us
    pallas_call x2, Pallas kernels, attend_back(): pl.pallas_call(attend_back_body, grid=(heads,), in_specs=[pl.BlockSpec((l...  34 us
    unnamed x156, local copies, waits for them, and re-layouts  26.8 us
  transfers between devices with their start and end apart: 50, of which 26 were waited for; matrix products, arithmetic and copies ran while one was open for 24% of the time, Pallas kernels for 15%

profile of v3, /device:TPU:2, one launch (start us, length us, event | category | flops | bytes accessed | tf_op | source)
XLA Modules:
  0.0 930.4 jit_solution(5591657582950191757)
XLA Ops:
  18.5 15.5 %all_to_all.10 = bf16[4,64,1664]{2,1,0:T(8,128)(2,1)} all-to-all(bf16[4,64,1664]{2,1,0:T(8,128)(2,1)S(1)} %copy.162), channel_id=1, replica_groups=mesh['expert'=8,'shard'=4] {'shard'}, dimensions={0} | all-to-all | bytes 1703936 | tf_op jit(solution)/shard_map/all_to_all | solution.py:409
  33.9 17.6 %all-gather.12.cloned.1.call-done = bf16[4,96,2048]{2,1,0:T(8,128)(2,1)} async-done(((bf16[1,96,2048]{2,1,0:T(8,128)(2,1)}), bf16[4,96,2048]{2,1,0:T(8,128)(2,1)}) %all-gather.12.cloned.1.call-update) | async-done | bytes 1572880 | tf_op jit(solution)/shard_map/all_gather | solution.py:410
  55.4 3.2 collective-permute-start.4
  63.5 3.0 fusion.78
  82.1 4.6 pad_maximum_fusion.4
  86.7 2.5 pad_maximum_fusion.3
  90.8 33.4 %collective-permute-done.3 = bf16[2,512,1024]{2,1,0:T(8,128)(2,1)} collective-permute-done((bf16[2,512,1024]{2,1,0:T(8,128)(2,1)}, bf16[2,512,1024]{2,1,0:T(8,128)(2,1)}, u32[]{:S(2)}, u32[]{:S(2)}) %collective-permute-start.3) | collective-permute-done | bytes 2097184 | tf_op jit(solution)/shard_map/ppermute | solution.py:40
  124.3 3.1 constant_dynamic-update-slice_fusion.15
  127.4 41.2 %collective-permute-done.1 = bf16[2,512,1024]{2,1,0:T(8,128)(2,1)} collective-permute-done((bf16[2,512,1024]{2,1,0:T(8,128)(2,1)S(1)}, bf16[2,512,1024]{2,1,0:T(8,128)(2,1)}, u32[]{:S(2)}, u32[]{:S(2)}) %collective-permute-start.1) | collective-permute-done | bytes 2097184 | tf_op jit(solution)/shard_map/ppermute | solution.py:40
  168.6 3.1 constant_dynamic-update-slice_fusion.17
  173.5 8.2 fusion.8.q_ref.k_ref.v_ref
  184.5 6.1 all_gather.38
  194.0 11.0 %shard_map.263 = (bf16[768,512]{1,0:T(8,128)(2,1)}, bf16[768,512]{1,0:T(8,128)(2,1)}, bf16[768,512]{1,0:T(8,128)(2,1)}, bf16[768,512]{1,0:T(8,128)(2,1)}, f32[8,384,1]{2,1,0:T(8,128)}) custom-call(f32[768,1536]{1,0:T(8,128)} %copy-done, f32[768,1536]{1,0:T(8,128)} %copy-done, f32[768,1536]{1,0:T(8,128)} %copy-done, f32[768,1]{1,0:T(8,128)} %copy.164.qi_ref, ...), custom_call_target="tpu_custom_call" | custom-call | tf_op jit(solution)/shard_map/pallas_call | solution.py:116
  205.0 14.6 %all-gather.16.cloned.1.call-done.wo_ref = bf16[512,2048]{1,0:T(8,128)(2,1)} async-done(((bf16[64,2048]{1,0:T(8,128)(2,1)}), bf16[512,2048]{1,0:T(8,128)(2,1)}) %all-gather.16.cloned.1.call-update) | async-done | bytes 2097168 | tf_op jit(solution)/shard_map/all_gather | solution.py:437
  219.7 3.6 fusion.86
  226.0 3.5 collective-permute-done.8
  234.4 18.2 %collective-permute-done.9 = bf16[2,96,2048]{2,1,0:T(8,128)(2,1)S(1)} collective-permute-done((bf16[2,96,2048]{2,1,0:T(8,128)(2,1)S(1)}, bf16[2,96,2048]{2,1,0:T(8,128)(2,1)S(1)}, u32[]{:S(2)}, u32[]{:S(2)}) %collective-permute-start.9) | collective-permute-done | bytes 786464 | tf_op jit(solution)/shard_map/ppermute | solution.py:40
  252.6 2.5 multiply_reduce_fusion.2
  257.5 5.2 all-gather.22.cloned.1.call-done
  266.2 2.6 collective-permute-done.10
  271.9 2.8 pad_maximum_fusion.5
  274.7 43.2 %collective-permute-done.11 = bf16[2,256,2048]{2,1,0:T(8,128)(2,1)} collective-permute-done((bf16[2,256,2048]{2,1,0:T(8,128)(2,1)}, bf16[2,256,2048]{2,1,0:T(8,128)(2,1)}, u32[]{:S(2)}, u32[]{:S(2)}) %collective-permute-start.11) | collective-permute-done | bytes 2097184 | tf_op jit(solution)/shard_map/ppermute | solution.py:40
  319.8 6.4 collective-permute-done.13
  330.2 10.0 %all-gather.20.cloned.1.call-done.bo_ref = bf16[8,96,2048]{2,1,0:T(8,128)(2,1)} async-done(((bf16[1,96,2048]{2,1,0:T(8,128)(2,1)}), bf16[8,96,2048]{2,1,0:T(8,128)(2,1)}) %all-gather.20.cloned.1.call-update) | async-done | bytes 3145744 | tf_op jit(solution)/shard_map/all_gather | solution.py:484
  346.2 45.1 %shard_map.264 = (bf16[8,112,2048]{2,1,0:T(8,128)(2,1)}, bf16[8,112,1024]{2,1,0:T(8,128)(2,1)}, bf16[8,112,2048]{2,1,0:T(8,128)(2,1)}, bf16[8,112,1024]{2,1,0:T(...) custom-call(s32[8,1,192]{2,1,0:T(1,128)} %get-tuple-element.247.slot, ...), custom_call_target="tpu_custom_call" | custom-call | tf_op jit(solution)/shard_map/pallas_call | solution.py:322
  391.5 5.7 collective-permute-done.15
  397.3 5.0 add_convert_fusion.3
  402.8 36.1 %collective-permute-done.17 = bf16[4,96,2048]{2,1,0:T(8,128)(2,1)S(1)} collective-permute-done((bf16[4,96,2048]{2,1,0:T(8,128)(2,1)}, bf16[4,96,2048]{2,1,0:T(8,128)(2,1)S(1)}, u32[]{:S(2)}, u32[]{:S(2)}) %collective-permute-start.17) | collective-permute-done | bytes 1572896 | tf_op jit(solution)/shard_map/ppermute | solution.py:66
  443.3 5.7 collective-permute-done.18.dn_ref
  449.1 44.6 %shard_map.265 = (bf16[8,112,2048]{2,1,0:T(8,128)(2,1)}, bf16[8,112,1024]{2,1,0:T(8,128)(2,1)}, bf16[8,112,2048]{2,1,0:T(8,128)(2,1)}, bf16[8,112,1024]{2,1,0:T(...) custom-call(s32[8,1,192]{2,1,0:T(1,128)} %get-tuple-element.248.slot, ...), custom_call_target="tpu_custom_call" | custom-call | tf_op jit(solution)/shard_map/pallas_call | solution.py:322
  495.4 4.3 pad_maximum_fusion.6
  499.7 7.6 pad_maximum_fusion.1
  507.2 6.1 add_convert_fusion.2
  513.7 2.5 reduce-scatter.7.cloned.1.call-done
  522.1 13.3 %fusion.14 = f32[2048,1024]{1,0:T(8,128)} fusion(bf16[1792,2048]{1,0:T(8,128)(2,1)} %pad_maximum_fusion.1, bf16[896,1024]{1,0:T(8,128)(2,1)} %bitcast.354, bf16[896,1024]{1,0:T(8,128)(2,1)} %bitcast.352), kind=kOutput, calls=%fused_computation.34 | convolution fusion | flops 7523532800 | bytes 19398656 | tf_op jit(solution)/shard_map/dot_general | solution.py:20
  535.5 11.9 %fusion.10 = f32[2048,1024]{1,0:T(8,128)} fusion(bf16[1792,2048]{1,0:T(8,128)(2,1)S(1)} %bitcast.275, bf16[896,1024]{1,0:T(8,128)(2,1)} %bitcast.353, bf16[896,1024]{1,0:T(8,128)(2,1)S(1)} %bitcast.351), kind=kOutput, calls=%fused_computation.30 | convolution fusion | flops 7523532800 | bytes 19398656 | tf_op jit(solution)/shard_map/dot_general | solution.py:20
  547.9 12.2 %fusion = f32[1024,2048]{1,0:T(8,128)} fusion(bf16[1792,1024]{1,0:T(8,128)(2,1)S(1)} %copy-done.14, bf16[896,2048]{1,0:T(8,128)(2,1)} %bitcast.350, bf16[896,2048]{1,0:T(8,128)(2,1)S(1)} %bitcast.349), kind=kOutput, calls=%fused_computation.3 | convolution fusion | flops 7530872832 | bytes 19398656 | tf_op jit(solution)/shard_map/dot_general | solution.py:20
  565.4 3.3 pad_maximum_fusion.2
  568.7 16.9 %shard_map.266 = (f32[384,512]{1,0:T(8,128)}, f32[384,512]{1,0:T(8,128)}, bf16[384,512]{1,0:T(8,128)(2,1)}, f32[1,512]{1,0:T(1,128)}, f32[1,512]{1,0:T(1,128)}, /*index=5*/f32[2,384]{1,0:T(2,128)}) custom-call(bf16[384,2048]{1,0:T(8,128)(2,1)} %pad_maximum_fusion.11.dh_ref, bf16[512,2048]{1,0:T(8,128)(2,1)} %all-gather.16.cloned.1.call-done.wo_ref, ...), custom_call_target="tpu_custom_call" | custom-call | tf_op jit(solution)/shard_map/pallas_call | solution.py:180
  585.6 5.8 all-gather.3.sum_ref
  591.5 3.7 shard_map.267
  600.6 10.0 %collective-permute-done.26 = bf16[96,2048]{1,0:T(8,128)(2,1)S(1)} collective-permute-done((bf16[96,2048]{1,0:T(8,128)(2,1)S(1)}, bf16[96,2048]{1,0:T(8,128)(2,1)S(1)}, u32[]{:S(2)}, u32[]{:S(2)}) %collective-permute-start.26) | collective-permute-done | bytes 393248 | tf_op jit(solution)/shard_map/ppermute | solution.py:40
  613.5 17.1 %shard_map.268 = (f32[384,512]{1,0:T(8,128)}, f32[384,512]{1,0:T(8,128)}, bf16[384,512]{1,0:T(8,128)(2,1)}, f32[1,512]{1,0:T(1,128)}, f32[1,512]{1,0:T(1,128)}, /*index=5*/f32[2,384]{1,0:T(2,128)}) custom-call(bf16[384,2048]{1,0:T(8,128)(2,1)} %pad_maximum_fusion.12.dh_ref, bf16[512,2048]{1,0:T(8,128)(2,1)} %all-gather.16.cloned.1.call-done.wo_ref, ...), custom_call_target="tpu_custom_call" | custom-call | tf_op jit(solution)/shard_map/pallas_call | solution.py:180
  642.5 3.9 copy.189
  646.4 5.6 all-gather.4.sum_ref
  652.0 3.8 shard_map.269
  655.9 7.9 convolution_convert_fusion
  663.9 4.2 pad_maximum_fusion
  668.1 46.5 %reduce-scatter.9.cloned.1.call-done = bf16[1,2,96,2048]{3,2,1,0:T(8,128)(2,1)} async-done(((bf16[8,2,96,2048]{3,2,1,0:T(8,128)(2,1)}), bf16[1,2,96,2048]{3,2,1,0:T(8,128)(2,1)}) %reduce-scatter.9.cloned.1.call-update) | async-done | bytes 786448 | tf_op jit(solution)/shard_map/reduce_scatter | solution.py:559
  715.9 4.7 fusion.85
  721.9 5.2 fusion.84
  731.4 8.7 collective-permute-done.29
  740.2 7.4 collective-permute-done.31
  756.2 40.6 %collective-permute-done.37 = bf16[2,256,2048]{2,1,0:T(8,128)(2,1)} collective-permute-done((bf16[2,256,2048]{2,1,0:T(8,128)(2,1)S(1)}, bf16[2,256,2048]{2,1,0:T(8,128)(2,1)}, u32[]{:S(2)}, u32[]{:S(2)}) %collective-permute-start.37) | collective-permute-done | bytes 2097184 | tf_op jit(solution)/shard_map/ppermute | solution.py:40
  796.8 4.4 convert_add_fusion
  803.9 37.8 %collective-permute-done.33 = bf16[2,512,1024]{2,1,0:T(8,128)(2,1)} collective-permute-done((bf16[2,512,1024]{2,1,0:T(8,128)(2,1)S(1)}, bf16[2,512,1024]{2,1,0:T(8,128)(2,1)}, u32[]{:S(2)}, u32[]{:S(2)}) %collective-permute-start.33) | collective-permute-done | bytes 2097184 | tf_op jit(solution)/shard_map/ppermute | solution.py:40
  841.7 2.6 convert_add_fusion.2
  845.7 39.4 %collective-permute-done.35 = bf16[2,512,1024]{2,1,0:T(8,128)(2,1)} collective-permute-done((bf16[2,512,1024]{2,1,0:T(8,128)(2,1)}, bf16[2,512,1024]{2,1,0:T(8,128)(2,1)}, u32[]{:S(2)}, u32[]{:S(2)}) %collective-permute-start.35) | collective-permute-done | bytes 2097184 | tf_op jit(solution)/shard_map/ppermute | solution.py:40
  885.0 4.4 convert_add_fusion.1
  895.6 3.5 all-to-all-start.1
  899.1 2.8 convert_dynamic-update-slice_fusion.2
  901.9 2.5 collective-permute-start.32
  904.5 2.8 convert_dynamic-update-slice_fusion.1
  907.3 12.1 %collective-permute-done.32 = bf16[64,2048]{1,0:T(8,128)(2,1)S(1)} collective-permute-done((bf16[64,2048]{1,0:T(8,128)(2,1)S(1)}, bf16[64,2048]{1,0:T(8,128)(2,1)S(1)}, u32[]{:S(2)}, u32[]{:S(2)}) %collective-permute-start.32) | collective-permute-done | bytes 262176 | tf_op jit(solution)/shard_map/ppermute | solution.py:603
  (405 shorter events, 141.5 us)
Async XLA Ops:
  7.2 44.4 %all-gather.12.cloned.1.call-start = ((), (), s32[]{:S(2)}) async-start(), calls=%async_computation.6 | async-start | bytes 1966080 | tf_op jit(solution)/shard_map/all_gather | solution.py:410
  13.2 158.5 %all-gather.14.cloned.1.call-start = ((), (), s32[]{:S(2)}) async-start(), calls=%async_computation.7 | async-start | bytes 7667712 | tf_op jit(solution)/shard_map/all_gather | solution.py:412
  53.8 165.9 %all-gather.16.cloned.1.call-start = ((), (), s32[]{:S(2)}) async-start(), calls=%async_computation.8 | async-start | bytes 2359296 | tf_op jit(solution)/shard_map/all_gather | solution.py:437
  53.8 24.0 %collective-permute-start.5 = (bf16[2,96,2048]{2,1,0:T(8,128)(2,1)}, bf16[2,96,2048]{2,1,0:T(8,128)(2,1)}, u32[]{:S(2)}, u32[]{:S(2)}) collective-permute-start(bf16[2,96,2048]{2,1,0:T(8,128)(2,1)} %param.16), channel_id=1, source_target_pairs={{0,1},{1,0},{2,3},{3,2},{4,5},{5,4},{6,7},{7,6},{8,9},{9,8},{10,11... | collective-permute-start | bytes 2359304 | tf_op jit(solution)/shard_map/ppermute | solution.py:36
  53.9 23.9 %collective-permute-start.6 = (bf16[2,96,2048]{2,1,0:T(8,128)(2,1)}, bf16[2,96,2048]{2,1,0:T(8,128)(2,1)}, u32[]{:S(2)}, u32[]{:S(2)}) collective-permute-start(bf16[2,96,2048]{2,1,0:T(8,128)(2,1)} %param.16), channel_id=1, source_target_pairs={{0,2},{1,3},{2,0},{3,1},{4,6},{5,7},{6,4},{7,5},{8,10},{9,11},{10,... | collective-permute-start | bytes 2359304 | tf_op jit(solution)/shard_map/ppermute | solution.py:40
  55.4 116.2 %collective-permute-start.4 = (bf16[64,2048]{1,0:T(8,128)(2,1)}, bf16[64,2048]{1,0:T(8,128)(2,1)}, u32[]{:S(2)}, u32[]{:S(2)}) collective-permute-start(bf16[64,2048]{1,0:T(8,128)(2,1)} %param.23), channel_id=1, source_target_pairs={{0,0},{1,4},{2,8},{3,12},{4,16},{5,20},{6,24},{7,28},{8,1},{9,5},{... | collective-permute-start | bytes 786440 | tf_op jit(solution)/shard_map/ppermute | solution.py:419
  59.7 12.4 %collective-permute-start = (bf16[1,512,1024]{2,1,0:T(8,128)(2,1)}, bf16[1,512,1024]{2,1,0:T(8,128)(2,1)}, u32[]{:S(2)}, u32[]{:S(2)}) collective-permute-start(bf16[1,512,1024]{2,1,0:T(8,128)(2,1)} %constant_dynamic-slice_fusion.8), channel_id=1, source_target_pairs={{0,1},{1,0},{2,3},{3,2},{4,5},{5,4},{6,7},{7,6},{8,9},{9,8},{10,11... | collective-permute-start | bytes 3145736 | tf_op jit(solution)/shard_map/ppermute | solution.py:36
  62.2 4.5 collective-permute-start.2
  69.0 55.3 %collective-permute-start.3 = (bf16[2,512,1024]{2,1,0:T(8,128)(2,1)}, bf16[2,512,1024]{2,1,0:T(8,128)(2,1)}, u32[]{:S(2)}, u32[]{:S(2)}) collective-permute-start(bf16[2,512,1024]{2,1,0:T(8,128)(2,1)} %constant_dynamic-update-slice_fusion.16), channel_id=1, source_target_pairs={{0,2},{1,3},{2,0},{3,1},{4,6},{5,7},{6,4},{7,5},{8,10},{9,11},{10,... | collective-permute-start | bytes 6291464 | tf_op jit(solution)/shard_map/ppermute | solution.py:40
  73.4 95.2 %collective-permute-start.1 = (bf16[2,512,1024]{2,1,0:T(8,128)(2,1)S(1)}, bf16[2,512,1024]{2,1,0:T(8,128)(2,1)}, u32[]{:S(2)}, u32[]{:S(2)}) collective-permute-start(bf16[2,512,1024]{2,1,0:T(8,128)(2,1)S(1)} %constant_dynamic-update-slice_fusion.18), channel_id=1, source_target_pairs={{0,2},{1,3},{2,0},{3,1},{4,6},{5,7},{6,4},{7,5},{8,10},{9,11},{10,... | collective-permute-start | bytes 6291464 | tf_op jit(solution)/shard_map/ppermute | solution.py:40
  77.9 11.3 %collective-permute-start.7 = (bf16[2,96,2048]{2,1,0:T(8,128)(2,1)}, bf16[2,96,2048]{2,1,0:T(8,128)(2,1)S(1)}, u32[]{:S(2)}, u32[]{:S(2)}) collective-permute-start(bf16[2,96,2048]{2,1,0:T(8,128)(2,1)} %collective-permute-done.6), channel_id=1, source_target_pairs={{0,1},{1,0},{2,3},{3,2},{4,5},{5,4},{6,7},{7,6},{8,9},{9,8},{10,11... | collective-permute-start | bytes 2359304 | tf_op jit(solution)/shard_map/ppermute | solution.py:36
  90.1 37.3 %copy-start.13 = (bf16[2,384,2048]{2,1,0:T(8,128)(2,1)}, bf16[2,384,2048]{2,1,0:T(8,128)(2,1)S(1)}, u32[]{:S(2)}) copy-start(bf16[2,384,2048]{2,1,0:T(8,128)(2,1)S(1)} %constant_dynamic-update-slice_fusion) | copy-start | bytes 9437188
  171.7 91.0 %all-gather.22.cloned.1.call-start = ((), (), s32[]{:S(2)}) async-start(), calls=%async_computation.15 | async-start | bytes 1966080 | tf_op jit(solution)/shard_map/all_gather | solution.py:491
  225.9 3.5 collective-permute-start.8
  225.9 114.3 %all-gather.20.cloned.1.call-start = ((), (), s32[]{:S(2)}) async-start(), calls=%async_computation.10 | async-start | bytes 3538944 | tf_op jit(solution)/shard_map/all_gather | solution.py:484
  231.2 21.4 %copy-start.19 = (bf16[2,96,2048]{2,1,0:T(8,128)(2,1)S(1)}, bf16[2,96,2048]{2,1,0:T(8,128)(2,1)}, u32[]{:S(2)}) copy-start(bf16[2,96,2048]{2,1,0:T(8,128)(2,1)} %param.16) | copy-start | bytes 2359300
  233.0 19.6 %collective-permute-start.9 = (bf16[2,96,2048]{2,1,0:T(8,128)(2,1)S(1)}, bf16[2,96,2048]{2,1,0:T(8,128)(2,1)S(1)}, u32[]{:S(2)}, u32[]{:S(2)}) collective-permute-start(bf16[2,96,2048]{2,1,0:T(8,128)(2,1)S(1)} %fusion.24), channel_id=1, source_target_pairs={{0,2},{1,3},{2,0},{3,1},{4,6},{5,7},{6,4},{7,5},{8,10},{9,11},{10,... | collective-permute-start | bytes 2359304 | tf_op jit(solution)/shard_map/ppermute | solution.py:40
  264.8 137.5 %all-gather.18.cloned.1.call-start = ((), (), s32[]{:S(2)}) async-start(), calls=%async_computation.9 | async-start | bytes 3538944 | tf_op jit(solution)/shard_map/all_gather | solution.py:484
  266.1 2.7 collective-permute-start.10
  269.9 48.0 %collective-permute-start.11 = (bf16[2,256,2048]{2,1,0:T(8,128)(2,1)}, bf16[2,256,2048]{2,1,0:T(8,128)(2,1)}, u32[]{:S(2)}, u32[]{:S(2)}) collective-permute-start(bf16[2,256,2048]{2,1,0:T(8,128)(2,1)} %constant_dynamic-update-slice_fusion.14), channel_id=1, source_target_pairs={{0,2},{1,3},{2,0},{3,1},{4,6},{5,7},{6,4},{7,5},{8,10},{9,11},{10,... | collective-permute-start | bytes 6291464 | tf_op jit(solution)/shard_map/ppermute | solution.py:40
  271.4 54.8 %collective-permute-start.13 = (bf16[4,96,2048]{2,1,0:T(8,128)(2,1)}, bf16[4,96,2048]{2,1,0:T(8,128)(2,1)}, u32[]{:S(2)}, u32[]{:S(2)}) collective-permute-start(bf16[4,96,2048]{2,1,0:T(8,128)(2,1)} %all-gather.12.cloned.1.call-done), channel_id=1, source_target_pairs={{0,4},{4,0},{8,12},{12,8},{16,20},{20,16},{24,28},{28,24},{1,5},{5... | collective-permute-start | bytes 4718600 | tf_op jit(solution)/shard_map/ppermute | solution.py:66
  330.2 15.5 %collective-permute-start.14 = (bf16[8,96,2048]{2,1,0:T(8,128)(2,1)}, bf16[8,96,2048]{2,1,0:T(8,128)(2,1)}, u32[]{:S(2)}, u32[]{:S(2)}) collective-permute-start(bf16[8,96,2048]{2,1,0:T(8,128)(2,1)} %bitcast.38.do_ref), channel_id=1, source_target_pairs={{0,1},{1,0},{2,3},{3,2},{4,5},{5,4},{6,7},{7,6},{8,9},{9,8},{10,11... | collective-permute-start | bytes 9437192 | tf_op jit(solution)/shard_map/ppermute | solution.py:36
  340.2 6.0 collective-permute-start.12
  340.9 175.3 %reduce-scatter.7.cloned.1.call-start = ((), (), s32[]{:S(2)}) async-start(), calls=%async_computation.12 | async-start | bytes 3538944 | tf_op jit(solution)/shard_map/reduce_scatter | solution.py:517
  391.3 5.9 collective-permute-start.15
  402.2 36.6 %collective-permute-start.17 = (bf16[4,96,2048]{2,1,0:T(8,128)(2,1)}, bf16[4,96,2048]{2,1,0:T(8,128)(2,1)S(1)}, u32[]{:S(2)}, u32[]{:S(2)}) collective-permute-start(bf16[4,96,2048]{2,1,0:T(8,128)(2,1)} %bitcast.313), channel_id=1, source_target_pairs={{0,4},{4,0},{8,12},{12,8},{16,20},{20,16},{24,28},{28,24},{1,5},{5... | collective-permute-start | bytes 4718600 | tf_op jit(solution)/shard_map/ppermute | solution.py:66
  402.8 40.5 %collective-permute-start.16 = (bf16[8,96,2048]{2,1,0:T(8,128)(2,1)}, bf16[8,96,2048]{2,1,0:T(8,128)(2,1)}, u32[]{:S(2)}, u32[]{:S(2)}) collective-permute-start(bf16[8,96,2048]{2,1,0:T(8,128)(2,1)} %all-gather.18.cloned.1.call-done.bo_ref), channel_id=1, source_target_pairs={{0,1},{1,0},{2,3},{3,2},{4,5},{5,4},{6,7},{7,6},{8,9},{9,8},{10,11... | collective-permute-start | bytes 9437192 | tf_op jit(solution)/shard_map/ppermute | solution.py:36
  443.1 6.0 collective-permute-start.18
  443.1 152.1 %reduce-scatter.5.cloned.1.call-start = ((), (), s32[]{:S(2)}) async-start(), calls=%async_computation.11 | async-start | bytes 3538944 | tf_op jit(solution)/shard_map/reduce_scatter | solution.py:517
  493.7 13.5 %collective-permute-start.19 = (bf16[8,96,2048]{2,1,0:T(8,128)(2,1)}, bf16[8,96,2048]{2,1,0:T(8,128)(2,1)}, u32[]{:S(2)}, u32[]{:S(2)}) collective-permute-start(bf16[8,96,2048]{2,1,0:T(8,128)(2,1)} %get-tuple-element.118), channel_id=1, source_target_pairs={{0,1},{1,0},{2,3},{3,2},{4,5},{5,4},{6,7},{7,6},{8,9},{9,8},{10,11... | collective-permute-start | bytes 9437192 | tf_op jit(solution)/shard_map/ppermute | solution.py:36
  495.4 22.7 %copy-start.41 = (f32[96]{0:T(128)}, f32[96]{0:T(128)S(1)}, u32[]{:S(2)}) copy-start(f32[96]{0:T(128)S(1)} %get-tuple-element.277) | copy-start | bytes 1156
  513.4 201.2 %reduce-scatter.9.cloned.1.call-start = ((), (), s32[]{:S(2)}) async-start(), calls=%async_computation.13 | async-start | bytes 7077888 | tf_op jit(solution)/shard_map/reduce_scatter | solution.py:559
  518.6 16.8 %slice-start = ((s8[7340032]{0:T(1024)(128)(4,1)}), s8[4194304]{0:T(1024)(128)(4,1)S(1)}, s32[]{:S(2)}) async-start(s8[7340032]{0:T(1024)(128)(4,1)} %bitcast.274), calls=%async_computation.16 | async-start | bytes 8388608
  520.0 27.4 %collective-permute-start.21 = (bf16[96,2048]{1,0:T(8,128)(2,1)S(1)}, bf16[96,2048]{1,0:T(8,128)(2,1)S(1)}, u32[]{:S(2)}, u32[]{:S(2)}) collective-permute-start(bf16[96,2048]{1,0:T(8,128)(2,1)S(1)} %fusion.73), channel_id=1, source_target_pairs={{0,2},{1,3},{2,0},{3,1},{4,6},{5,7},{6,4},{7,5},{8,10},{9,11},{10,... | collective-permute-start | bytes 1179656 | tf_op jit(solution)/shard_map/ppermute | solution.py:40
  521.6 38.5 %collective-permute-start.20 = (bf16[96,2048]{1,0:T(8,128)(2,1)S(1)}, bf16[96,2048]{1,0:T(8,128)(2,1)S(1)}, u32[]{:S(2)}, u32[]{:S(2)}) collective-permute-start(bf16[96,2048]{1,0:T(8,128)(2,1)S(1)} %fusion.73), channel_id=1, source_target_pairs={{0,1},{1,0},{2,3},{3,2},{4,5},{5,4},{6,7},{7,6},{8,9},{9,8},{10,11... | collective-permute-start | bytes 1179656 | tf_op jit(solution)/shard_map/ppermute | solution.py:36
  521.6 39.8 %collective-permute-start.23 = (bf16[8,96,2048]{2,1,0:T(8,128)(2,1)S(1)}, bf16[8,96,2048]{2,1,0:T(8,128)(2,1)S(1)}, u32[]{:S(2)}, u32[]{:S(2)}) collective-permute-start(bf16[8,96,2048]{2,1,0:T(8,128)(2,1)S(1)} %copy-done.60), channel_id=1, source_target_pairs={{0,1},{1,0},{2,3},{3,2},{4,5},{5,4},{6,7},{7,6},{8,9},{9,8},{10,11... | collective-permute-start | bytes 9437192 | tf_op jit(solution)/shard_map/ppermute | solution.py:36
  522.1 41.9 %collective-permute-start.24 = (bf16[8,96,2048]{2,1,0:T(8,128)(2,1)}, bf16[8,96,2048]{2,1,0:T(8,128)(2,1)S(1)}, u32[]{:S(2)}, u32[]{:S(2)}) collective-permute-start(bf16[8,96,2048]{2,1,0:T(8,128)(2,1)} %get-tuple-element.139), channel_id=1, source_target_pairs={{0,1},{1,0},{2,3},{3,2},{4,5},{5,4},{6,7},{7,6},{8,9},{9,8},{10,11... | collective-permute-start | bytes 9437192 | tf_op jit(solution)/shard_map/ppermute | solution.py:36
  522.1 13.4 %slice-start.1 = ((s8[7340032]{0:T(1024)(128)(4,1)}), s8[3145728]{0:T(1024)(128)(4,1)S(1)}, s32[]{:S(2)}) async-start(s8[7340032]{0:T(1024)(128)(4,1)} %bitcast.274), calls=%async_computation.17 | async-start | bytes 6291456
  522.1 13.4 %copy-start.61 = (bf16[8,112,1024]{2,1,0:T(8,128)(2,1)S(1)}, bf16[8,112,1024]{2,1,0:T(8,128)(2,1)}, u32[]{:S(2)}) copy-start(bf16[8,112,1024]{2,1,0:T(8,128)(2,1)} %get-tuple-element.129) | copy-start | bytes 5505028
  547.4 12.7 %collective-permute-start.22 = (bf16[96,2048]{1,0:T(8,128)(2,1)S(1)}, bf16[96,2048]{1,0:T(8,128)(2,1)S(1)}, u32[]{:S(2)}, u32[]{:S(2)}) collective-permute-start(bf16[96,2048]{1,0:T(8,128)(2,1)S(1)} %collective-permute-done.21), channel_id=1, source_target_pairs={{0,1},{1,0},{2,3},{3,2},{4,5},{5,4},{6,7},{7,6},{8,9},{9,8},{10,11... | collective-permute-start | bytes 1179656 | tf_op jit(solution)/shard_map/ppermute | solution.py:36
  595.2 297.6 %reduce-scatter.11.cloned.1.call-start = ((), (), s32[]{:S(2)}) async-start(), calls=%async_computation.14 | async-start | bytes 10027008 | tf_op jit(solution)/shard_map/reduce_scatter | solution.py:583
  599.2 11.4 %collective-permute-start.26 = (bf16[96,2048]{1,0:T(8,128)(2,1)S(1)}, bf16[96,2048]{1,0:T(8,128)(2,1)S(1)}, u32[]{:S(2)}, u32[]{:S(2)}) collective-permute-start(bf16[96,2048]{1,0:T(8,128)(2,1)S(1)} %get-tuple-element.218), channel_id=1, source_target_pairs={{0,2},{1,3},{2,0},{3,1},{4,6},{5,7},{6,4},{7,5},{8,10},{9,11},{10,... | collective-permute-start | bytes 1179656 | tf_op jit(solution)/shard_map/ppermute | solution.py:40
  600.4 10.1 %collective-permute-start.25 = (bf16[96,2048]{1,0:T(8,128)(2,1)S(1)}, bf16[96,2048]{1,0:T(8,128)(2,1)S(1)}, u32[]{:S(2)}, u32[]{:S(2)}) collective-permute-start(bf16[96,2048]{1,0:T(8,128)(2,1)S(1)} %get-tuple-element.218), channel_id=1, source_target_pairs={{0,1},{1,0},{2,3},{3,2},{4,5},{5,4},{6,7},{7,6},{8,9},{9,8},{10,11... | collective-permute-start | bytes 1179656 | tf_op jit(solution)/shard_map/ppermute | solution.py:36
  610.5 1.7 collective-permute-start.27
  613.5 17.1 %copy-start.55 = (f32[1,512]{1,0:T(1,128)S(1)}, f32[1,512]{1,0:T(1,128)}, u32[]{:S(2)}) copy-start(f32[1,512]{1,0:T(1,128)} %get-tuple-element.158) | copy-start | bytes 6148
  613.5 17.8 %copy-start.54 = (f32[1,512]{1,0:T(1,128)S(1)}, f32[1,512]{1,0:T(1,128)}, u32[]{:S(2)}) copy-start(f32[1,512]{1,0:T(1,128)} %get-tuple-element.156) | copy-start | bytes 6148
  720.7 7.0 collective-permute-start.28
  721.9 25.9 %slice-start.6 = ((s8[8388608]{0:T(1024)(128)(4,1)}), s8[4194304]{0:T(1024)(128)(4,1)S(1)}, s32[]{:S(2)}) async-start(s8[8388608]{0:T(1024)(128)(4,1)} %bitcast.289), calls=%async_computation.22 | async-start | bytes 8388608
  721.9 28.8 %slice-start.4 = ((s8[8388608]{0:T(1024)(128)(4,1)}), s8[4194304]{0:T(1024)(128)(4,1)S(1)}, s32[]{:S(2)}) async-start(s8[8388608]{0:T(1024)(128)(4,1)} %bitcast.285), calls=%async_computation.20 | async-start | bytes 8388608
  727.1 20.7 %slice-start.7 = ((s8[8388608]{0:T(1024)(128)(4,1)}), s8[4194304]{0:T(1024)(128)(4,1)S(1)}, s32[]{:S(2)}) async-start(s8[8388608]{0:T(1024)(128)(4,1)} %bitcast.289), calls=%async_computation.23 | async-start | bytes 8388608
  727.2 2.4 collective-permute-start.30
  727.7 23.0 %slice-start.5 = ((s8[8388608]{0:T(1024)(128)(4,1)}), s8[4194304]{0:T(1024)(128)(4,1)S(1)}, s32[]{:S(2)}) async-start(s8[8388608]{0:T(1024)(128)(4,1)} %bitcast.285), calls=%async_computation.21 | async-start | bytes 8388608
  728.0 12.1 %collective-permute-start.29 = (bf16[96,2048]{1,0:T(8,128)(2,1)S(1)}, bf16[96,2048]{1,0:T(8,128)(2,1)S(1)}, u32[]{:S(2)}, u32[]{:S(2)}) collective-permute-start(bf16[96,2048]{1,0:T(8,128)(2,1)S(1)} %fusion.49), channel_id=1, source_target_pairs={{0,2},{1,3},{2,0},{3,1},{4,6},{5,7},{6,4},{7,5},{8,10},{9,11},{10,... | collective-permute-start | bytes 1179656 | tf_op jit(solution)/shard_map/ppermute | solution.py:40
  729.7 21.9 %slice-start.2 = ((s8[8388608]{0:T(1024)(128)(4,1)}), s8[4194304]{0:T(1024)(128)(4,1)S(1)}, s32[]{:S(2)}) async-start(s8[8388608]{0:T(1024)(128)(4,1)} %bitcast.281), calls=%async_computation.18 | async-start | bytes 8388608
  729.8 17.8 %collective-permute-start.31 = (bf16[96,2048]{1,0:T(8,128)(2,1)S(1)}, bf16[96,2048]{1,0:T(8,128)(2,1)S(1)}, u32[]{:S(2)}, u32[]{:S(2)}) collective-permute-start(bf16[96,2048]{1,0:T(8,128)(2,1)S(1)} %fusion.44), channel_id=1, source_target_pairs={{0,2},{1,3},{2,0},{3,1},{4,6},{5,7},{6,4},{7,5},{8,10},{9,11},{10,... | collective-permute-start | bytes 1179656 | tf_op jit(solution)/shard_map/ppermute | solution.py:40
  748.1 48.7 %collective-permute-start.37 = (bf16[2,256,2048]{2,1,0:T(8,128)(2,1)S(1)}, bf16[2,256,2048]{2,1,0:T(8,128)(2,1)}, u32[]{:S(2)}, u32[]{:S(2)}) collective-permute-start(bf16[2,256,2048]{2,1,0:T(8,128)(2,1)S(1)} %dynamic-slice_convert_fusion), channel_id=1, source_target_pairs={{0,2},{1,3},{2,0},{3,1},{4,6},{5,7},{6,4},{7,5},{8,10},{9,11},{10,... | collective-permute-start | bytes 6291464 | tf_op jit(solution)/shard_map/ppermute | solution.py:40
  751.0 90.7 %collective-permute-start.33 = (bf16[2,512,1024]{2,1,0:T(8,128)(2,1)S(1)}, bf16[2,512,1024]{2,1,0:T(8,128)(2,1)}, u32[]{:S(2)}, u32[]{:S(2)}) collective-permute-start(bf16[2,512,1024]{2,1,0:T(8,128)(2,1)S(1)} %dynamic-slice_convert_fusion.2), channel_id=1, source_target_pairs={{0,2},{1,3},{2,0},{3,1},{4,6},{5,7},{6,4},{7,5},{8,10},{9,11},{10,... | collective-permute-start | bytes 6291464 | tf_op jit(solution)/shard_map/ppermute | solution.py:40
  753.4 131.7 %collective-permute-start.35 = (bf16[2,512,1024]{2,1,0:T(8,128)(2,1)}, bf16[2,512,1024]{2,1,0:T(8,128)(2,1)}, u32[]{:S(2)}, u32[]{:S(2)}) collective-permute-start(bf16[2,512,1024]{2,1,0:T(8,128)(2,1)} %dynamic-slice_convert_fusion.1), channel_id=1, source_target_pairs={{0,2},{1,3},{2,0},{3,1},{4,6},{5,7},{6,4},{7,5},{8,10},{9,11},{10,... | collective-permute-start | bytes 6291464 | tf_op jit(solution)/shard_map/ppermute | solution.py:40
  802.9 88.4 %collective-permute-start.38 = (bf16[1,256,2048]{2,1,0:T(8,128)(2,1)S(1)}, bf16[1,256,2048]{2,1,0:T(8,128)(2,1)S(1)}, u32[]{:S(2)}, u32[]{:S(2)}) collective-permute-start(bf16[1,256,2048]{2,1,0:T(8,128)(2,1)S(1)} %dynamic-slice_convert_fusion.3), channel_id=1, source_target_pairs={{0,1},{1,0},{2,3},{3,2},{4,5},{5,4},{6,7},{7,6},{8,9},{9,8},{10,11... | collective-permute-start | bytes 3145736 | tf_op jit(solution)/shard_map/ppermute | solution.py:36
  844.3 45.1 %copy-start.11 = (f32[2,512,1024]{2,1,0:T(8,128)}, f32[2,512,1024]{2,1,0:T(8,128)S(1)}, u32[]{:S(2)}) copy-start(f32[2,512,1024]{2,1,0:T(8,128)S(1)} %convert_add_fusion.2) | copy-start | bytes 12582916
  845.7 53.4 %collective-permute-start.34 = (bf16[1,512,1024]{2,1,0:T(8,128)(2,1)}, bf16[1,512,1024]{2,1,0:T(8,128)(2,1)}, u32[]{:S(2)}, u32[]{:S(2)}) collective-permute-start(bf16[1,512,1024]{2,1,0:T(8,128)(2,1)} %dynamic-slice_convert_fusion.5), channel_id=1, source_target_pairs={{0,1},{1,0},{2,3},{3,2},{4,5},{5,4},{6,7},{7,6},{8,9},{9,8},{10,11... | collective-permute-start | bytes 3145736 | tf_op jit(solution)/shard_map/ppermute | solution.py:36
  891.2 13.3 %collective-permute-start.36 = (bf16[1,512,1024]{2,1,0:T(8,128)(2,1)S(1)}, bf16[1,512,1024]{2,1,0:T(8,128)(2,1)}, u32[]{:S(2)}, u32[]{:S(2)}) collective-permute-start(bf16[1,512,1024]{2,1,0:T(8,128)(2,1)S(1)} %dynamic-slice_convert_fusion.4), channel_id=1, source_target_pairs={{0,1},{1,0},{2,3},{3,2},{4,5},{5,4},{6,7},{7,6},{8,9},{9,8},{10,11... | collective-permute-start | bytes 3145736 | tf_op jit(solution)/shard_map/ppermute | solution.py:36
  895.6 24.6 %all-to-all-start.1 = ((bf16[4,64,1664]{2,1,0:T(8,128)(2,1)}), bf16[4,64,1664]{2,1,0:T(8,128)(2,1)S(1)}, u32[]{:S(2)}, u32[]{:S(2)}) async-start(bf16[4,64,1664]{2,1,0:T(8,128)(2,1)} %pad_maximum_fusion.13), calls=%async_computation.5 | async-start | bytes 1703936 | tf_op jit(solution)/shard_map/all_to_all | solution.py:605
  901.9 17.4 %collective-permute-start.32 = (bf16[64,2048]{1,0:T(8,128)(2,1)S(1)}, bf16[64,2048]{1,0:T(8,128)(2,1)S(1)}, u32[]{:S(2)}, u32[]{:S(2)}) collective-permute-start(bf16[64,2048]{1,0:T(8,128)(2,1)S(1)} %bitcast.327), channel_id=1, source_target_pairs={{0,0},{4,1},{8,2},{12,3},{16,4},{20,5},{24,6},{28,7},{1,8},{5,9},{... | collective-permute-start | bytes 786440 | tf_op jit(solution)/shard_map/ppermute | solution.py:603
  (56 other events, 192.6 us)
Sparse Core Ops, SparseCore 0:
  13.3 38.2 all-gather.11
  53.9 116.2 all-gather.13
  172.4 47.2 all-gather.15
  226.0 36.5 all-gather.21
  265.2 74.9 all-gather.19
  342.3 57.4 all-gather.17
  443.2 72.9 reduce-scatter.6
  520.4 73.3 reduce-scatter.4
  597.4 117.1 reduce-scatter.8
  718.1 154.4 reduce-scatter.10

commit v4 on v2

--- a/solution.py
+++ b/solution.py
@@ -512,9 +512,9 @@
         db_list.append(lax.psum_scatter(db_half, "expert", scatter_dimension=0, tiled=True)[0])
         out_parts.append((out_mine, out_near))
         kept.append([v.reshape(owners * pack, v.shape[2]) for v in saved])
+    outs = [v for pair in out_parts for v in pair]
+    _, db_list[0], kept, *outs = tie(db_half, db_list[0], kept, *outs)
     x_k, act_k, dy_k, dgl_k, dul_k = [jnp.concatenate(group, axis=0) for group in zip(*kept)]
-    outs = [v for pair in out_parts for v in pair]
-    _, db_list[0], x_k, act_k, *outs = tie(db_half, db_list[0], x_k, act_k, *outs)
     out_parts = [
         (outs[2 * m].astype(f32) + swap_core(outs[2 * m + 1]).astype(f32)).astype(bf16) for m in range(micro)
     ]

time: 926 us -> 926 us (level)
  other arithmetic: 99.7 us -> 86.3 us
  waiting for transfers between devices: 438 us -> 448 us
    concatenate x2 -> x0, other arithmetic: 11.8 us -> none  [local(): jnp.concatenate(group, axis=0)]
    unnamed x144 -> x147, local copies, waits for them, and re-layouts: 25.9 us -> 31.9 us
  transfers between devices with their start and end apart: 47 -> 47, of which waited for: 25 -> 26; matrix products, arithmetic and copies ran while one was open for 25% -> 24% of each run, Pallas kernels for 15% -> 16%
where the time goes in v4:
time: 926 us; the launch traced here: 917 us
  waiting for transfers between devices  448 us (48%)
  Pallas kernels  142 us (15%)
  local copies, waits for them, and re-layouts  91 us (10%)
  other arithmetic  86.3 us (9%)
  matrix products  71 us (8%)
  blocking collectives  32.7 us (4%)
  starting transfers between devices  30 us (3%)
  between operations  15.5 us (2%)
    ppermute x12, waiting for transfers between devices, swap_side(): return lax.ppermute(values, 'shard', [(s, s ^ 2) for s in range(4)])  277 us
    pallas_call x2, Pallas kernels, expert_step(): pl.pallas_call(expert_body, grid=(owners // group,), in_specs=[pl.BlockSp...  89.6 us
    dot_general x12, matrix products, dot(): lax.dot_general(left, right, (dims, ((), ())), preferred_element_type=f32)  70.8 us
    all_gather x2, waiting for transfers between devices, gather_expert(): return lax.all_gather(own, 'expert', axis=0, tiled=True)  47.6 us
    reduce_scatter x1, waiting for transfers between devices, local(): lax.psum_scatter(out_part, 'expert', scatter_dimension=0, tiled=True)[0]  46.6 us
    pallas_call x2, Pallas kernels, attend_back(): pl.pallas_call(attend_back_body, grid=(heads,), in_specs=[pl.BlockSpec((l...  34 us
    unnamed x147, local copies, waits for them, and re-layouts  31.9 us
    ppermute x22, waiting for transfers between devices, swap_core(): return lax.ppermute(values, 'shard', [(s, s ^ 1) for s in range(4)])  26.8 us
  transfers between devices with their start and end apart: 47, of which 26 were waited for; matrix products, arithmetic and copies ran while one was open for 24% of the time, Pallas kernels for 16%

profile of v4, /device:TPU:2, one launch (start us, length us, event | category | flops | bytes accessed | tf_op | source)
XLA Modules:
  0.0 916.8 jit_solution(873134959239035416)
XLA Ops:
  28.3 15.5 %all_to_all.10 = bf16[4,64,1664]{2,1,0:T(8,128)(2,1)} all-to-all(bf16[4,64,1664]{2,1,0:T(8,128)(2,1)S(1)} %copy.159), channel_id=1, replica_groups=mesh['expert'=8,'shard'=4] {'shard'}, dimensions={0} | all-to-all | bytes 1703936 | tf_op jit(solution)/shard_map/all_to_all | solution.py:409
  43.8 7.6 all-gather.11.cloned.1.call-done
  55.3 3.2 collective-permute-start.4
  59.7 2.4 constant_dynamic-slice_fusion.7
  64.1 3.0 fusion.81
  81.9 4.6 pad_maximum_fusion.3
  86.5 2.5 pad_maximum_fusion.2
  90.7 33.4 %collective-permute-done.3 = bf16[2,512,1024]{2,1,0:T(8,128)(2,1)} collective-permute-done((bf16[2,512,1024]{2,1,0:T(8,128)(2,1)}, bf16[2,512,1024]{2,1,0:T(8,128)(2,1)}, u32[]{:S(2)}, u32[]{:S(2)}) %collective-permute-start.3) | collective-permute-done | bytes 2097184 | tf_op jit(solution)/shard_map/ppermute | solution.py:40
  124.1 3.1 constant_dynamic-update-slice_fusion.17
  127.2 41.2 %collective-permute-done.1 = bf16[2,512,1024]{2,1,0:T(8,128)(2,1)} collective-permute-done((bf16[2,512,1024]{2,1,0:T(8,128)(2,1)S(1)}, bf16[2,512,1024]{2,1,0:T(8,128)(2,1)}, u32[]{:S(2)}, u32[]{:S(2)}) %collective-permute-start.1) | collective-permute-done | bytes 2097184 | tf_op jit(solution)/shard_map/ppermute | solution.py:40
  168.4 3.1 constant_dynamic-update-slice_fusion.19
  173.4 8.2 fusion.8.q_ref.k_ref.v_ref
  184.4 6.3 all_gather.32
  194.1 11.1 %shard_map.263 = (bf16[768,512]{1,0:T(8,128)(2,1)}, bf16[768,512]{1,0:T(8,128)(2,1)}, bf16[768,512]{1,0:T(8,128)(2,1)}, bf16[768,512]{1,0:T(8,128)(2,1)}, f32[8,384,1]{2,1,0:T(8,128)}) custom-call(f32[768,1536]{1,0:T(8,128)} %copy-done, f32[768,1536]{1,0:T(8,128)} %copy-done, f32[768,1536]{1,0:T(8,128)} %copy-done, f32[768,1]{1,0:T(8,128)} %copy.161.qi_ref, ...), custom_call_target="tpu_custom_call" | custom-call | tf_op jit(solution)/shard_map/pallas_call | solution.py:116
  205.2 14.2 %all-gather.15.cloned.1.call-done.wo_ref = bf16[512,2048]{1,0:T(8,128)(2,1)} async-done(((bf16[64,2048]{1,0:T(8,128)(2,1)}), bf16[512,2048]{1,0:T(8,128)(2,1)}) %all-gather.15.cloned.1.call-update) | async-done | bytes 2097168 | tf_op jit(solution)/shard_map/all_gather | solution.py:437
  219.4 3.6 fusion.90
  223.5 3.4 collective-permute-done.8
  229.0 18.1 %collective-permute-done.9 = bf16[2,96,2048]{2,1,0:T(8,128)(2,1)S(1)} collective-permute-done((bf16[2,96,2048]{2,1,0:T(8,128)(2,1)S(1)}, bf16[2,96,2048]{2,1,0:T(8,128)(2,1)S(1)}, u32[]{:S(2)}, u32[]{:S(2)}) %collective-permute-start.9) | collective-permute-done | bytes 786464 | tf_op jit(solution)/shard_map/ppermute | solution.py:40
  250.5 2.3 constant_dynamic-slice_fusion
  255.8 2.3 constant_dynamic-update-slice_fusion.16
  261.2 2.6 pad_maximum_fusion.4
  263.8 42.4 %collective-permute-done.11 = bf16[2,256,2048]{2,1,0:T(8,128)(2,1)} collective-permute-done((bf16[2,256,2048]{2,1,0:T(8,128)(2,1)}, bf16[2,256,2048]{2,1,0:T(8,128)(2,1)}, u32[]{:S(2)}, u32[]{:S(2)}) %collective-permute-start.11) | collective-permute-done | bytes 2097184 | tf_op jit(solution)/shard_map/ppermute | solution.py:40
  308.0 4.5 collective-permute-done.13
  316.1 10.6 %all-gather.17.cloned.1.call-done.bo_ref = bf16[8,96,2048]{2,1,0:T(8,128)(2,1)} async-done(((bf16[1,96,2048]{2,1,0:T(8,128)(2,1)}), bf16[8,96,2048]{2,1,0:T(8,128)(2,1)}) %all-gather.17.cloned.1.call-update) | async-done | bytes 3145744 | tf_op jit(solution)/shard_map/all_gather | solution.py:484
  332.7 45.4 %shard_map.264 = (bf16[8,112,2048]{2,1,0:T(8,128)(2,1)}, bf16[8,112,1024]{2,1,0:T(8,128)(2,1)}, bf16[8,112,2048]{2,1,0:T(8,128)(2,1)}, bf16[8,112,1024]{2,1,0:T(...) custom-call(s32[8,1,192]{2,1,0:T(1,128)} %get-tuple-element.253.slot, ...), custom_call_target="tpu_custom_call" | custom-call | tf_op jit(solution)/shard_map/pallas_call | solution.py:322
  378.3 5.7 collective-permute-done.15
  384.0 4.9 add_convert_fusion.3
  388.9 37.1 %all-gather.19.cloned.1.call-done = bf16[16,96,2048]{2,1,0:T(8,128)(2,1)} async-done(((bf16[2,96,2048]{2,1,0:T(8,128)(2,1)}), bf16[16,96,2048]{2,1,0:T(8,128)(2,1)}) %all-gather.19.cloned.1.call-update) | async-done | bytes 6291472 | tf_op jit(solution)/shard_map/all_gather | solution.py:484
  426.3 10.3 %collective-permute-done.16.bn_ref.dn_ref = bf16[8,2,96,2048]{3,2,1,0:T(8,128)(2,1)} collective-permute-done((bf16[8,2,96,2048]{3,2,1,0:T(8,128)(2,1)}, bf16[8,2,96,2048]{3,2,1,0:T(8,128)(2,1)}, u32[]{:S(2)}, u32[]{:S(2)}) %collective-permute-start.16) | collective-permute-done | bytes 6291488 | tf_op jit(solution)/shard_map/ppermute | solution.py:36
  436.5 44.2 %shard_map.265 = (bf16[8,112,2048]{2,1,0:T(8,128)(2,1)}, bf16[8,112,1024]{2,1,0:T(8,128)(2,1)}, bf16[8,112,2048]{2,1,0:T(8,128)(2,1)}, bf16[8,112,1024]{2,1,0:T(...) custom-call(s32[8,1,192]{2,1,0:T(1,128)} %get-tuple-element.254.slot, ...), custom_call_target="tpu_custom_call" | custom-call | tf_op jit(solution)/shard_map/pallas_call | solution.py:322
  482.4 4.2 collective-permute-done.17
  486.7 4.9 add_convert_fusion.2
  491.7 11.2 %reduce-scatter.7.cloned.1.call-done = bf16[1,96,2048]{2,1,0:T(8,128)(2,1)} async-done(((bf16[8,96,2048]{2,1,0:T(8,128)(2,1)}), bf16[1,96,2048]{2,1,0:T(8,128)(2,1)}) %reduce-scatter.7.cloned.1.call-update) | async-done | bytes 393232 | tf_op jit(solution)/shard_map/reduce_scatter | solution.py:512
  508.5 2.3 constant_dynamic-update-slice_fusion.7
  512.8 10.7 %fusion.14 = f32[2048,1024]{1,0:T(8,128)} fusion(bf16[1792,2048]{1,0:T(8,128)(2,1)S(1)} %constant_dynamic-update-slice_fusion.6, bf16[896,1024]{1,0:T(8,128)(2,1)S(1)} %bitcast.346, bf16[896,1024]{1,0:T(8,128)(2,1)S(1)} %bitcast.343), kind=kOutput, calls=%fused_computation.32 | convolution fusion | flops 7523532800 | bytes 19398656 | tf_op jit(solution)/shard_map/dot_general | solution.py:20
  523.6 10.5 %fusion.10 = f32[2048,1024]{1,0:T(8,128)} fusion(bf16[1792,2048]{1,0:T(8,128)(2,1)S(1)} %constant_dynamic-update-slice_fusion.6, bf16[896,1024]{1,0:T(8,128)(2,1)S(1)} %bitcast.345, bf16[896,1024]{1,0:T(8,128)(2,1)S(1)} %bitcast.342), kind=kOutput, calls=%fused_computation.28 | convolution fusion | flops 7523532800 | bytes 19398656 | tf_op jit(solution)/shard_map/dot_general | solution.py:20
  534.7 12.7 %fusion = f32[1024,2048]{1,0:T(8,128)} fusion(bf16[896,2048]{1,0:T(8,128)(2,1)} %bitcast.340, bf16[896,2048]{1,0:T(8,128)(2,1)S(1)} %bitcast.339, bf16[896,1024]{1,0:T(8,128)(2,1)} %bitcast.344, bf16[896,1024]{1,0:T(8,128)(2,1)S(1)} %bitcast.341), kind=kOutput, calls=%fused_computation.2 | convolution fusion | flops 7538212864 | bytes 19398656 | tf_op jit(solution)/shard_map/dot_general | solution.py:20
  552.7 3.3 pad_maximum_fusion.1
  555.9 16.9 %shard_map.266 = (f32[384,512]{1,0:T(8,128)}, f32[384,512]{1,0:T(8,128)}, bf16[384,512]{1,0:T(8,128)(2,1)}, f32[1,512]{1,0:T(1,128)}, f32[1,512]{1,0:T(1,128)}, /*index=5*/f32[2,384]{1,0:T(2,128)}) custom-call(bf16[384,2048]{1,0:T(8,128)(2,1)} %pad_maximum_fusion.8.dh_ref, bf16[512,2048]{1,0:T(8,128)(2,1)} %all-gather.15.cloned.1.call-done.wo_ref, ...), custom_call_target="tpu_custom_call" | custom-call | tf_op jit(solution)/shard_map/pallas_call | solution.py:180
  572.8 5.7 all-gather.3.sum_ref
  578.6 3.7 shard_map.267
  587.7 9.9 %collective-permute-done.24 = bf16[96,2048]{1,0:T(8,128)(2,1)S(1)} collective-permute-done((bf16[96,2048]{1,0:T(8,128)(2,1)S(1)}, bf16[96,2048]{1,0:T(8,128)(2,1)S(1)}, u32[]{:S(2)}, u32[]{:S(2)}) %collective-permute-start.24) | collective-permute-done | bytes 393248 | tf_op jit(solution)/shard_map/ppermute | solution.py:40
  600.5 17.1 %shard_map.268 = (f32[384,512]{1,0:T(8,128)}, f32[384,512]{1,0:T(8,128)}, bf16[384,512]{1,0:T(8,128)(2,1)}, f32[1,512]{1,0:T(1,128)}, f32[1,512]{1,0:T(1,128)}, /*index=5*/f32[2,384]{1,0:T(2,128)}) custom-call(bf16[384,2048]{1,0:T(8,128)(2,1)} %pad_maximum_fusion.9.dh_ref, bf16[512,2048]{1,0:T(8,128)(2,1)} %all-gather.15.cloned.1.call-done.wo_ref, ...), custom_call_target="tpu_custom_call" | custom-call | tf_op jit(solution)/shard_map/pallas_call | solution.py:180
  629.5 3.9 copy.185
  633.5 5.2 all-gather.4.sum_ref
  638.6 3.9 shard_map.269
  642.5 8.0 convolution_convert_fusion
  650.5 4.3 pad_maximum_fusion
  654.8 46.6 %reduce-scatter.9.cloned.1.call-done = bf16[1,2,96,2048]{3,2,1,0:T(8,128)(2,1)} async-done(((bf16[8,2,96,2048]{3,2,1,0:T(8,128)(2,1)}), bf16[1,2,96,2048]{3,2,1,0:T(8,128)(2,1)}) %reduce-scatter.9.cloned.1.call-update) | async-done | bytes 786448 | tf_op jit(solution)/shard_map/reduce_scatter | solution.py:554
  702.7 4.7 fusion.89
  708.6 5.2 fusion.88
  718.2 8.7 collective-permute-done.27
  727.0 7.4 collective-permute-done.29
  742.9 40.6 %collective-permute-done.35 = bf16[2,256,2048]{2,1,0:T(8,128)(2,1)} collective-permute-done((bf16[2,256,2048]{2,1,0:T(8,128)(2,1)S(1)}, bf16[2,256,2048]{2,1,0:T(8,128)(2,1)}, u32[]{:S(2)}, u32[]{:S(2)}) %collective-permute-start.35) | collective-permute-done | bytes 2097184 | tf_op jit(solution)/shard_map/ppermute | solution.py:40
  783.6 4.3 convert_add_fusion
  790.6 37.9 %collective-permute-done.31 = bf16[2,512,1024]{2,1,0:T(8,128)(2,1)} collective-permute-done((bf16[2,512,1024]{2,1,0:T(8,128)(2,1)S(1)}, bf16[2,512,1024]{2,1,0:T(8,128)(2,1)}, u32[]{:S(2)}, u32[]{:S(2)}) %collective-permute-start.31) | collective-permute-done | bytes 2097184 | tf_op jit(solution)/shard_map/ppermute | solution.py:40
  828.5 2.6 convert_add_fusion.2
  834.3 37.4 %collective-permute-done.33 = bf16[2,512,1024]{2,1,0:T(8,128)(2,1)} collective-permute-done((bf16[2,512,1024]{2,1,0:T(8,128)(2,1)}, bf16[2,512,1024]{2,1,0:T(8,128)(2,1)}, u32[]{:S(2)}, u32[]{:S(2)}) %collective-permute-start.33) | collective-permute-done | bytes 2097184 | tf_op jit(solution)/shard_map/ppermute | solution.py:40
  871.8 4.4 convert_add_fusion.1
  882.3 3.5 all-to-all-start.1
  885.8 2.8 convert_dynamic-update-slice_fusion.2
  888.7 2.6 collective-permute-start.30
  891.2 2.8 convert_dynamic-update-slice_fusion.1
  894.0 12.0 %collective-permute-done.30 = bf16[64,2048]{1,0:T(8,128)(2,1)S(1)} collective-permute-done((bf16[64,2048]{1,0:T(8,128)(2,1)S(1)}, bf16[64,2048]{1,0:T(8,128)(2,1)S(1)}, u32[]{:S(2)}, u32[]{:S(2)}) %collective-permute-start.30) | collective-permute-done | bytes 262176 | tf_op jit(solution)/shard_map/ppermute | solution.py:598
  (385 shorter events, 142.9 us)
Async XLA Ops:
  7.2 44.2 %all-gather.11.cloned.1.call-start = ((), (), s32[]{:S(2)}) async-start(), calls=%async_computation.6 | async-start | bytes 1966080 | tf_op jit(solution)/shard_map/all_gather | solution.py:410
  10.8 14.1 %copy-start.27 = (bf16[64,2048]{1,0:T(8,128)(2,1)S(1)}, bf16[64,2048]{1,0:T(8,128)(2,1)}, u32[]{:S(2)}) copy-start(bf16[64,2048]{1,0:T(8,128)(2,1)} %param.22) | copy-start | bytes 786436
  13.0 158.5 %all-gather.13.cloned.1.call-start = ((), (), s32[]{:S(2)}) async-start(), calls=%async_computation.7 | async-start | bytes 7667712 | tf_op jit(solution)/shard_map/all_gather | solution.py:412
  53.6 165.8 %all-gather.15.cloned.1.call-start = ((), (), s32[]{:S(2)}) async-start(), calls=%async_computation.8 | async-start | bytes 2359296 | tf_op jit(solution)/shard_map/all_gather | solution.py:437
  53.7 24.0 %collective-permute-start.5 = (bf16[2,96,2048]{2,1,0:T(8,128)(2,1)}, bf16[2,96,2048]{2,1,0:T(8,128)(2,1)}, u32[]{:S(2)}, u32[]{:S(2)}) collective-permute-start(bf16[2,96,2048]{2,1,0:T(8,128)(2,1)} %param.16), channel_id=1, source_target_pairs={{0,1},{1,0},{2,3},{3,2},{4,5},{5,4},{6,7},{7,6},{8,9},{9,8},{10,11... | collective-permute-start | bytes 2359304 | tf_op jit(solution)/shard_map/ppermute | solution.py:36
  53.8 23.9 %collective-permute-start.6 = (bf16[2,96,2048]{2,1,0:T(8,128)(2,1)}, bf16[2,96,2048]{2,1,0:T(8,128)(2,1)}, u32[]{:S(2)}, u32[]{:S(2)}) collective-permute-start(bf16[2,96,2048]{2,1,0:T(8,128)(2,1)} %param.16), channel_id=1, source_target_pairs={{0,2},{1,3},{2,0},{3,1},{4,6},{5,7},{6,4},{7,5},{8,10},{9,11},{10,... | collective-permute-start | bytes 2359304 | tf_op jit(solution)/shard_map/ppermute | solution.py:40
  55.3 116.2 %collective-permute-start.4 = (bf16[64,2048]{1,0:T(8,128)(2,1)}, bf16[64,2048]{1,0:T(8,128)(2,1)}, u32[]{:S(2)}, u32[]{:S(2)}) collective-permute-start(bf16[64,2048]{1,0:T(8,128)(2,1)} %param.23), channel_id=1, source_target_pairs={{0,0},{1,4},{2,8},{3,12},{4,16},{5,20},{6,24},{7,28},{8,1},{9,5},{... | collective-permute-start | bytes 786440 | tf_op jit(solution)/shard_map/ppermute | solution.py:419
  59.6 13.1 %collective-permute-start = (bf16[1,512,1024]{2,1,0:T(8,128)(2,1)}, bf16[1,512,1024]{2,1,0:T(8,128)(2,1)}, u32[]{:S(2)}, u32[]{:S(2)}) collective-permute-start(bf16[1,512,1024]{2,1,0:T(8,128)(2,1)} %constant_dynamic-slice_fusion.8), channel_id=1, source_target_pairs={{0,1},{1,0},{2,3},{3,2},{4,5},{5,4},{6,7},{7,6},{8,9},{9,8},{10,11... | collective-permute-start | bytes 3145736 | tf_op jit(solution)/shard_map/ppermute | solution.py:36
  62.0 5.2 collective-permute-start.2
  69.6 54.6 %collective-permute-start.3 = (bf16[2,512,1024]{2,1,0:T(8,128)(2,1)}, bf16[2,512,1024]{2,1,0:T(8,128)(2,1)}, u32[]{:S(2)}, u32[]{:S(2)}) collective-permute-start(bf16[2,512,1024]{2,1,0:T(8,128)(2,1)} %constant_dynamic-update-slice_fusion.18), channel_id=1, source_target_pairs={{0,2},{1,3},{2,0},{3,1},{4,6},{5,7},{6,4},{7,5},{8,10},{9,11},{10,... | collective-permute-start | bytes 6291464 | tf_op jit(solution)/shard_map/ppermute | solution.py:40
  74.0 94.4 %collective-permute-start.1 = (bf16[2,512,1024]{2,1,0:T(8,128)(2,1)S(1)}, bf16[2,512,1024]{2,1,0:T(8,128)(2,1)}, u32[]{:S(2)}, u32[]{:S(2)}) collective-permute-start(bf16[2,512,1024]{2,1,0:T(8,128)(2,1)S(1)} %constant_dynamic-update-slice_fusion.20), channel_id=1, source_target_pairs={{0,2},{1,3},{2,0},{3,1},{4,6},{5,7},{6,4},{7,5},{8,10},{9,11},{10,... | collective-permute-start | bytes 6291464 | tf_op jit(solution)/shard_map/ppermute | solution.py:40
  77.7 11.3 %collective-permute-start.7 = (bf16[2,96,2048]{2,1,0:T(8,128)(2,1)}, bf16[2,96,2048]{2,1,0:T(8,128)(2,1)S(1)}, u32[]{:S(2)}, u32[]{:S(2)}) collective-permute-start(bf16[2,96,2048]{2,1,0:T(8,128)(2,1)} %collective-permute-done.6), channel_id=1, source_target_pairs={{0,1},{1,0},{2,3},{3,2},{4,5},{5,4},{6,7},{7,6},{8,9},{9,8},{10,11... | collective-permute-start | bytes 2359304 | tf_op jit(solution)/shard_map/ppermute | solution.py:36
  90.0 37.3 %copy-start.12 = (bf16[2,384,2048]{2,1,0:T(8,128)(2,1)}, bf16[2,384,2048]{2,1,0:T(8,128)(2,1)S(1)}, u32[]{:S(2)}) copy-start(bf16[2,384,2048]{2,1,0:T(8,128)(2,1)S(1)} %constant_dynamic-update-slice_fusion) | copy-start | bytes 9437188
  171.5 155.2 %all-gather.17.cloned.1.call-start = ((), (), s32[]{:S(2)}) async-start(), calls=%async_computation.9 | async-start | bytes 3538944 | tf_op jit(solution)/shard_map/all_gather | solution.py:484
  223.4 3.5 collective-permute-start.8
  227.3 19.8 %copy-start.18 = (bf16[2,96,2048]{2,1,0:T(8,128)(2,1)S(1)}, bf16[2,96,2048]{2,1,0:T(8,128)(2,1)}, u32[]{:S(2)}) copy-start(bf16[2,96,2048]{2,1,0:T(8,128)(2,1)} %param.16) | copy-start | bytes 2359300
  227.5 19.6 %collective-permute-start.9 = (bf16[2,96,2048]{2,1,0:T(8,128)(2,1)S(1)}, bf16[2,96,2048]{2,1,0:T(8,128)(2,1)S(1)}, u32[]{:S(2)}, u32[]{:S(2)}) collective-permute-start(bf16[2,96,2048]{2,1,0:T(8,128)(2,1)S(1)} %fusion.27), channel_id=1, source_target_pairs={{0,2},{1,3},{2,0},{3,1},{4,6},{5,7},{6,4},{7,5},{8,10},{9,11},{10,... | collective-permute-start | bytes 2359304 | tf_op jit(solution)/shard_map/ppermute | solution.py:40
  250.5 175.6 %all-gather.19.cloned.1.call-start = ((), (), s32[]{:S(2)}) async-start(), calls=%async_computation.14 | async-start | bytes 7077888 | tf_op jit(solution)/shard_map/all_gather | solution.py:484
  252.8 3.0 collective-permute-start.10
  253.8 249.1 %reduce-scatter.7.cloned.1.call-start = ((), (), s32[]{:S(2)}) async-start(), calls=%async_computation.11 | async-start | bytes 3538944 | tf_op jit(solution)/shard_map/reduce_scatter | solution.py:512
  258.2 48.0 %collective-permute-start.11 = (bf16[2,256,2048]{2,1,0:T(8,128)(2,1)}, bf16[2,256,2048]{2,1,0:T(8,128)(2,1)}, u32[]{:S(2)}, u32[]{:S(2)}) collective-permute-start(bf16[2,256,2048]{2,1,0:T(8,128)(2,1)} %constant_dynamic-update-slice_fusion.16), channel_id=1, source_target_pairs={{0,2},{1,3},{2,0},{3,1},{4,6},{5,7},{6,4},{7,5},{8,10},{9,11},{10,... | collective-permute-start | bytes 6291464 | tf_op jit(solution)/shard_map/ppermute | solution.py:40
  259.6 52.9 %collective-permute-start.13 = (bf16[4,96,2048]{2,1,0:T(8,128)(2,1)}, bf16[4,96,2048]{2,1,0:T(8,128)(2,1)}, u32[]{:S(2)}, u32[]{:S(2)}) collective-permute-start(bf16[4,96,2048]{2,1,0:T(8,128)(2,1)} %all-gather.11.cloned.1.call-done), channel_id=1, source_target_pairs={{0,4},{4,0},{8,12},{12,8},{16,20},{20,16},{24,28},{28,24},{1,5},{5... | collective-permute-start | bytes 4718600 | tf_op jit(solution)/shard_map/ppermute | solution.py:66
  263.7 48.7 %copy-start.24 = (bf16[4,96,2048]{2,1,0:T(8,128)(2,1)S(1)}, bf16[4,96,2048]{2,1,0:T(8,128)(2,1)}, u32[]{:S(2)}) copy-start(bf16[4,96,2048]{2,1,0:T(8,128)(2,1)} %all-gather.11.cloned.1.call-done) | copy-start | bytes 4718596
  316.1 15.6 %collective-permute-start.14 = (bf16[8,96,2048]{2,1,0:T(8,128)(2,1)}, bf16[8,96,2048]{2,1,0:T(8,128)(2,1)}, u32[]{:S(2)}, u32[]{:S(2)}) collective-permute-start(bf16[8,96,2048]{2,1,0:T(8,128)(2,1)} %bitcast.37.do_ref), channel_id=1, source_target_pairs={{0,1},{1,0},{2,3},{3,2},{4,5},{5,4},{6,7},{7,6},{8,9},{9,8},{10,11... | collective-permute-start | bytes 9437192 | tf_op jit(solution)/shard_map/ppermute | solution.py:36
  326.7 6.0 collective-permute-start.12
  378.1 5.9 collective-permute-start.15
  426.0 10.5 %collective-permute-start.16 = (bf16[8,2,96,2048]{3,2,1,0:T(8,128)(2,1)}, bf16[8,2,96,2048]{3,2,1,0:T(8,128)(2,1)}, u32[]{:S(2)}, u32[]{:S(2)}) collective-permute-start(bf16[8,2,96,2048]{3,2,1,0:T(8,128)(2,1)} %bitcast.263), channel_id=1, source_target_pairs={{0,1},{1,0},{2,3},{3,2},{4,5},{5,4},{6,7},{7,6},{8,9},{9,8},{10,11... | collective-permute-start | bytes 18874376 | tf_op jit(solution)/shard_map/ppermute | solution.py:36
  426.1 156.2 %reduce-scatter.5.cloned.1.call-start = ((), (), s32[]{:S(2)}) async-start(), calls=%async_computation.10 | async-start | bytes 3538944 | tf_op jit(solution)/shard_map/reduce_scatter | solution.py:512
  480.7 5.9 collective-permute-start.17
  482.4 22.3 %copy-start.40 = (f32[96]{0:T(128)}, f32[96]{0:T(128)S(1)}, u32[]{:S(2)}) copy-start(f32[96]{0:T(128)S(1)} %get-tuple-element.283) | copy-start | bytes 1156
  491.6 209.8 %reduce-scatter.9.cloned.1.call-start = ((), (), s32[]{:S(2)}) async-start(), calls=%async_computation.12 | async-start | bytes 7077888 | tf_op jit(solution)/shard_map/reduce_scatter | solution.py:554
  506.4 27.7 %collective-permute-start.19 = (bf16[96,2048]{1,0:T(8,128)(2,1)S(1)}, bf16[96,2048]{1,0:T(8,128)(2,1)S(1)}, u32[]{:S(2)}, u32[]{:S(2)}) collective-permute-start(bf16[96,2048]{1,0:T(8,128)(2,1)S(1)} %fusion.76), channel_id=1, source_target_pairs={{0,2},{1,3},{2,0},{3,1},{4,6},{5,7},{6,4},{7,5},{8,10},{9,11},{10,... | collective-permute-start | bytes 1179656 | tf_op jit(solution)/shard_map/ppermute | solution.py:40
  508.0 39.4 %collective-permute-start.18 = (bf16[96,2048]{1,0:T(8,128)(2,1)S(1)}, bf16[96,2048]{1,0:T(8,128)(2,1)S(1)}, u32[]{:S(2)}, u32[]{:S(2)}) collective-permute-start(bf16[96,2048]{1,0:T(8,128)(2,1)S(1)} %fusion.76), channel_id=1, source_target_pairs={{0,1},{1,0},{2,3},{3,2},{4,5},{5,4},{6,7},{7,6},{8,9},{9,8},{10,11... | collective-permute-start | bytes 1179656 | tf_op jit(solution)/shard_map/ppermute | solution.py:36
  508.0 40.7 %collective-permute-start.21 = (bf16[8,96,2048]{2,1,0:T(8,128)(2,1)}, bf16[8,96,2048]{2,1,0:T(8,128)(2,1)S(1)}, u32[]{:S(2)}, u32[]{:S(2)}) collective-permute-start(bf16[8,96,2048]{2,1,0:T(8,128)(2,1)} %get-tuple-element.145), channel_id=1, source_target_pairs={{0,1},{1,0},{2,3},{3,2},{4,5},{5,4},{6,7},{7,6},{8,9},{9,8},{10,11... | collective-permute-start | bytes 9437192 | tf_op jit(solution)/shard_map/ppermute | solution.py:36
  508.5 42.8 %collective-permute-start.22 = (bf16[8,96,2048]{2,1,0:T(8,128)(2,1)}, bf16[8,96,2048]{2,1,0:T(8,128)(2,1)S(1)}, u32[]{:S(2)}, u32[]{:S(2)}) collective-permute-start(bf16[8,96,2048]{2,1,0:T(8,128)(2,1)} %get-tuple-element.147), channel_id=1, source_target_pairs={{0,1},{1,0},{2,3},{3,2},{4,5},{5,4},{6,7},{7,6},{8,9},{9,8},{10,11... | collective-permute-start | bytes 9437192 | tf_op jit(solution)/shard_map/ppermute | solution.py:36
  512.8 10.7 %copy-start.55 = (bf16[8,112,1024]{2,1,0:T(8,128)(2,1)S(1)}, bf16[8,112,1024]{2,1,0:T(8,128)(2,1)}, u32[]{:S(2)}) copy-start(bf16[8,112,1024]{2,1,0:T(8,128)(2,1)} %get-tuple-element.122) | copy-start | bytes 5505028
  512.8 10.7 %copy-start.57 = (bf16[8,112,1024]{2,1,0:T(8,128)(2,1)S(1)}, bf16[8,112,1024]{2,1,0:T(8,128)(2,1)}, u32[]{:S(2)}) copy-start(bf16[8,112,1024]{2,1,0:T(8,128)(2,1)} %get-tuple-element.127) | copy-start | bytes 5505028
  523.6 11.1 %copy-start.53 = (bf16[8,112,2048]{2,1,0:T(8,128)(2,1)S(1)}, bf16[8,112,2048]{2,1,0:T(8,128)(2,1)}, u32[]{:S(2)}) copy-start(bf16[8,112,2048]{2,1,0:T(8,128)(2,1)} %get-tuple-element.121) | copy-start | bytes 11010052
  523.6 11.1 %copy-start.54 = (bf16[8,112,1024]{2,1,0:T(8,128)(2,1)S(1)}, bf16[8,112,1024]{2,1,0:T(8,128)(2,1)}, u32[]{:S(2)}) copy-start(bf16[8,112,1024]{2,1,0:T(8,128)(2,1)} %get-tuple-element.120) | copy-start | bytes 5505028
  534.1 13.3 %collective-permute-start.20 = (bf16[96,2048]{1,0:T(8,128)(2,1)S(1)}, bf16[96,2048]{1,0:T(8,128)(2,1)S(1)}, u32[]{:S(2)}, u32[]{:S(2)}) collective-permute-start(bf16[96,2048]{1,0:T(8,128)(2,1)S(1)} %collective-permute-done.19), channel_id=1, source_target_pairs={{0,1},{1,0},{2,3},{3,2},{4,5},{5,4},{6,7},{7,6},{8,9},{9,8},{10,11... | collective-permute-start | bytes 1179656 | tf_op jit(solution)/shard_map/ppermute | solution.py:36
  582.3 297.3 %reduce-scatter.11.cloned.1.call-start = ((), (), s32[]{:S(2)}) async-start(), calls=%async_computation.13 | async-start | bytes 10027008 | tf_op jit(solution)/shard_map/reduce_scatter | solution.py:578
  586.2 11.4 %collective-permute-start.24 = (bf16[96,2048]{1,0:T(8,128)(2,1)S(1)}, bf16[96,2048]{1,0:T(8,128)(2,1)S(1)}, u32[]{:S(2)}, u32[]{:S(2)}) collective-permute-start(bf16[96,2048]{1,0:T(8,128)(2,1)S(1)} %get-tuple-element.226), channel_id=1, source_target_pairs={{0,2},{1,3},{2,0},{3,1},{4,6},{5,7},{6,4},{7,5},{8,10},{9,11},{10,... | collective-permute-start | bytes 1179656 | tf_op jit(solution)/shard_map/ppermute | solution.py:40
  587.6 10.0 %collective-permute-start.23 = (bf16[96,2048]{1,0:T(8,128)(2,1)S(1)}, bf16[96,2048]{1,0:T(8,128)(2,1)S(1)}, u32[]{:S(2)}, u32[]{:S(2)}) collective-permute-start(bf16[96,2048]{1,0:T(8,128)(2,1)S(1)} %get-tuple-element.226), channel_id=1, source_target_pairs={{0,1},{1,0},{2,3},{3,2},{4,5},{5,4},{6,7},{7,6},{8,9},{9,8},{10,11... | collective-permute-start | bytes 1179656 | tf_op jit(solution)/shard_map/ppermute | solution.py:36
  597.6 1.7 collective-permute-start.25
  600.5 17.1 %copy-start.52 = (f32[1,512]{1,0:T(1,128)S(1)}, f32[1,512]{1,0:T(1,128)}, u32[]{:S(2)}) copy-start(f32[1,512]{1,0:T(1,128)} %get-tuple-element.166) | copy-start | bytes 6148
  600.5 17.8 %copy-start.51 = (f32[1,512]{1,0:T(1,128)S(1)}, f32[1,512]{1,0:T(1,128)}, u32[]{:S(2)}) copy-start(f32[1,512]{1,0:T(1,128)} %get-tuple-element.164) | copy-start | bytes 6148
  707.5 7.0 collective-permute-start.26
  708.6 25.9 %slice-start.4 = ((s8[8388608]{0:T(1024)(128)(4,1)}), s8[4194304]{0:T(1024)(128)(4,1)S(1)}, s32[]{:S(2)}) async-start(s8[8388608]{0:T(1024)(128)(4,1)} %bitcast.283), calls=%async_computation.19 | async-start | bytes 8388608
  708.6 28.9 %slice-start.2 = ((s8[8388608]{0:T(1024)(128)(4,1)}), s8[4194304]{0:T(1024)(128)(4,1)S(1)}, s32[]{:S(2)}) async-start(s8[8388608]{0:T(1024)(128)(4,1)} %bitcast.279), calls=%async_computation.17 | async-start | bytes 8388608
  713.8 20.7 %slice-start.5 = ((s8[8388608]{0:T(1024)(128)(4,1)}), s8[4194304]{0:T(1024)(128)(4,1)S(1)}, s32[]{:S(2)}) async-start(s8[8388608]{0:T(1024)(128)(4,1)} %bitcast.283), calls=%async_computation.20 | async-start | bytes 8388608
  714.0 2.4 collective-permute-start.28
  714.5 23.0 %slice-start.3 = ((s8[8388608]{0:T(1024)(128)(4,1)}), s8[4194304]{0:T(1024)(128)(4,1)S(1)}, s32[]{:S(2)}) async-start(s8[8388608]{0:T(1024)(128)(4,1)} %bitcast.279), calls=%async_computation.18 | async-start | bytes 8388608
  714.8 12.1 %collective-permute-start.27 = (bf16[96,2048]{1,0:T(8,128)(2,1)S(1)}, bf16[96,2048]{1,0:T(8,128)(2,1)S(1)}, u32[]{:S(2)}, u32[]{:S(2)}) collective-permute-start(bf16[96,2048]{1,0:T(8,128)(2,1)S(1)} %fusion.52), channel_id=1, source_target_pairs={{0,2},{1,3},{2,0},{3,1},{4,6},{5,7},{6,4},{7,5},{8,10},{9,11},{10,... | collective-permute-start | bytes 1179656 | tf_op jit(solution)/shard_map/ppermute | solution.py:40
  716.5 21.9 %slice-start = ((s8[8388608]{0:T(1024)(128)(4,1)}), s8[4194304]{0:T(1024)(128)(4,1)S(1)}, s32[]{:S(2)}) async-start(s8[8388608]{0:T(1024)(128)(4,1)} %bitcast.275), calls=%async_computation.15 | async-start | bytes 8388608
  716.6 17.8 %collective-permute-start.29 = (bf16[96,2048]{1,0:T(8,128)(2,1)S(1)}, bf16[96,2048]{1,0:T(8,128)(2,1)S(1)}, u32[]{:S(2)}, u32[]{:S(2)}) collective-permute-start(bf16[96,2048]{1,0:T(8,128)(2,1)S(1)} %fusion.47), channel_id=1, source_target_pairs={{0,2},{1,3},{2,0},{3,1},{4,6},{5,7},{6,4},{7,5},{8,10},{9,11},{10,... | collective-permute-start | bytes 1179656 | tf_op jit(solution)/shard_map/ppermute | solution.py:40
  727.0 9.4 %copy-start.4 = (f32[2,96,2048]{2,1,0:T(8,128)S(1)}, f32[2,96,2048]{2,1,0:T(8,128)}, u32[]{:S(2)}) copy-start(f32[2,96,2048]{2,1,0:T(8,128)} %copy-done.3) | copy-start | bytes 4718596
  734.9 48.7 %collective-permute-start.35 = (bf16[2,256,2048]{2,1,0:T(8,128)(2,1)S(1)}, bf16[2,256,2048]{2,1,0:T(8,128)(2,1)}, u32[]{:S(2)}, u32[]{:S(2)}) collective-permute-start(bf16[2,256,2048]{2,1,0:T(8,128)(2,1)S(1)} %dynamic-slice_convert_fusion), channel_id=1, source_target_pairs={{0,2},{1,3},{2,0},{3,1},{4,6},{5,7},{6,4},{7,5},{8,10},{9,11},{10,... | collective-permute-start | bytes 6291464 | tf_op jit(solution)/shard_map/ppermute | solution.py:40
  737.8 90.7 %collective-permute-start.31 = (bf16[2,512,1024]{2,1,0:T(8,128)(2,1)S(1)}, bf16[2,512,1024]{2,1,0:T(8,128)(2,1)}, u32[]{:S(2)}, u32[]{:S(2)}) collective-permute-start(bf16[2,512,1024]{2,1,0:T(8,128)(2,1)S(1)} %dynamic-slice_convert_fusion.2), channel_id=1, source_target_pairs={{0,2},{1,3},{2,0},{3,1},{4,6},{5,7},{6,4},{7,5},{8,10},{9,11},{10,... | collective-permute-start | bytes 6291464 | tf_op jit(solution)/shard_map/ppermute | solution.py:40
  740.1 131.6 %collective-permute-start.33 = (bf16[2,512,1024]{2,1,0:T(8,128)(2,1)}, bf16[2,512,1024]{2,1,0:T(8,128)(2,1)}, u32[]{:S(2)}, u32[]{:S(2)}) collective-permute-start(bf16[2,512,1024]{2,1,0:T(8,128)(2,1)} %dynamic-slice_convert_fusion.1), channel_id=1, source_target_pairs={{0,2},{1,3},{2,0},{3,1},{4,6},{5,7},{6,4},{7,5},{8,10},{9,11},{10,... | collective-permute-start | bytes 6291464 | tf_op jit(solution)/shard_map/ppermute | solution.py:40
  789.6 88.4 %collective-permute-start.36 = (bf16[1,256,2048]{2,1,0:T(8,128)(2,1)S(1)}, bf16[1,256,2048]{2,1,0:T(8,128)(2,1)S(1)}, u32[]{:S(2)}, u32[]{:S(2)}) collective-permute-start(bf16[1,256,2048]{2,1,0:T(8,128)(2,1)S(1)} %dynamic-slice_convert_fusion.3), channel_id=1, source_target_pairs={{0,1},{1,0},{2,3},{3,2},{4,5},{5,4},{6,7},{7,6},{8,9},{9,8},{10,11... | collective-permute-start | bytes 3145736 | tf_op jit(solution)/shard_map/ppermute | solution.py:36
  834.3 51.5 %collective-permute-start.32 = (bf16[1,512,1024]{2,1,0:T(8,128)(2,1)}, bf16[1,512,1024]{2,1,0:T(8,128)(2,1)}, u32[]{:S(2)}, u32[]{:S(2)}) collective-permute-start(bf16[1,512,1024]{2,1,0:T(8,128)(2,1)} %dynamic-slice_convert_fusion.5), channel_id=1, source_target_pairs={{0,1},{1,0},{2,3},{3,2},{4,5},{5,4},{6,7},{7,6},{8,9},{9,8},{10,11... | collective-permute-start | bytes 3145736 | tf_op jit(solution)/shard_map/ppermute | solution.py:36
  877.9 13.3 %collective-permute-start.34 = (bf16[1,512,1024]{2,1,0:T(8,128)(2,1)S(1)}, bf16[1,512,1024]{2,1,0:T(8,128)(2,1)}, u32[]{:S(2)}, u32[]{:S(2)}) collective-permute-start(bf16[1,512,1024]{2,1,0:T(8,128)(2,1)S(1)} %dynamic-slice_convert_fusion.4), channel_id=1, source_target_pairs={{0,1},{1,0},{2,3},{3,2},{4,5},{5,4},{6,7},{7,6},{8,9},{9,8},{10,11... | collective-permute-start | bytes 3145736 | tf_op jit(solution)/shard_map/ppermute | solution.py:36
  882.3 24.6 %all-to-all-start.1 = ((bf16[4,64,1664]{2,1,0:T(8,128)(2,1)}), bf16[4,64,1664]{2,1,0:T(8,128)(2,1)S(1)}, u32[]{:S(2)}, u32[]{:S(2)}) async-start(bf16[4,64,1664]{2,1,0:T(8,128)(2,1)} %pad_maximum_fusion.10), calls=%async_computation.5 | async-start | bytes 1703936 | tf_op jit(solution)/shard_map/all_to_all | solution.py:600
  888.7 17.4 %collective-permute-start.30 = (bf16[64,2048]{1,0:T(8,128)(2,1)S(1)}, bf16[64,2048]{1,0:T(8,128)(2,1)S(1)}, u32[]{:S(2)}, u32[]{:S(2)}) collective-permute-start(bf16[64,2048]{1,0:T(8,128)(2,1)S(1)} %bitcast.317), channel_id=1, source_target_pairs={{0,0},{4,1},{8,2},{12,3},{16,4},{20,5},{24,6},{28,7},{1,8},{5,9},{... | collective-permute-start | bytes 786440 | tf_op jit(solution)/shard_map/ppermute | solution.py:598
  (48 other events, 134.6 us)
Sparse Core Ops, SparseCore 0:
  13.1 38.2 all-gather.10
  53.8 116.2 all-gather.12
  172.2 47.1 all-gather.14
  250.6 76.0 all-gather.16
  328.7 97.2 all-gather.18
  429.5 73.3 reduce-scatter.6
  507.0 73.4 reduce-scatter.4
  584.1 117.2 reduce-scatter.8
  705.1 154.4 reduce-scatter.10
